TPU v7x, 32 devices: a whole 2x2x4 slice. The times are simulated.
32 devices in a mesh: leaf: 8 (over y, x, core), front: 4 (over z).
Axes of the slice: x: 2, y: 2, z: 4, core: 2. Of those that a mesh axis runs over, the one named last changes fastest.
Arguments:
- leaf_rhs: float32 [8, 64, 256], P('leaf', None, 'front'), may hold values from -6 to 6
- sep_rhs: float32 [8, 64, 256], P('leaf', None, 'front'), may hold values from -6 to 6
- leaf_inverse: float32 [8, 256, 256], P('leaf', 'front'), as said below
- sep_inverse: float32 [8, 256, 256], P('leaf', 'front')
- leaf_block: float32 [8, 32, 256], P('leaf', None, 'front'), may hold values from -0.375 to 0.375
- sep_block: float32 [8, 32, 256], P('leaf', None, 'front'), may hold values from -0.375 to 0.375
- pattern: int32 [2, 8, 32], replicated, may hold values from 0 to 255, as said below
- outer_solution: float32 [64, 256], P(None, 'front'), may hold values from -6 to 6
Outputs:
- solution: float32 [2, 8, 64, 256], P(None, 'leaf', None, 'front')
Inputs may be any that keep to these rules, and one draw needn't show every extreme that they name: `pattern`: within one supernode the 32 entries are distinct and rising, the first is 0 and the last is 255. `leaf_inverse`: each leaf block is lower triangular with its diagonal bounded away from zero.
All inputs are finite; a program needn't handle non-finite values.
Results may differ from a plain program's by a relative error of at most 0.0003.
Values sent between devices are 32-bit elements; how exact they have to be, the bound alone decides.
No kernel may reach another device: no remote copies, remote signals or barrier semaphores. Data moves between devices by JAX's collectives and lax.ppermute only.
A program may use at most 64 MiB of HBM per device.

v0:
```python
import jax
import jax.numpy as jnp
from jax import lax
from jax.sharding import PartitionSpec as P


def partner(block, axis, distance):
    count = lax.axis_size(axis)
    route = []
    for low in range(count):
        high = low | 1 << distance
        if high != low and high < count:
            route += [(low, high), (high, low)]
    return lax.ppermute(block, axis, route)


def times_rows(vectors, matrix):
    return jnp.dot(
        vectors, matrix, precision=lax.Precision.HIGHEST, preferred_element_type=jnp.float32
    )


def against_rows(vectors, matrix):
    return lax.dot_general(
        vectors,
        matrix,
        (((1,), (1,)), ((), ())),
        precision=lax.Precision.HIGHEST,
        preferred_element_type=jnp.float32,
    )


def body(
    leaf_rhs, sep_rhs, leaf_inverse, sep_inverse, leaf_block, sep_block, pattern, outer_solution
):
    group_count = lax.axis_size("leaf")
    depth = group_count.bit_length() - 1
    group_pos = lax.axis_index("leaf")
    front_pos = lax.axis_index("front")
    local_rows = leaf_rhs.shape[-1]
    full_rows = leaf_inverse.shape[-1]
    vector_count = leaf_rhs.shape[1]
    leaf_r = leaf_rhs[0]
    leaf_inv = leaf_inverse[0]
    leaf_u = leaf_block[0]
    sep_r = sep_rhs[0]
    sep_inv = sep_inverse[0]
    sep_u = sep_block[0]
    all_rows = jnp.arange(full_rows, dtype=jnp.int32)

    def geometry(level):
        blocks = 2 ** min(level, depth)
        share = local_rows // blocks
        offset = local_rows - (local_rows >> level - 1)
        return (share, offset, group_pos % blocks)

    def label_of(level):
        if level > depth:
            return jnp.int32(0)
        return group_pos // 2**level * 2**level + 2 ** (level - 1)

    def ids_of(level):
        return lax.dynamic_index_in_dim(pattern[1], label_of(level), 0, keepdims=False)

    def block_sum(term, level):
        nbits = min(level, depth)
        if nbits == depth:
            return lax.psum(term, ("leaf", "front"))
        piece = lax.psum_scatter(term, "front", scatter_dimension=1, tiled=True)
        for bit in range(nbits):
            piece = piece + partner(piece, "leaf", bit)
        return lax.all_gather(piece, "front", axis=1, tiled=True)

    leaf_y = against_rows(lax.all_gather(leaf_r, "front", axis=1, tiled=True), leaf_inv)
    leaf_ids = lax.dynamic_index_in_dim(pattern[0], group_pos, 0, keepdims=False)
    child_part = against_rows(leaf_y, leaf_u)
    child_ids = leaf_ids
    solved = {}
    for level in range(1, depth + 2):
        share, offset, inner_pos = geometry(level)
        own_r = sep_r[:, offset : offset + share]
        start_col = front_pos * local_rows + inner_pos * share
        contribution = jnp.zeros((vector_count, full_rows), jnp.float32)
        contribution = lax.dynamic_update_slice(contribution, own_r, (jnp.int32(0), start_col))
        selector = (child_ids[:, None] == all_rows[None, :]).astype(jnp.float32)
        contribution = contribution - times_rows(child_part, selector)
        whole_v = block_sum(contribution, level)
        y_level = against_rows(whole_v, sep_inv[offset : offset + share, :])
        solved[level] = y_level
        if level <= depth:
            child_part = against_rows(y_level, sep_u[:, offset : offset + share])
            child_ids = ids_of(level)
    parent_x = lax.all_gather(outer_solution, "front", axis=1, tiled=True)
    sep_full = jnp.zeros((vector_count, full_rows), jnp.float32)
    for level in range(depth + 1, 0, -1):
        share, offset, inner_pos = geometry(level)
        picked = jnp.take(parent_x, ids_of(level), axis=1)
        rest = solved[level] - times_rows(picked, sep_u[:, offset : offset + share])
        term = times_rows(rest, sep_inv[offset : offset + share, :])
        parent_x = block_sum(term, level)
        sep_full = jnp.where(label_of(level) == group_pos, parent_x, sep_full)
    picked = jnp.take(parent_x, leaf_ids, axis=1)
    rest = leaf_y - times_rows(picked, leaf_u)
    leaf_x = lax.psum_scatter(times_rows(rest, leaf_inv), "front", scatter_dimension=1, tiled=True)
    sep_x = lax.dynamic_slice_in_dim(sep_full, front_pos * local_rows, local_rows, 1)
    return jnp.stack([leaf_x, sep_x])[:, None]


def solution(mesh):
    placed = (
        P("leaf", None, "front"),
        P("leaf", None, "front"),
        P("leaf", "front", None),
        P("leaf", "front", None),
        P("leaf", None, "front"),
        P("leaf", None, "front"),
        P(),
        P(None, "front"),
    )
    return jax.shard_map(
        body, mesh=mesh, in_specs=placed, out_specs=P(None, "leaf", None, "front"), check_vma=False
    )
```

profile of v0, /device:TPU:0, one launch (start us, length us, event | category | flops | bytes accessed | tf_op | source)
XLA Modules:
  0.0 694.5 jit_solution(14276887811836147891)
XLA Ops:
  6.6 0.7 copy-done.9
  7.4 15.1 %all-gather = f32[1,64,256]{1,0,2:T(1,128)S(1)} all-gather(f32[1,64,64]{1,0,2:T(1,128)S(1)} %copy.15), channel_id=2, replica_groups=mesh['leaf'=8,'front'=4] {'front'}, dimensions={2}, use_global_device_ids=true | all-gather | bytes 81920 | tf_op jit(solution)/shard_map/all_gather | solution.py:74
  22.5 0.4 fusion.1
  22.9 0.3 copy-done.6
  23.4 0.7 copy-done.1
  24.1 0.4 dynamic_update_slice.12
  24.8 0.7 copy.26
  25.6 20.6 %reduce-scatter.16.cloned.1.call-done = f32[64,64]{1,0:T(8,128)} async-done(((f32[256,64]{1,0:T(8,128)}), f32[64,64]{1,0:T(8,128)}) %reduce-scatter.16.cloned.1.call-update) | async-done | bytes 16400
  46.2 0.8 copy.27
  47.2 0.4 dynamic_update_slice.13
  47.7 0.6 collective-permute-done
  48.4 13.5 %all_gather.19 = f32[64,256]{0,1:T(8,128)S(1)} all-gather(f32[64,64]{0,1:T(8,128)S(1)} %copy.16), channel_id=1, replica_groups=mesh['leaf'=8,'front'=4] {'front'}, dimensions={1}, use_global_device_ids=true | all-gather | bytes 81920 | tf_op jit(solution)/shard_map/all_gather | solution.py:72
  62.1 0.5 copy-done.2
  63.1 0.7 copy.28
  64.0 17.4 %reduce-scatter.18.cloned.1.call-done = f32[64,64]{1,0:T(8,128)} async-done(((f32[256,64]{1,0:T(8,128)}), f32[64,64]{1,0:T(8,128)}) %reduce-scatter.18.cloned.1.call-update) | async-done | bytes 16400
  81.4 0.8 copy.29
  82.3 1.2 collective-permute-done.1
  83.5 1.5 collective-permute-start.2
  85.0 0.4 dynamic_update_slice.14
  85.5 2.0 collective-permute-done.2
  87.5 13.4 %all_gather.20 = f32[64,256]{0,1:T(8,128)S(1)} all-gather(f32[64,64]{0,1:T(8,128)S(1)} %copy.17), channel_id=1, replica_groups=mesh['leaf'=8,'front'=4] {'front'}, dimensions={1}, use_global_device_ids=true | all-gather | bytes 81920 | tf_op jit(solution)/shard_map/all_gather | solution.py:72
  101.1 0.3 fusion.36
  101.4 0.9 convolution_subtract_fusion.1
  102.3 0.4 dynamic_update_slice.15
  102.8 115.3 %all-reduce.5.cloned.1.call-done = f32[64,256]{1,0:T(8,128)} async-done(((f32[64,256]{1,0:T(8,128)}), f32[64,256]{1,0:T(8,128)}) %all-reduce.5.cloned.1.call-update) | async-done | bytes 65552 | tf_op jit(solution)/shard_map/psum | solution.py:68
  218.1 1.0 fusion.49
  219.0 0.3 fusion.33
  219.3 0.9 convolution_subtract_fusion
  220.3 0.7 copy-done.8
  221.0 14.3 %all_gather.21 = f32[64,256]{0,1:T(8,128)S(1)} all-gather(f32[64,64]{0,1:T(8,128)S(1)} %copy.18), channel_id=1, replica_groups=mesh['leaf'=8,'front'=4] {'front'}, dimensions={1}, use_global_device_ids=true | all-gather | bytes 81920 | tf_op jit(solution)/shard_map/all_gather | solution.py:93
  235.4 0.6 gather_fusion
  235.9 105.9 %all-reduce.7.cloned.1.call-done = f32[64,256]{1,0:T(8,128)} async-done(((f32[64,256]{1,0:T(8,128)}), f32[64,256]{1,0:T(8,128)}) %all-reduce.7.cloned.1.call-update) | async-done | bytes 65552 | tf_op jit(solution)/shard_map/psum | solution.py:68
  341.9 1.0 fusion.45
  342.9 0.3 convolution_subtract_fusion.5
  343.2 0.8 fusion.43
  344.1 121.5 %all-reduce.9.cloned.1.call-done = f32[64,256]{1,0:T(8,128)} async-done(((f32[64,256]{1,0:T(8,128)}), f32[64,256]{1,0:T(8,128)}) %all-reduce.9.cloned.1.call-update) | async-done | bytes 65552 | tf_op jit(solution)/shard_map/psum | solution.py:68
  465.6 0.9 copy.19
  466.6 0.6 gather_fusion.1
  467.2 0.3 convolution_subtract_fusion.8
  467.4 0.9 fusion.47
  468.4 121.0 %all-reduce.11.cloned.1.call-done = f32[64,256]{1,0:T(8,128)} async-done(((f32[64,256]{1,0:T(8,128)}), f32[64,256]{1,0:T(8,128)}) %all-reduce.11.cloned.1.call-update) | async-done | bytes 65552 | tf_op jit(solution)/shard_map/psum | solution.py:68
  589.4 0.9 copy.20
  590.4 0.6 gather_fusion.2
  591.0 0.3 convolution_subtract_fusion.7
  591.2 1.1 convolution_bitcast_fusion.2
  592.4 20.0 %reduce-scatter.20.cloned.1.call-done = f32[64,64]{1,0:T(8,128)} async-done(((f32[256,64]{1,0:T(8,128)}), f32[64,64]{1,0:T(8,128)}) %reduce-scatter.20.cloned.1.call-update) | async-done | bytes 16400
  612.4 0.8 copy.31
  613.3 1.2 collective-permute-done.3
  614.5 1.6 collective-permute-start.4
  616.0 2.3 collective-permute-done.4
  618.5 13.3 %all_gather.22 = f32[64,256]{0,1:T(8,128)S(1)} all-gather(f32[64,64]{0,1:T(8,128)S(1)} %copy.21), channel_id=1, replica_groups=mesh['leaf'=8,'front'=4] {'front'}, dimensions={1}, use_global_device_ids=true | all-gather | bytes 81920 | tf_op jit(solution)/shard_map/all_gather | solution.py:72
  631.8 0.6 gather_fusion.3
  632.6 1.0 convolution_bitcast_fusion.1
  633.8 17.6 %reduce-scatter.22.cloned.1.call-done = f32[64,64]{1,0:T(8,128)} async-done(((f32[256,64]{1,0:T(8,128)}), f32[64,64]{1,0:T(8,128)}) %reduce-scatter.22.cloned.1.call-update) | async-done | bytes 16400
  651.3 0.8 copy.33
  652.3 1.1 collective-permute-done.5
  653.5 13.4 %all_gather.23 = f32[64,256]{0,1:T(8,128)S(1)} all-gather(f32[64,64]{0,1:T(8,128)S(1)} %copy.22), channel_id=1, replica_groups=mesh['leaf'=8,'front'=4] {'front'}, dimensions={1}, use_global_device_ids=true | all-gather | bytes 81920 | tf_op jit(solution)/shard_map/all_gather | solution.py:72
  666.9 0.6 gather_fusion.4
  667.5 0.3 convolution_subtract_fusion.4
  667.9 1.0 convolution_bitcast_fusion
  668.9 0.8 copy-done.4
  669.9 16.6 %reduce-scatter.24.cloned.1.call-done = f32[64,64]{1,0:T(8,128)} async-done(((f32[256,64]{1,0:T(8,128)}), f32[64,64]{1,0:T(8,128)}) %reduce-scatter.24.cloned.1.call-update) | async-done | bytes 16400
  686.5 0.8 copy.35
  687.4 0.6 maximum_bitcast_fusion
  (79 shorter events, 3.3 us)
Async XLA Ops:
  6.5 15.9 %copy-start = (f32[1,64,256]{2,1,0:T(8,128)S(1)}, f32[1,64,256]{2,1,0:T(8,128)}, u32[]{:S(2)}) copy-start(f32[1,64,256]{2,1,0:T(8,128)} %param.12) | copy-start | bytes 196612
  6.5 0.8 copy-start.7
  6.5 39.7 %reduce-scatter.16.cloned.1.call-start = ((), (), s32[]{:S(2)}) async-start(), calls=%async_computation.9 | async-start | bytes 163840
  6.5 0.7 copy-start.9
  22.5 0.7 copy-start.6
  23.4 0.8 copy-start.1
  25.5 55.9 %reduce-scatter.18.cloned.1.call-start = ((), (), s32[]{:S(2)}) async-start(), calls=%async_computation.10 | async-start | bytes 163840
  47.0 1.3 collective-permute-start
  48.4 13.5 %copy-start.3 = (f32[1,64,256]{2,1,0:T(8,128)S(1)}, f32[1,64,256]{2,1,0:T(8,128)}, u32[]{:S(2)}) copy-start(f32[1,64,256]{2,1,0:T(8,128)} %param.13) | copy-start | bytes 196612
  61.9 0.7 copy-start.2
  63.9 154.2 %all-reduce.5.cloned.1.call-start = ((), (), s32[]{:S(2)}) async-start(), calls=%async_computation.5 | async-start | bytes 131072 | tf_op jit(solution)/shard_map/psum | solution.py:68
  82.2 1.3 collective-permute-start.1
  83.5 3.9 collective-permute-start.2
  102.3 239.6 %all-reduce.7.cloned.1.call-start = ((), (), s32[]{:S(2)}) async-start(), calls=%async_computation.6 | async-start | bytes 131072 | tf_op jit(solution)/shard_map/psum | solution.py:68
  220.2 0.8 copy-start.8
  220.2 245.4 %all-reduce.9.cloned.1.call-start = ((), (), s32[]{:S(2)}) async-start(), calls=%async_computation.7 | async-start | bytes 131072 | tf_op jit(solution)/shard_map/psum | solution.py:68
  344.0 245.4 %all-reduce.11.cloned.1.call-start = ((), (), s32[]{:S(2)}) async-start(), calls=%async_computation.8 | async-start | bytes 131072 | tf_op jit(solution)/shard_map/psum | solution.py:68
  468.4 144.0 %reduce-scatter.20.cloned.1.call-start = ((), (), s32[]{:S(2)}) async-start(), calls=%async_computation.11 | async-start | bytes 163840
  592.3 59.0 %reduce-scatter.22.cloned.1.call-start = ((), (), s32[]{:S(2)}) async-start(), calls=%async_computation.12 | async-start | bytes 163840
  613.2 1.3 collective-permute-start.3
  614.5 3.9 collective-permute-start.4
  633.7 52.8 %reduce-scatter.24.cloned.1.call-start = ((), (), s32[]{:S(2)}) async-start(), calls=%async_computation.13 | async-start | bytes 163840
  652.2 1.3 collective-permute-start.5
  668.9 0.8 copy-start.4
  668.9 0.9 copy-start.5
Sparse Core Ops, SparseCore 0:
  25.6 20.5 reduce-scatter.15
  64.0 17.3 reduce-scatter.17
  102.4 115.6 all-reduce.4
  223.5 118.3 all-reduce.6
  347.3 118.3 all-reduce.8
  471.1 118.3 all-reduce.10
  592.4 19.9 reduce-scatter.19
  633.8 17.4 reduce-scatter.21
  669.1 17.4 reduce-scatter.23
where the time goes:
time: 696 us; the launch traced here: 695 us
  waiting for transfers between devices  565 us (81%)
  blocking collectives  83.1 us (12%)
  local copies, waits for them, and re-layouts  16.8 us (2%)
  between operations  13.6 us (2%)
  matrix products  12.1 us (2%)
    psum x4, waiting for transfers between devices, block_sum(): return lax.psum(term, ('leaf', 'front'))  464 us
    unnamed x14, waiting for transfers between devices  92.4 us
    all_gather x4, blocking collectives, block_sum(): return lax.all_gather(piece, 'front', axis=1, tiled=True)  53.7 us
    all_gather x1, blocking collectives, body(): lax.all_gather(leaf_r, 'front', axis=1, tiled=True)  15.1 us
    all_gather x1, blocking collectives, body(): parent_x = lax.all_gather(outer_solution, 'front', axis=1, tiled=True)  14.3 us
  transfers between devices with their start and end apart: 15, of which 15 were waited for; matrix products, arithmetic and copies ran while one was open for 0% of the time, Pallas kernels for 0%

commit v1 on v0

--- a/solution.py
+++ b/solution.py
@@ -1,7 +1,185 @@
+import functools
 import jax
 import jax.numpy as jnp
 from jax import lax
+from jax.experimental import pallas as pl
+from jax.experimental.pallas import tpu as pltpu
 from jax.sharding import PartitionSpec as P
+
+HI = lax.Precision.HIGHEST
+
+
+def nn(left, right):
+    return lax.dot_general(
+        left, right, (((1,), (0,)), ((), ())), precision=HI, preferred_element_type=jnp.float32
+    )
+
+
+def nt(left, right):
+    return lax.dot_general(
+        left, right, (((1,), (1,)), ((), ())), precision=HI, preferred_element_type=jnp.float32
+    )
+
+
+def exchange(block, axis, mask):
+    count = lax.axis_size(axis)
+    return lax.ppermute(block, axis, [(src, src ^ mask) for src in range(count)])
+
+
+def call(kernel, outs, args, scratch=(), smem=()):
+    specs = [
+        pl.BlockSpec(memory_space=pltpu.SMEM if pos in smem else pltpu.VMEM)
+        for pos in range(len(args))
+    ]
+    return pl.pallas_call(
+        kernel,
+        out_shape=[jax.ShapeDtypeStruct(shape, jnp.float32) for shape in outs],
+        in_specs=specs,
+        out_specs=[pl.BlockSpec(memory_space=pltpu.VMEM) for _ in outs],
+        scratch_shapes=list(scratch),
+        cost_estimate=pl.CostEstimate(flops=1000000, bytes_accessed=1000000, transcendentals=0),
+    )(*args)
+
+
+class Plan:
+    def __init__(self, groups, fronts, rhs, upd, rows):
+        self.groups, self.fronts, self.rhs, self.upd, self.rows = groups, fronts, rhs, upd, rows
+        self.depth = groups.bit_length() - 1
+        self.full = fronts * rows
+        self.width = self.full + 128
+        self.share, self.offset, self.base, self.blocks = {}, {}, {}, {}
+        base = 0
+        for level in range(1, self.depth + 2):
+            self.blocks[level] = 2 ** min(level, self.depth)
+            self.share[level] = rows // self.blocks[level]
+            self.offset[level] = rows - (rows >> level - 1)
+            self.base[level] = base
+            base += fronts * self.share[level]
+
+    def label(self, level, group):
+        if level > self.depth:
+            return jnp.int32(0)
+        return (group // 2**level) * 2**level + 2 ** (level - 1)
+
+
+def pack_kernel(plan, lr, sr, li, si, lu, su, outer, leaf_out, sep_out):
+    half = plan.rhs // 2
+    full = plan.full
+    leaf_out[:, :full] = li[0]
+    leaf_out[:, full:] = jnp.concatenate([lr[0], lu[0], outer[:half]], axis=0).T
+    sep_out[:, :full] = si[0]
+    sep_out[:, full:] = jnp.concatenate([sr[0], su[0], outer[half:]], axis=0).T
+
+
+def one_hot(plan, pattern, kind, label):
+    ids = pattern[kind, pl.ds(label, 1), :]
+    rows = lax.broadcasted_iota(jnp.int32, (plan.full, plan.upd), 0)
+    return (rows == ids).astype(jnp.float32)
+
+
+def gathered_kernel(plan, where, *refs):
+    count = plan.fronts
+    leafs, seps = refs[:count], refs[count : 2 * count]
+    leaf_all, sep_all, x_part, y_part, update, y_leaf, outer_all, lanes = refs[2 * count :]
+    front = where[0]
+    for slot in range(count):
+        at = pl.multiple_of((front ^ slot) * plan.rows, plan.rows)
+        leaf_all[pl.ds(at, plan.rows), :] = leafs[slot][...]
+        lanes[pl.ds(at, plan.rows), :] = seps[slot][:, plan.full :]
+        for level in range(1, plan.depth + 2):
+            share, offset = plan.share[level], plan.offset[level]
+            piece = seps[slot][offset : offset + share, :]
+            dest = pl.multiple_of(plan.base[level] + (front ^ slot) * share, share)
+            sep_all[pl.ds(dest, share), :] = piece
+            if level >= 2:
+                x_part[pl.ds(pl.multiple_of(dest - plan.base[2], share), share), :] = piece
+            if level >= 3:
+                y_part[pl.ds(pl.multiple_of(dest - plan.base[3], share), share), :] = piece
+    flipped = leaf_all[:, plan.full :].T
+    leaf_y = nt(flipped[: plan.rhs], leaf_all[:, : plan.full])
+    y_leaf[...] = leaf_y
+    update[...] = nt(leaf_y, flipped[plan.rhs : plan.rhs + plan.upd])
+    half = plan.rhs // 2
+    outer_all[:half] = flipped[plan.rhs + plan.upd :]
+    outer_all[half:] = lanes[...].T[plan.rhs + plan.upd :]
+
+
+def assemble(plan, level, group, parts, out):
+    share, blocks = plan.share[level], plan.blocks[level]
+    for slot in range(blocks):
+        ref, start = parts[slot]
+        inner = (group & (blocks - 1)) ^ slot
+        for front in range(plan.fronts):
+            dest = pl.multiple_of(front * plan.rows + inner * share, share)
+            out[pl.ds(dest, share), :] = ref[start + front * share : start + (front + 1) * share, :]
+
+
+def forward_step(plan, level, group, whole, pattern, mine, other):
+    kind = 0 if level == 1 else 1
+    if level == 1:
+        labels = (group, group ^ 1)
+    else:
+        labels = (plan.label(level - 1, group), plan.label(level - 1, group ^ 2 ** (level - 1)))
+    flipped = whole[:, plan.full :].T
+    right = flipped[: plan.rhs]
+    block = flipped[plan.rhs : plan.rhs + plan.upd]
+    right = right - nt(mine, one_hot(plan, pattern, kind, labels[0]))
+    if other is not None:
+        right = right - nt(other, one_hot(plan, pattern, kind, labels[1]))
+    return nt(right, whole[:, : plan.full]), block
+
+
+def level_kernel(plan, level, where, pattern, mine, other, *refs):
+    blocks = plan.blocks[level]
+    parts, (whole, y_out, u_out) = refs[:blocks], refs[blocks:]
+    group = where[1]
+    starts = [plan.base[level] - (0 if slot < 2 else plan.base[2]) for slot in range(blocks)]
+    assemble(plan, level, group, list(zip(parts, starts)), whole)
+    y_level, block = forward_step(plan, level, group, whole, pattern, mine[...], other[...])
+    y_out[...] = y_level
+    u_out[...] = nt(y_level, block)
+
+
+def finish_kernel(plan, where, pattern, mine, other, *refs):
+    parts = refs[:8]
+    outer, leaf_all, y_leaf, whole1, y1, whole2, y2, out, whole3, whole4 = refs[8:]
+    group, front = where[1], where[0]
+    full = plan.full
+
+    def starts(level):
+        bases = [plan.base[1]] * 2 + [plan.base[2]] * 2 + [plan.base[3]] * 4
+        return [(parts[slot], plan.base[level] - bases[slot]) for slot in range(8)]
+
+    assemble(plan, 3, group, starts(3), whole3)
+    assemble(plan, 4, group, starts(4), whole4)
+    y3, block3 = forward_step(plan, 3, group, whole3, pattern, mine[...], other[...])
+    u3 = nt(y3, block3)
+    y4, block4 = forward_step(plan, 4, group, whole4, pattern, u3, None)
+    picked = nn(outer[...], one_hot(plan, pattern, 1, 0))
+    x4 = nn(y4 - nn(picked, block4), whole4[:, :full])
+    picked = nn(x4, one_hot(plan, pattern, 1, plan.label(3, group)))
+    x3 = nn(y3 - nn(picked, block3), whole3[:, :full])
+    picked = nn(x3, one_hot(plan, pattern, 1, plan.label(2, group)))
+    block2 = whole2[:, full:].T[plan.rhs : plan.rhs + plan.upd]
+    x2 = nn(y2[...] - nn(picked, block2), whole2[:, :full])
+    picked = nn(x2, one_hot(plan, pattern, 1, plan.label(1, group)))
+    block1 = whole1[:, full:].T[plan.rhs : plan.rhs + plan.upd]
+    x1 = nn(y1[...] - nn(picked, block1), whole1[:, :full])
+    picked = nn(x1, one_hot(plan, pattern, 0, group))
+    block0 = leaf_all[:, full:].T[plan.rhs : plan.rhs + plan.upd]
+    x0 = nn(y_leaf[...] - nn(picked, block0), leaf_all[:, :full])
+    sep_x = x4
+    for level, value in ((3, x3), (2, x2), (1, x1)):
+        sep_x = jnp.where(plan.label(level, group) == group, value, sep_x)
+
+    def own_columns(value):
+        result = value[:, : plan.rows]
+        for slot in range(1, plan.fronts):
+            result = jnp.where(front == slot, value[:, slot * plan.rows : (slot + 1) * plan.rows], result)
+        return result
+
+    out[0, 0] = own_columns(x0)
+    out[1, 0] = own_columns(sep_x)
 
 
 def partner(block, axis, distance):
@@ -30,7 +208,7 @@
     )
 
 
-def body(
+def general(
     leaf_rhs, sep_rhs, leaf_inverse, sep_inverse, leaf_block, sep_block, pattern, outer_solution
 ):
     group_count = lax.axis_size("leaf")
@@ -106,6 +284,79 @@
     return jnp.stack([leaf_x, sep_x])[:, None]
 
 
+def chain(
+    plan, leaf_rhs, sep_rhs, leaf_inverse, sep_inverse, leaf_block, sep_block, pattern, outer
+):
+    full, rows, rhs, upd, width = plan.full, plan.rows, plan.rhs, plan.upd, plan.width
+    group = lax.axis_index("leaf")
+    where = jnp.stack([lax.axis_index("front"), group]).astype(jnp.int32)
+    leaf_pack, sep_pack = call(
+        functools.partial(pack_kernel, plan),
+        [(rows, width)] * 2,
+        (leaf_rhs, sep_rhs, leaf_inverse, sep_inverse, leaf_block, sep_block, outer),
+    )
+    leafs, seps = [leaf_pack] + [None] * 3, [sep_pack] + [None] * 3
+    for mask in (3, 2, 1):
+        leafs[mask] = exchange(leaf_pack, "front", mask)
+        seps[mask] = exchange(sep_pack, "front", mask)
+    last = plan.fronts * rows
+    leaf_all, sep_all, x_part, y_part, update, y_leaf, outer_all = call(
+        functools.partial(gathered_kernel, plan),
+        [
+            (full, width),
+            (full, width),
+            (last - plan.base[2], width),
+            (last - plan.base[3], width),
+            (rhs, upd),
+            (rhs, full),
+            (rhs, full),
+        ],
+        (where, *leafs, *seps),
+        scratch=[pltpu.VMEM((full, 128), jnp.float32)],
+        smem=(0,),
+    )
+    update_other = exchange(update, "leaf", 1)
+    sep_core = exchange(sep_all, "leaf", 1)
+    by_x = exchange(x_part, "leaf", 2)
+    by_y = exchange(y_part, "leaf", 4)
+    by_xy = exchange(y_part, "leaf", 6)
+    whole1, y1, u1 = call(
+        functools.partial(level_kernel, plan, 1),
+        [(full, width), (rhs, full), (rhs, upd)],
+        (where, pattern, update, update_other, sep_all, sep_core),
+        smem=(0,),
+    )
+    u1_other = exchange(u1, "leaf", 2)
+    by_x_core = exchange(by_x, "leaf", 1)
+    whole2, y2, u2 = call(
+        functools.partial(level_kernel, plan, 2),
+        [(full, width), (rhs, full), (rhs, upd)],
+        (where, pattern, u1, u1_other, sep_all, sep_core, by_x, by_x_core),
+        smem=(0,),
+    )
+    u2_other = exchange(u2, "leaf", 4)
+    by_y_core = exchange(by_y, "leaf", 1)
+    by_xy_core = exchange(by_xy, "leaf", 1)
+    parts = (sep_all, sep_core, by_x, by_x_core, by_y, by_y_core, by_xy, by_xy_core)
+    (out,) = call(
+        functools.partial(finish_kernel, plan),
+        [(2, 1, rhs, rows)],
+        (where, pattern, u2, u2_other, *parts, outer_all, leaf_all, y_leaf, whole1, y1, whole2, y2),
+        scratch=[pltpu.VMEM((full, width), jnp.float32)] * 2,
+        smem=(0,),
+    )
+    return out
+
+
+def body(*args):
+    groups, fronts = lax.axis_size("leaf"), lax.axis_size("front")
+    rhs, rows, upd = args[0].shape[1], args[0].shape[2], args[4].shape[1]
+    plan = Plan(groups, fronts, rhs, upd, rows)
+    if (groups, fronts) == (8, 4) and rows == 64 and rhs + upd + rhs // 2 == 128:
+        return chain(plan, *args)
+    return general(*args)
+
+
 def solution(mesh):
     placed = (
         P("leaf", None, "front"),

time: 696 us -> 70 us (0.10)
  waiting for transfers between devices: 565 us -> 22.9 us
  blocking collectives: 83.1 us -> 0 us
  starting transfers between devices: 3.61 us -> 24.3 us
  Pallas kernels: 0 us -> 18 us
  between operations: 13.6 us -> 0.09 us
  local copies, waits for them, and re-layouts: 16.8 us -> 3.84 us
  matrix products: 12.1 us -> 0 us
    psum x4 -> x0, waiting for transfers between devices: 464 us -> none  [block_sum(): return lax.psum(term, ('leaf', 'front'))]
    unnamed x14 -> x0, waiting for transfers between devices: 92.4 us -> none
    all_gather x6 -> x0, blocking collectives: 83.1 us -> none  [the longest x4 53.7 us: block_sum(): return lax.all_gather(piece, 'front', axis=1, tiled=True)]
    ppermute x6 -> x16, starting transfers between devices: 3.27 us -> 24.3 us  [exchange(): lax.ppermute(block, axis, [(src, src ^ mask) for src in range(count)])]
    pallas_call x0 -> x5, Pallas kernels: none -> 18 us  [call(): pl.pallas_call(kernel, out_shape=[jax.ShapeDtypeStruct(shape, jnp.float32...]
    ppermute x6 -> x16, waiting for transfers between devices: 8.38 us -> 22.9 us  [exchange(): lax.ppermute(block, axis, [(src, src ^ mask) for src in range(count)])]
    dot_general x20 -> x0, matrix products: 8.97 us -> none  [the longest x11 5.28 us: times_rows(): jnp.dot(vectors, matrix, precision=lax.Precision.HIGHEST, preferred_eleme...]
  transfers between devices with their start and end apart: 15 -> 16, of which waited for: 15 -> 8; matrix products, arithmetic and copies ran while one was open for 0% -> 1% of each run, Pallas kernels for 0% -> 8%
where the time goes in v1:
time: 70 us; the launch traced here: 69.7 us
  starting transfers between devices  24.3 us (35%)
  waiting for transfers between devices  22.9 us (33%)
  Pallas kernels  18 us (26%)
  local copies, waits for them, and re-layouts  3.84 us (5%)
    ppermute x16, starting transfers between devices, exchange(): lax.ppermute(block, axis, [(src, src ^ mask) for src in range(count)])  24.3 us
    ppermute x16, waiting for transfers between devices, exchange(): lax.ppermute(block, axis, [(src, src ^ mask) for src in range(count)])  22.9 us
    pallas_call x5, Pallas kernels, call(): pl.pallas_call(kernel, out_shape=[jax.ShapeDtypeStruct(shape, jnp.float32...  18 us
    unnamed x32, local copies, waits for them, and re-layouts  3.84 us
  transfers between devices with their start and end apart: 16, of which 8 were waited for; matrix products, arithmetic and copies ran while one was open for 1% of the time, Pallas kernels for 8%

profile of v1, /device:TPU:0, one launch (start us, length us, event | category | flops | bytes accessed | tf_op | source)
XLA Modules:
  0.0 69.7 jit_solution(12033831035646924071)
XLA Ops:
  0.0 1.7 %shard_map.82 = (f32[64,384]{1,0:T(8,128)}, f32[64,384]{1,0:T(8,128)}) custom-call(f32[1,64,64]{2,1,0:T(8,128)} %lr.1, f32[1,64,64]{2,1,0:T(8,128)} %sr.1, f32[1,64,256]{2,1,0:T(8,128)} %li.1, f32[1,64,256]{2,1,0:T(8,128)} %si.1, f32[1,32,64]{2,1,0:T(8,128)} %lu.1, f32[1,32,64]{2,1,0:T(8,128)} %su.1, f32[64,64]{1,0:T(8,128)} %outer.1), custom_call_target="tpu_custom_call" | custom-call | flops 1000000 | bytes 1000000 | tf_op jit(solution)/shard_map/pallas_call | solution.py:34
  1.7 5.0 %collective-permute-start.2 = (f32[64,384]{1,0:T(8,128)}, f32[64,384]{1,0:T(8,128)S(1)}, u32[]{:S(2)}, u32[]{:S(2)}) collective-permute-start(f32[64,384]{1,0:T(8,128)} %get-tuple-element.20.refs_0_), channel_id=1, source_target_pairs={{0,3},{1,2},{2,1},{3,0},{4,7},{5,6},{6,5},{7,4},{8,11},{9,10},{10,... | collective-permute-start | bytes 294920 | tf_op jit(solution)/shard_map/ppermute | solution.py:26
  6.7 0.0 collective-permute-start.1
  6.7 0.6 collective-permute-start
  7.3 3.8 %collective-permute-start.5 = (f32[64,384]{1,0:T(8,128)}, f32[64,384]{1,0:T(8,128)S(1)}, u32[]{:S(2)}, u32[]{:S(2)}) collective-permute-start(f32[64,384]{1,0:T(8,128)} %get-tuple-element.21.refs_4_), channel_id=1, source_target_pairs={{0,3},{1,2},{2,1},{3,0},{4,7},{5,6},{6,5},{7,4},{8,11},{9,10},{10,... | collective-permute-start | bytes 294920 | tf_op jit(solution)/shard_map/ppermute | solution.py:26
  11.1 0.0 collective-permute-start.4
  11.1 0.0 collective-permute-done.2.refs_3_
  11.1 6.7 %collective-permute-start.3 = (f32[64,384]{1,0:T(8,128)}, f32[64,384]{1,0:T(8,128)S(1)}, u32[]{:S(2)}, u32[]{:S(2)}) collective-permute-start(f32[64,384]{1,0:T(8,128)} %get-tuple-element.21.refs_4_), channel_id=1, source_target_pairs={{0,1},{1,0},{2,3},{3,2},{4,5},{5,4},{6,7},{7,6},{8,9},{9,8},{10,11... | collective-permute-start | bytes 294920 | tf_op jit(solution)/shard_map/ppermute | solution.py:26
  17.9 0.6 pad_add_fusion.where
  18.4 1.9 %collective-permute-done.1.refs_2_ = f32[64,384]{1,0:T(8,128)S(1)} collective-permute-done((f32[64,384]{1,0:T(8,128)}, f32[64,384]{1,0:T(8,128)S(1)}, u32[]{:S(2)}, u32[]{:S(2)}) %collective-permute-start.1) | collective-permute-done | bytes 98336 | tf_op jit(solution)/shard_map/ppermute | solution.py:26
  20.4 0.0 copy-start.4
  20.4 0.0 collective-permute-done.refs_1_
  20.4 0.0 collective-permute-done.5.refs_7_
  20.4 0.0 copy-start.6
  20.4 3.2 %collective-permute-done.4.refs_6_ = f32[64,384]{1,0:T(8,128)S(1)} collective-permute-done((f32[64,384]{1,0:T(8,128)}, f32[64,384]{1,0:T(8,128)S(1)}, u32[]{:S(2)}, u32[]{:S(2)}) %collective-permute-start.4) | collective-permute-done | bytes 98336 | tf_op jit(solution)/shard_map/ppermute | solution.py:26
  23.6 0.0 copy-start.7
  23.6 0.0 collective-permute-done.3.refs_5_
  23.6 0.0 copy-done.3
  23.6 0.0 copy-done.4
  23.6 0.0 copy-done.5
  23.7 0.0 copy-done.6
  23.7 0.6 copy-done.7
  24.3 0.0 copy-start.8
  24.3 0.6 copy-done.8
  24.9 2.8 %shard_map.83 = (f32[256,384]{1,0:T(8,128)}, f32[256,384]{1,0:T(8,128)}, f32[128,384]{1,0:T(8,128)}, f32[64,384]{1,0:T(8,128)}, f32[64,32]{1,0:T(8,128)}, /*index=5*/f32[64,256]{1,0:T(8,128)}, f32[64,256]{1,0:T(8,128)}) custom-call(s32[2]{0:T(128)} %pad_add_fusion.where, f32[64,384]{1,0:T(8,128)} %get-tuple-element.20.refs_0_, f32[64,384]{1,0:T(8,128)} %copy-done.5, ...), custom_call_target="tpu_custom_call" | custom-call | flops 1000000 | bytes 1000000 | tf_op jit(solution)/shard_map/pallas_call | solution.py:34
  27.7 0.0 collective-permute-start.7
  27.7 1.6 %collective-permute-start.9 = (f32[128,384]{1,0:T(8,128)}, f32[128,384]{1,0:T(8,128)S(1)}, u32[]{:S(2)}, u32[]{:S(2)}) collective-permute-start(f32[128,384]{1,0:T(8,128)} %get-tuple-element.25), channel_id=1, source_target_pairs={{0,8},{4,12},{8,0},{12,4},{16,24},{20,28},{24,16},{28,20},{1,9},{5... | collective-permute-start | bytes 589832 | tf_op jit(solution)/shard_map/ppermute | solution.py:26
  29.3 6.0 %collective-permute-done.9.refs_2_ = f32[128,384]{1,0:T(8,128)S(1)} collective-permute-done((f32[128,384]{1,0:T(8,128)}, f32[128,384]{1,0:T(8,128)S(1)}, u32[]{:S(2)}, u32[]{:S(2)}) %collective-permute-start.9) | collective-permute-done | bytes 196640 | tf_op jit(solution)/shard_map/ppermute | solution.py:26
  35.3 0.0 copy-start.1
  35.3 0.0 collective-permute-start.10
  35.3 2.4 %collective-permute-start.14 = (f32[64,384]{1,0:T(8,128)}, f32[64,384]{1,0:T(8,128)S(1)}, u32[]{:S(2)}, u32[]{:S(2)}) collective-permute-start(f32[64,384]{1,0:T(8,128)} %get-tuple-element.27), channel_id=1, source_target_pairs={{0,24},{4,28},{8,16},{12,20},{16,8},{20,12},{24,0},{28,4},{1,25},{... | collective-permute-start | bytes 294920 | tf_op jit(solution)/shard_map/ppermute | solution.py:26
  37.7 0.5 collective-permute-start.12
  38.2 3.4 %collective-permute-done.14.refs_6_ = f32[64,384]{1,0:T(8,128)S(1)} collective-permute-done((f32[64,384]{1,0:T(8,128)}, f32[64,384]{1,0:T(8,128)S(1)}, u32[]{:S(2)}, u32[]{:S(2)}) %collective-permute-start.14) | collective-permute-done | bytes 98336 | tf_op jit(solution)/shard_map/ppermute | solution.py:26
  41.7 0.0 copy-start.9
  41.7 0.0 collective-permute-start.15
  41.7 2.0 %collective-permute-done.12.refs_4_ = f32[64,384]{1,0:T(8,128)S(1)} collective-permute-done((f32[64,384]{1,0:T(8,128)}, f32[64,384]{1,0:T(8,128)S(1)}, u32[]{:S(2)}, u32[]{:S(2)}) %collective-permute-start.12) | collective-permute-done | bytes 98336 | tf_op jit(solution)/shard_map/ppermute | solution.py:26
  43.7 0.0 copy-start.10
  43.7 0.0 collective-permute-start.13
  43.7 0.5 collective-permute-start.6
  44.2 1.1 %collective-permute-done.6.other = f32[64,32]{1,0:T(8,128)S(1)} collective-permute-done((f32[64,32]{1,0:T(8,128)}, f32[64,32]{1,0:T(8,128)S(1)}, u32[]{:S(2)}, u32[]{:S(2)}) %collective-permute-start.6) | collective-permute-done | bytes 8224 | tf_op jit(solution)/shard_map/ppermute | solution.py:26
  45.3 0.0 copy-start.14
  45.3 0.0 collective-permute-done.7.refs_1_
  45.3 0.6 copy-done.14
  45.9 0.0 copy-start
  45.9 0.8 %copy-done = f32[256,384]{1,0:T(8,128)} copy-done((f32[256,384]{1,0:T(8,128)}, f32[256,384]{1,0:T(8,128)S(1)}, u32[]{:S(2)}) %copy-start) | copy-done | bytes 393240
  46.6 2.7 %shard_map.84 = (f32[256,384]{1,0:T(8,128)}, f32[64,256]{1,0:T(8,128)}, f32[64,32]{1,0:T(8,128)}) custom-call(s32[2]{0:T(128)} %pad_add_fusion.where, s32[2,8,32]{2,1,0:T(8,128)} %pattern.5, f32[64,32]{1,0:T(8,128)} %get-tuple-element.22.mine, f32[64,32]{1,0:T(8,128)} %copy-done.14, f32[256,384]{1,0:T(8,128)} %get-tuple-element.23.refs_0_, f32[256,384]{1,0:T(8,128)} %copy-done), custom_call_target="tpu_custom_call" | custom-call | flops 1000000 | bytes 1000000 | tf_op jit(solution)/shard_map/pallas_call | solution.py:34
  49.4 0.0 copy-done.9
  49.4 0.0 copy-done.10
  49.4 1.6 %collective-permute-start.8 = (f32[64,32]{1,0:T(8,128)}, f32[64,32]{1,0:T(8,128)S(1)}, u32[]{:S(2)}, u32[]{:S(2)}) collective-permute-start(f32[64,32]{1,0:T(8,128)} %get-tuple-element.24.mine), channel_id=1, source_target_pairs={{0,8},{4,12},{8,0},{12,4},{16,24},{20,28},{24,16},{28,20},{1,9},{5... | collective-permute-start | bytes 24584 | tf_op jit(solution)/shard_map/ppermute | solution.py:26
  50.9 0.0 collective-permute-done.10.refs_3_
  50.9 2.6 %collective-permute-done.8.other = f32[64,32]{1,0:T(8,128)S(1)} collective-permute-done((f32[64,32]{1,0:T(8,128)}, f32[64,32]{1,0:T(8,128)S(1)}, u32[]{:S(2)}, u32[]{:S(2)}) %collective-permute-start.8) | collective-permute-done | bytes 8224 | tf_op jit(solution)/shard_map/ppermute | solution.py:26
  53.6 0.0 copy-done.1
  53.6 0.0 copy-done.2
  53.6 0.6 copy-done.15
  54.2 2.9 %shard_map.85 = (f32[256,384]{1,0:T(8,128)}, f32[64,256]{1,0:T(8,128)}, f32[64,32]{1,0:T(8,128)}) custom-call(s32[2]{0:T(128)} %pad_add_fusion.where, s32[2,8,32]{2,1,0:T(8,128)} %pattern.5, f32[64,32]{1,0:T(8,128)} %get-tuple-element.24.mine, f32[64,32]{1,0:T(8,128)} %copy-done.15, f32[256,384]{1,0:T(8,128)} %get-tuple-element.23.refs_0_, ...), custom_call_target="tpu_custom_call" | custom-call | flops 1000000 | bytes 1000000 | tf_op jit(solution)/shard_map/pallas_call | solution.py:34
  57.0 1.5 %collective-permute-start.11 = (f32[64,32]{1,0:T(8,128)}, f32[64,32]{1,0:T(8,128)S(1)}, u32[]{:S(2)}, u32[]{:S(2)}) collective-permute-start(f32[64,32]{1,0:T(8,128)} %get-tuple-element.26.mine), channel_id=1, source_target_pairs={{0,16},{4,20},{8,24},{12,28},{16,0},{20,4},{24,8},{28,12},{1,17},{... | collective-permute-start | bytes 24584 | tf_op jit(solution)/shard_map/ppermute | solution.py:26
  58.6 0.0 collective-permute-done.15.refs_7_
  58.6 0.0 collective-permute-done.13.refs_5_
  58.6 0.0 copy-start.12
  58.6 2.6 %collective-permute-done.11.other = f32[64,32]{1,0:T(8,128)S(1)} collective-permute-done((f32[64,32]{1,0:T(8,128)}, f32[64,32]{1,0:T(8,128)S(1)}, u32[]{:S(2)}, u32[]{:S(2)}) %collective-permute-start.11) | collective-permute-done | bytes 8224 | tf_op jit(solution)/shard_map/ppermute | solution.py:26
  61.2 0.0 copy-done.11
  61.2 0.0 copy-done.12
  61.2 0.6 copy-done.13
  61.8 8.0 %shard_map.86 = f32[2,1,64,64]{3,2,1,0:T(8,128)} custom-call(s32[2]{0:T(128)} %pad_add_fusion.where, s32[2,8,32]{2,1,0:T(8,128)} %pattern.5, f32[64,32]{1,0:T(8,128)} %get-tuple-element.26.mine, f32[64,32]{1,0:T(8,128)} %copy-done.13, f32[256,384]{1,0:T(8,128)} %get-tuple-element.23.refs_0_, f32[256,384]{1,0:T(8,128)} %copy-done, f32[128,384]{1,0:T(8,128)} %copy-done.1, ...), custom_call_target="tpu_custom_call" | custom-call | flops 1000000 | bytes 1000000 | tf_op jit(solution)/shard_map/pallas_call | solution.py:34
  (6 shorter events, 0.0 us)
Async XLA Ops:
  1.7 9.4 %collective-permute-start.2 = (f32[64,384]{1,0:T(8,128)}, f32[64,384]{1,0:T(8,128)S(1)}, u32[]{:S(2)}, u32[]{:S(2)}) collective-permute-start(f32[64,384]{1,0:T(8,128)} %get-tuple-element.20.refs_0_), channel_id=1, source_target_pairs={{0,3},{1,2},{2,1},{3,0},{4,7},{5,6},{6,5},{7,4},{8,11},{9,10},{10,... | collective-permute-start | bytes 294920 | tf_op jit(solution)/shard_map/ppermute | solution.py:26
  6.7 13.6 %collective-permute-start.1 = (f32[64,384]{1,0:T(8,128)}, f32[64,384]{1,0:T(8,128)S(1)}, u32[]{:S(2)}, u32[]{:S(2)}) collective-permute-start(f32[64,384]{1,0:T(8,128)} %get-tuple-element.20.refs_0_), channel_id=1, source_target_pairs={{0,2},{1,3},{2,0},{3,1},{4,6},{5,7},{6,4},{7,5},{8,10},{9,11},{10,... | collective-permute-start | bytes 294920 | tf_op jit(solution)/shard_map/ppermute | solution.py:26
  6.7 13.7 %collective-permute-start = (f32[64,384]{1,0:T(8,128)}, f32[64,384]{1,0:T(8,128)S(1)}, u32[]{:S(2)}, u32[]{:S(2)}) collective-permute-start(f32[64,384]{1,0:T(8,128)} %get-tuple-element.20.refs_0_), channel_id=1, source_target_pairs={{0,1},{1,0},{2,3},{3,2},{4,5},{5,4},{6,7},{7,6},{8,9},{9,8},{10,11... | collective-permute-start | bytes 294920 | tf_op jit(solution)/shard_map/ppermute | solution.py:26
  7.3 13.1 %collective-permute-start.5 = (f32[64,384]{1,0:T(8,128)}, f32[64,384]{1,0:T(8,128)S(1)}, u32[]{:S(2)}, u32[]{:S(2)}) collective-permute-start(f32[64,384]{1,0:T(8,128)} %get-tuple-element.21.refs_4_), channel_id=1, source_target_pairs={{0,3},{1,2},{2,1},{3,0},{4,7},{5,6},{6,5},{7,4},{8,11},{9,10},{10,... | collective-permute-start | bytes 294920 | tf_op jit(solution)/shard_map/ppermute | solution.py:26
  11.1 12.5 %collective-permute-start.4 = (f32[64,384]{1,0:T(8,128)}, f32[64,384]{1,0:T(8,128)S(1)}, u32[]{:S(2)}, u32[]{:S(2)}) collective-permute-start(f32[64,384]{1,0:T(8,128)} %get-tuple-element.21.refs_4_), channel_id=1, source_target_pairs={{0,2},{1,3},{2,0},{3,1},{4,6},{5,7},{6,4},{7,5},{8,10},{9,11},{10,... | collective-permute-start | bytes 294920 | tf_op jit(solution)/shard_map/ppermute | solution.py:26
  11.1 12.5 %copy-start.3 = (f32[64,384]{1,0:T(8,128)}, f32[64,384]{1,0:T(8,128)S(1)}, u32[]{:S(2)}) copy-start(f32[64,384]{1,0:T(8,128)S(1)} %collective-permute-done.2.refs_3_) | copy-start | bytes 294916
  11.1 12.5 %collective-permute-start.3 = (f32[64,384]{1,0:T(8,128)}, f32[64,384]{1,0:T(8,128)S(1)}, u32[]{:S(2)}, u32[]{:S(2)}) collective-permute-start(f32[64,384]{1,0:T(8,128)} %get-tuple-element.21.refs_4_), channel_id=1, source_target_pairs={{0,1},{1,0},{2,3},{3,2},{4,5},{5,4},{6,7},{7,6},{8,9},{9,8},{10,11... | collective-permute-start | bytes 294920 | tf_op jit(solution)/shard_map/ppermute | solution.py:26
  20.4 3.3 %copy-start.4 = (f32[64,384]{1,0:T(8,128)}, f32[64,384]{1,0:T(8,128)S(1)}, u32[]{:S(2)}) copy-start(f32[64,384]{1,0:T(8,128)S(1)} %collective-permute-done.1.refs_2_) | copy-start | bytes 294916
  20.4 3.3 %copy-start.5 = (f32[64,384]{1,0:T(8,128)}, f32[64,384]{1,0:T(8,128)S(1)}, u32[]{:S(2)}) copy-start(f32[64,384]{1,0:T(8,128)S(1)} %collective-permute-done.refs_1_) | copy-start | bytes 294916
  20.4 3.3 %copy-start.6 = (f32[64,384]{1,0:T(8,128)}, f32[64,384]{1,0:T(8,128)S(1)}, u32[]{:S(2)}) copy-start(f32[64,384]{1,0:T(8,128)S(1)} %collective-permute-done.5.refs_7_) | copy-start | bytes 294916
  23.6 0.6 copy-start.7
  24.3 0.6 copy-start.8
  27.7 17.5 %collective-permute-start.7 = (f32[256,384]{1,0:T(8,128)}, f32[256,384]{1,0:T(8,128)S(1)}, u32[]{:S(2)}, u32[]{:S(2)}) collective-permute-start(f32[256,384]{1,0:T(8,128)} %get-tuple-element.23.refs_0_), channel_id=1, source_target_pairs={{0,4},{4,0},{8,12},{12,8},{16,20},{20,16},{24,28},{28,24},{1,5},{5... | collective-permute-start | bytes 1179656 | tf_op jit(solution)/shard_map/ppermute | solution.py:26
  27.7 7.5 %collective-permute-start.9 = (f32[128,384]{1,0:T(8,128)}, f32[128,384]{1,0:T(8,128)S(1)}, u32[]{:S(2)}, u32[]{:S(2)}) collective-permute-start(f32[128,384]{1,0:T(8,128)} %get-tuple-element.25), channel_id=1, source_target_pairs={{0,8},{4,12},{8,0},{12,4},{16,24},{20,28},{24,16},{28,20},{1,9},{5... | collective-permute-start | bytes 589832 | tf_op jit(solution)/shard_map/ppermute | solution.py:26
  35.3 18.3 %copy-start.1 = (f32[128,384]{1,0:T(8,128)}, f32[128,384]{1,0:T(8,128)S(1)}, u32[]{:S(2)}) copy-start(f32[128,384]{1,0:T(8,128)S(1)} %collective-permute-done.9.refs_2_) | copy-start | bytes 589828
  35.3 15.7 %collective-permute-start.10 = (f32[128,384]{1,0:T(8,128)S(1)}, f32[128,384]{1,0:T(8,128)S(1)}, u32[]{:S(2)}, u32[]{:S(2)}) collective-permute-start(f32[128,384]{1,0:T(8,128)S(1)} %collective-permute-done.9.refs_2_), channel_id=1, source_target_pairs={{0,4},{4,0},{8,12},{12,8},{16,20},{20,16},{24,28},{28,24},{1,5},{5... | collective-permute-start | bytes 589832 | tf_op jit(solution)/shard_map/ppermute | solution.py:26
  35.3 6.4 %collective-permute-start.14 = (f32[64,384]{1,0:T(8,128)}, f32[64,384]{1,0:T(8,128)S(1)}, u32[]{:S(2)}, u32[]{:S(2)}) collective-permute-start(f32[64,384]{1,0:T(8,128)} %get-tuple-element.27), channel_id=1, source_target_pairs={{0,24},{4,28},{8,16},{12,20},{16,8},{20,12},{24,0},{28,4},{1,25},{... | collective-permute-start | bytes 294920 | tf_op jit(solution)/shard_map/ppermute | solution.py:26
  37.7 6.0 %collective-permute-start.12 = (f32[64,384]{1,0:T(8,128)}, f32[64,384]{1,0:T(8,128)S(1)}, u32[]{:S(2)}, u32[]{:S(2)}) collective-permute-start(f32[64,384]{1,0:T(8,128)} %get-tuple-element.27), channel_id=1, source_target_pairs={{0,16},{4,20},{8,24},{12,28},{16,0},{20,4},{24,8},{28,12},{1,17},{... | collective-permute-start | bytes 294920 | tf_op jit(solution)/shard_map/ppermute | solution.py:26
  41.7 7.7 %copy-start.9 = (f32[64,384]{1,0:T(8,128)}, f32[64,384]{1,0:T(8,128)S(1)}, u32[]{:S(2)}) copy-start(f32[64,384]{1,0:T(8,128)S(1)} %collective-permute-done.14.refs_6_) | copy-start | bytes 294916
  41.7 16.9 %collective-permute-start.15 = (f32[64,384]{1,0:T(8,128)S(1)}, f32[64,384]{1,0:T(8,128)S(1)}, u32[]{:S(2)}, u32[]{:S(2)}) collective-permute-start(f32[64,384]{1,0:T(8,128)S(1)} %collective-permute-done.14.refs_6_), channel_id=1, source_target_pairs={{0,4},{4,0},{8,12},{12,8},{16,20},{20,16},{24,28},{28,24},{1,5},{5... | collective-permute-start | bytes 294920 | tf_op jit(solution)/shard_map/ppermute | solution.py:26
  43.7 5.7 %copy-start.10 = (f32[64,384]{1,0:T(8,128)}, f32[64,384]{1,0:T(8,128)S(1)}, u32[]{:S(2)}) copy-start(f32[64,384]{1,0:T(8,128)S(1)} %collective-permute-done.12.refs_4_) | copy-start | bytes 294916
  43.7 14.9 %collective-permute-start.13 = (f32[64,384]{1,0:T(8,128)S(1)}, f32[64,384]{1,0:T(8,128)S(1)}, u32[]{:S(2)}, u32[]{:S(2)}) collective-permute-start(f32[64,384]{1,0:T(8,128)S(1)} %collective-permute-done.12.refs_4_), channel_id=1, source_target_pairs={{0,4},{4,0},{8,12},{12,8},{16,20},{20,16},{24,28},{28,24},{1,5},{5... | collective-permute-start | bytes 294920 | tf_op jit(solution)/shard_map/ppermute | solution.py:26
  43.7 1.5 %collective-permute-start.6 = (f32[64,32]{1,0:T(8,128)}, f32[64,32]{1,0:T(8,128)S(1)}, u32[]{:S(2)}, u32[]{:S(2)}) collective-permute-start(f32[64,32]{1,0:T(8,128)} %get-tuple-element.22.mine), channel_id=1, source_target_pairs={{0,4},{4,0},{8,12},{12,8},{16,20},{20,16},{24,28},{28,24},{1,5},{5... | collective-permute-start | bytes 24584 | tf_op jit(solution)/shard_map/ppermute | solution.py:26
  45.3 0.6 copy-start.14
  45.9 0.8 %copy-start = (f32[256,384]{1,0:T(8,128)}, f32[256,384]{1,0:T(8,128)S(1)}, u32[]{:S(2)}) copy-start(f32[256,384]{1,0:T(8,128)S(1)} %collective-permute-done.7.refs_1_) | copy-start | bytes 1179652
  49.4 4.2 %collective-permute-start.8 = (f32[64,32]{1,0:T(8,128)}, f32[64,32]{1,0:T(8,128)S(1)}, u32[]{:S(2)}, u32[]{:S(2)}) collective-permute-start(f32[64,32]{1,0:T(8,128)} %get-tuple-element.24.mine), channel_id=1, source_target_pairs={{0,8},{4,12},{8,0},{12,4},{16,24},{20,28},{24,16},{28,20},{1,9},{5... | collective-permute-start | bytes 24584 | tf_op jit(solution)/shard_map/ppermute | solution.py:26
  50.9 2.6 %copy-start.2 = (f32[128,384]{1,0:T(8,128)}, f32[128,384]{1,0:T(8,128)S(1)}, u32[]{:S(2)}) copy-start(f32[128,384]{1,0:T(8,128)S(1)} %collective-permute-done.10.refs_3_) | copy-start | bytes 589828
  53.6 0.6 copy-start.15
  57.0 4.1 %collective-permute-start.11 = (f32[64,32]{1,0:T(8,128)}, f32[64,32]{1,0:T(8,128)S(1)}, u32[]{:S(2)}, u32[]{:S(2)}) collective-permute-start(f32[64,32]{1,0:T(8,128)} %get-tuple-element.26.mine), channel_id=1, source_target_pairs={{0,16},{4,20},{8,24},{12,28},{16,0},{20,4},{24,8},{28,12},{1,17},{... | collective-permute-start | bytes 24584 | tf_op jit(solution)/shard_map/ppermute | solution.py:26
  58.6 2.6 %copy-start.11 = (f32[64,384]{1,0:T(8,128)}, f32[64,384]{1,0:T(8,128)S(1)}, u32[]{:S(2)}) copy-start(f32[64,384]{1,0:T(8,128)S(1)} %collective-permute-done.15.refs_7_) | copy-start | bytes 294916
  58.6 2.6 %copy-start.12 = (f32[64,384]{1,0:T(8,128)}, f32[64,384]{1,0:T(8,128)S(1)}, u32[]{:S(2)}) copy-start(f32[64,384]{1,0:T(8,128)S(1)} %collective-permute-done.13.refs_5_) | copy-start | bytes 294916
  61.2 0.6 copy-start.13

commit v2 on v0

--- a/solution.py
+++ b/solution.py
@@ -1,7 +1,233 @@
+import functools
 import jax
 import jax.numpy as jnp
 from jax import lax
+from jax.experimental import pallas as pl
+from jax.experimental.pallas import tpu as pltpu
 from jax.sharding import PartitionSpec as P
+
+def halves(value):
+    high = value.astype(jnp.bfloat16)
+    return high, (value - high.astype(jnp.float32)).astype(jnp.bfloat16)
+
+
+def product(left, right, side):
+    def term(one, two):
+        return lax.dot_general(
+            one, two, (((1,), (side,)), ((), ())), preferred_element_type=jnp.float32
+        )
+
+    (left_high, left_low), (right_high, right_low) = halves(left), halves(right)
+    return term(left_high, right_high) + (term(left_high, right_low) + term(left_low, right_high))
+
+
+def nn(left, right):
+    return product(left, right, 0)
+
+
+def nt(left, right):
+    return product(left, right, 1)
+
+
+def exchange(block, axis, mask):
+    count = lax.axis_size(axis)
+    return lax.ppermute(block, axis, [(src, src ^ mask) for src in range(count)])
+
+
+def call(kernel, outs, args, scratch=(), chip=True, cost=1000):
+    if chip:
+        args = [
+            pltpu.with_memory_space_constraint(arg, pltpu.VMEM)
+            if arg.ndim == 2 and arg.dtype == jnp.float32
+            else arg
+            for arg in args
+        ]
+    return pl.pallas_call(
+        kernel,
+        out_shape=[
+            pltpu.VMEM(shape, jnp.float32)
+            if len(shape) < 4
+            else jax.ShapeDtypeStruct(shape, jnp.float32)
+            for shape in outs
+        ],
+        in_specs=[pl.BlockSpec(memory_space=pltpu.VMEM) for _ in args],
+        out_specs=[pl.BlockSpec(memory_space=pltpu.VMEM) for _ in outs],
+        scratch_shapes=list(scratch),
+        compiler_params=pltpu.CompilerParams(vmem_limit_bytes=8 << 20) if chip else None,
+        cost_estimate=pl.CostEstimate(flops=cost, bytes_accessed=cost, transcendentals=0),
+    )(*args)
+
+
+class Plan:
+    def __init__(self, groups, fronts, rhs, upd, rows):
+        self.groups, self.fronts, self.rhs, self.upd, self.rows = groups, fronts, rhs, upd, rows
+        self.depth = groups.bit_length() - 1
+        self.full = fronts * rows
+        self.width = self.full + 128
+        self.share, self.offset, self.base, self.blocks = {}, {}, {}, {}
+        base = 0
+        for level in range(1, self.depth + 2):
+            self.blocks[level] = 2 ** min(level, self.depth)
+            self.share[level] = rows // self.blocks[level]
+            self.offset[level] = rows - (rows >> level - 1)
+            self.base[level] = base
+            base += fronts * self.share[level]
+
+    def label(self, level, group):
+        if level > self.depth:
+            return jnp.int32(0)
+        return (group // 2**level) * 2**level + 2 ** (level - 1)
+
+    def child_ids(self, level, group, pattern):
+        if level == 1:
+            kind, labels = 0, (group, group ^ 1)
+        elif level > self.depth:
+            kind, labels = 1, (self.label(level - 1, group),)
+        else:
+            kind = 1
+            labels = tuple(self.label(level - 1, far) for far in (group, group ^ 2 ** (level - 1)))
+        return jnp.concatenate([pattern[kind, pl.ds(label, 1), :] for label in labels], axis=1)
+
+
+def one_hot(ids, count, start=0):
+    rows = lax.broadcasted_iota(jnp.int32, (count, ids.shape[1]), 0) + start
+    return (rows == ids).astype(jnp.float32)
+
+
+def own_columns(plan, front, value):
+    rows = plan.rows
+    result = value[:, :rows]
+    for slot in range(1, plan.fronts):
+        result = jnp.where(front == slot, value[:, slot * rows : (slot + 1) * rows], result)
+    return result
+
+
+def place():
+    return lax.axis_index("front"), lax.axis_index("leaf")
+
+
+def pack_kernel(plan, pattern, lr, sr, li, si, lu, su, outer, out):
+    full, rhs, upd, rows = plan.full, plan.rhs, plan.upd, plan.rows
+    front, _ = place()
+    flat = jnp.concatenate([sr[0], su[0], jnp.zeros((upd, rows), jnp.float32), lr[0]], axis=0).T
+    out[:rows, :full] = si[0]
+    out[:rows, full:] = flat[:, :128]
+    out[:rows, full + rhs + upd :] = nn(outer[...], one_hot(pattern[1, 0:1, :], rows, front * rows))
+    out[rows:, :full] = nn(lu[0], li[0])
+    out[rows:, full : full + rhs] = flat[: rows // 2, 128:]
+    out[rows:, full + rhs :] = flat[rows // 2 :, 128:]
+
+
+def spread_kernel(plan, *refs):
+    count = plan.fronts
+    packs = refs[:count]
+    sep_all, x_part, y_part, picked, update, leaf_r, fold, turned = refs[count:]
+    full, rhs, rows = plan.full, plan.rhs, plan.rows
+    front, _ = place()
+    for slot in range(count):
+        at = pl.multiple_of((front ^ slot) * rows, rows)
+        turned[pl.ds(at, rows // 2), :] = packs[slot][rows:, full : full + rhs]
+        turned[pl.ds(at + rows // 2, rows // 2), :] = packs[slot][rows:, full + rhs :]
+    folded = packs[0][rows:, :full]
+    total = packs[0][:rows, full + rhs + plan.upd :]
+    for slot in range(1, count):
+        folded = folded + packs[slot][rows:, :full]
+        total = total + packs[slot][:rows, full + rhs + plan.upd :]
+    right = turned[...].T
+    first = nt(right, folded)
+    for slot in range(count):
+        for level in range(1, plan.depth + 2):
+            share, offset = plan.share[level], plan.offset[level]
+            piece = packs[slot][offset : offset + share, :]
+            dest = pl.multiple_of(plan.base[level] + (front ^ slot) * share, share)
+            sep_all[pl.ds(dest, share), :] = piece
+            if level >= 2:
+                x_part[pl.ds(pl.multiple_of(dest - plan.base[2], share), share), :] = piece
+            if level >= 3:
+                y_part[pl.ds(pl.multiple_of(dest - plan.base[3], share), share), :] = piece
+    sep_all[:rhs, full + rhs + plan.upd :] = first
+    update[...] = first
+    picked[...] = total
+    leaf_r[...] = right
+    fold[...] = own_columns(plan, front, folded)
+
+
+def leaf_back_kernel(plan, leaf_r, matrix, keep, send):
+    front, _ = place()
+    term = nn(nt(leaf_r[...], matrix[0]), matrix[0])
+    low, high = term[:, : plan.full // 2], term[:, plan.full // 2 :]
+    upper = front // 2 == 1
+    keep[...] = jnp.where(upper, high, low)
+    send[...] = jnp.where(upper, low, high)
+
+
+def leaf_part_kernel(plan, kept, got, keep, send):
+    front, _ = place()
+    term = kept[...] + got[...]
+    low, high = term[:, : plan.rows], term[:, plan.rows :]
+    upper = front % 2 == 1
+    keep[...] = jnp.where(upper, high, low)
+    send[...] = jnp.where(upper, low, high)
+
+
+def level_kernel(plan, level, pattern, *refs):
+    blocks, share = plan.blocks[level], plan.share[level]
+    parts, (whole, cross, start) = refs[:blocks], refs[blocks:]
+    _, group = place()
+    bases = [1, 1, 2, 2, 3, 3, 3, 3]
+    for slot in range(blocks):
+        first = plan.base[level] - plan.base[bases[slot]]
+        inner = (group & (blocks - 1)) ^ slot
+        for front in range(plan.fronts):
+            dest = pl.multiple_of(front * plan.rows + inner * share, share)
+            whole[pl.ds(dest, share), :] = parts[slot][first + front * share : first + (front + 1) * share, :]
+    flipped = whole[:, plan.full :].T
+    folded = nn(flipped[plan.rhs : plan.rhs + plan.upd], whole[:, : plan.full])
+    cross[...] = nn(folded, one_hot(plan.child_ids(level, group, pattern), plan.full))
+    start[...] = nt(flipped[: plan.rhs], folded)
+
+
+def back_kernel(plan, level, pattern, whole, picks, columns):
+    front, group = place()
+    ids = plan.child_ids(level, group, pattern)
+    hot = one_hot(ids, plan.full)
+    matrix = whole[:, : plan.full]
+    flipped = whole[:, plan.full :].T
+    ahead = nt(jnp.concatenate([flipped[: plan.rhs], hot.T], axis=0), matrix)
+    both = nn(jnp.concatenate([ahead, flipped[plan.rhs : plan.rhs + plan.upd]], axis=0), matrix)
+    picks[...] = nn(both, hot[:, : plan.upd])
+    columns[...] = own_columns(plan, front, both)
+
+
+def update_kernel(plan, start, cross, mine, other, out):
+    upd = plan.upd
+    out[...] = start[...] - nt(mine[...], cross[:, :upd]) - nt(other[...], cross[:, upd:])
+
+
+def finish_kernel(plan, *refs):
+    start3, cross3, top_s, fold, leaf_kept, leaf_got = refs[:6]
+    updates = [(refs[6 + 2 * pos][...], refs[7 + 2 * pos][...]) for pos in range(3)]
+    picks = [ref for ref in refs[12:16]]
+    columns = [ref for ref in refs[16:20]]
+    out = refs[20]
+    rhs, upd = plan.rhs, plan.upd
+    _, group = place()
+    u3 = start3[...] - nt(updates[2][0], cross3[:, :upd]) - nt(updates[2][1], cross3[:, upd:])
+    s_level = {4: top_s[...]}
+    weights = {4: jnp.concatenate([u3, s_level[4]], axis=1)}
+    s_level[3] = picks[3][:rhs] - nn(weights[4], picks[3][rhs:])
+    for level in (3, 2, 1):
+        weights[level] = jnp.concatenate([*updates[level - 1], s_level[level]], axis=1)
+        s_level[level - 1] = picks[level - 1][:rhs] - nn(weights[level], picks[level - 1][rhs:])
+    out[0, 0] = leaf_kept[...] + leaf_got[...] - nn(s_level[0], fold[...])
+    empty = jnp.zeros((upd, plan.rows), jnp.float32)
+    chosen = jnp.concatenate([columns[3][: rhs + upd], empty, columns[3][rhs + upd :]], axis=0)
+    weight = jnp.concatenate([u3, jnp.zeros((rhs, upd), jnp.float32), s_level[4]], axis=1)
+    for level in (3, 2, 1):
+        here = plan.label(level, group) == group
+        chosen = jnp.where(here, columns[level - 1][...], chosen)
+        weight = jnp.where(here, weights[level], weight)
+    out[1, 0] = chosen[:rhs] - nn(weight, chosen[rhs:])
 
 
 def partner(block, axis, distance):
@@ -30,7 +256,7 @@
     )
 
 
-def body(
+def general(
     leaf_rhs, sep_rhs, leaf_inverse, sep_inverse, leaf_block, sep_block, pattern, outer_solution
 ):
     group_count = lax.axis_size("leaf")
@@ -106,6 +332,99 @@
     return jnp.stack([leaf_x, sep_x])[:, None]
 
 
+def chain(
+    plan, leaf_rhs, sep_rhs, leaf_inverse, sep_inverse, leaf_block, sep_block, pattern, outer
+):
+    full, rows, rhs, upd, width = plan.full, plan.rows, plan.rhs, plan.upd, plan.width
+
+    def kernel(body, outs, *args, extra=(), **kw):
+        return call(functools.partial(body, plan, *extra), outs, args, **kw)
+
+    (pack,) = kernel(
+        pack_kernel,
+        [(rows + upd, width)],
+        pattern, leaf_rhs, sep_rhs, leaf_inverse, sep_inverse, leaf_block, sep_block, outer,
+        chip=False,
+    )
+    across = exchange(pack, "front", 3)
+    beside = exchange(pack, "front", 1)
+    beyond = exchange(across, "front", 1)
+    sep_all, x_part, y_part, top_s, u0, leaf_r, fold = kernel(
+        spread_kernel,
+        [
+            (full, width),
+            (full - plan.base[2], width),
+            (full - plan.base[3], width),
+            (rhs, upd),
+            (rhs, upd),
+            (rhs, full),
+            (upd, rows),
+        ],
+        pack, beside, beyond, across,
+        scratch=[pltpu.VMEM((full, rhs), jnp.float32)],
+    )
+    sep_core = exchange(sep_all, "leaf", 1)
+    by_x = exchange(x_part, "leaf", 2)
+    by_y = exchange(y_part, "leaf", 4)
+    by_xy = exchange(y_part, "leaf", 6)
+    u0_far = sep_core[:rhs, full + rhs + upd :]
+
+    def level_of(level, *parts):
+        kids = 2 if level <= plan.depth else 1
+        return kernel(
+            level_kernel,
+            [(full, width), (upd, kids * upd), (rhs, upd)],
+            pattern, *parts,
+            extra=(level,),
+        )
+
+    def back_of(level, whole):
+        kids = 2 if level <= plan.depth else 1
+        tall = rhs + (kids + 1) * upd
+        return kernel(back_kernel, [(tall, upd), (tall, rows)], pattern, whole, extra=(level,))
+
+    whole1, cross1, start1 = level_of(1, sep_all, sep_core)
+    (u1,) = kernel(update_kernel, [(rhs, upd)], start1, cross1, u0, u0_far)
+    u1_far = exchange(u1, "leaf", 2)
+    leaf_r, _ = lax.optimization_barrier((leaf_r, u1))
+    leaf_half, leaf_send = kernel(leaf_back_kernel, [(rhs, full // 2)] * 2, leaf_r, leaf_inverse)
+    leaf_sent = exchange(leaf_send, "front", 2)
+    picks1, columns1 = back_of(1, whole1)
+    by_x, by_y, by_xy, u1_far, leaf_sent, picks1 = lax.optimization_barrier(
+        (by_x, by_y, by_xy, u1_far, leaf_sent, picks1)
+    )
+    by_x_core = exchange(by_x, "leaf", 1)
+    by_y_core, by_xy_core = exchange(by_y, "leaf", 1), exchange(by_xy, "leaf", 1)
+    whole2, cross2, start2 = level_of(2, sep_all, sep_core, by_x, by_x_core)
+    (u2,) = kernel(update_kernel, [(rhs, upd)], start2, cross2, u1, u1_far)
+    u2_far = exchange(u2, "leaf", 4)
+    leaf_sent, whole2, by_y, _ = lax.optimization_barrier((leaf_sent, whole2, by_y, u2))
+    leaf_kept, leaf_send = kernel(leaf_part_kernel, [(rhs, rows)] * 2, leaf_half, leaf_sent)
+    leaf_got = exchange(leaf_send, "front", 1)
+    parts = (sep_all, sep_core, by_x, by_x_core, by_y, by_y_core, by_xy, by_xy_core)
+    picks2, columns2 = back_of(2, whole2)
+    whole3, cross3, start3 = level_of(3, *parts)
+    picks3, columns3 = back_of(3, whole3)
+    whole4, _, _ = level_of(4, *parts)
+    picks4, columns4 = back_of(4, whole4)
+    (out,) = kernel(
+        finish_kernel,
+        [(2, 1, rhs, rows)],
+        start3, cross3, top_s, fold, leaf_kept, leaf_got, u0, u0_far, u1, u1_far, u2, u2_far,
+        picks1, picks2, picks3, picks4, columns1, columns2, columns3, columns4,
+    )
+    return out
+
+
+def body(*args):
+    groups, fronts = lax.axis_size("leaf"), lax.axis_size("front")
+    rhs, rows, upd = args[0].shape[1], args[0].shape[2], args[4].shape[1]
+    plan = Plan(groups, fronts, rhs, upd, rows)
+    if (groups, fronts) == (8, 4) and rows == 64 and rhs == 64 and upd == 32:
+        return chain(plan, *args)
+    return general(*args)
+
+
 def solution(mesh):
     placed = (
         P("leaf", None, "front"),

time: 696 us -> 40.6 us (0.06)
  waiting for transfers between devices: 565 us -> 10.7 us
  blocking collectives: 83.1 us -> 0 us
  local copies, waits for them, and re-layouts: 16.8 us -> 0.73 us
  starting transfers between devices: 3.61 us -> 18.3 us
  between operations: 13.6 us -> 0.08 us
  matrix products: 12.1 us -> 0 us
  Pallas kernels: 0 us -> 10.5 us
    psum x4 -> x0, waiting for transfers between devices: 464 us -> none  [block_sum(): return lax.psum(term, ('leaf', 'front'))]
    unnamed x14 -> x0, waiting for transfers between devices: 92.4 us -> none
    all_gather x6 -> x0, blocking collectives: 83.1 us -> none  [the longest x4 53.7 us: block_sum(): return lax.all_gather(piece, 'front', axis=1, tiled=True)]
    ppermute x6 -> x14, starting transfers between devices: 3.27 us -> 18.3 us  [exchange(): lax.ppermute(block, axis, [(src, src ^ mask) for src in range(count)])]
    pallas_call x0 -> x15, Pallas kernels: none -> 10.5 us  [call(): pl.pallas_call(kernel, out_shape=[pltpu.VMEM(shape, jnp.float32) if len(s...]
    unnamed x31 -> x4, local copies, waits for them, and re-layouts: 9.82 us -> 0.65 us
    dot_general x20 -> x0, matrix products: 8.97 us -> none  [the longest x11 5.28 us: times_rows(): jnp.dot(vectors, matrix, precision=lax.Precision.HIGHEST, preferred_eleme...]
  transfers between devices with their start and end apart: 15 -> 14, of which waited for: 15 -> 5; matrix products, arithmetic and copies ran while one was open for 0% -> 0% of each run, Pallas kernels for 0% -> 18%
where the time goes in v2:
time: 40.6 us; the launch traced here: 40.4 us
  starting transfers between devices  18.3 us (45%)
  waiting for transfers between devices  10.7 us (26%)
  Pallas kernels  10.5 us (26%)
  local copies, waits for them, and re-layouts  0.73 us (2%)
    ppermute x14, starting transfers between devices, exchange(): lax.ppermute(block, axis, [(src, src ^ mask) for src in range(count)])  18.3 us
    ppermute x14, waiting for transfers between devices, exchange(): lax.ppermute(block, axis, [(src, src ^ mask) for src in range(count)])  10.7 us
    pallas_call x15, Pallas kernels, call(): pl.pallas_call(kernel, out_shape=[pltpu.VMEM(shape, jnp.float32) if len(s...  10.5 us
  transfers between devices with their start and end apart: 14, of which 5 were waited for; matrix products, arithmetic and copies ran while one was open for 0% of the time, Pallas kernels for 18%

profile of v2, /device:TPU:0, one launch (start us, length us, event | category | flops | bytes accessed | tf_op | source)
XLA Modules:
  0.0 40.4 jit_solution(16321616046514212073)
XLA Ops:
  0.0 1.2 %shard_map.82.refs_0_ = f32[96,384]{1,0:T(8,128)S(1)} custom-call(s32[2,8,32]{2,1,0:T(8,128)} %pattern.17, f32[1,64,64]{2,1,0:T(8,128)} %lr.1, f32[1,64,64]{2,1,0:T(8,128)} %sr.1, f32[1,64,256]{2,1,0:T(8,128)} %matrix.1, f32[1,64,256]{2,1,0:T(8,128)} %si.1, f32[1,32,64]{2,1,0:T(8,128)} %lu.1, f32[1,32,64]{2,1,0:T(8,128)} %su.1, f32[64,64]{1,0:T(8,128)} %outer.1), custom_call_target="tpu_custom_call" | custom-call | flops 1000 | bytes 1000 | tf_op jit(solution)/shard_map/pallas_call | solution.py:45
  1.2 5.1 %collective-permute-start.1 = (f32[96,384]{1,0:T(8,128)S(1)}, f32[96,384]{1,0:T(8,128)S(1)}, u32[]{:S(2)}, u32[]{:S(2)}) collective-permute-start(f32[96,384]{1,0:T(8,128)S(1)} %shard_map.82.refs_0_), channel_id=1, source_target_pairs={{0,3},{1,2},{2,1},{3,0},{4,7},{5,6},{6,5},{7,4},{8,11},{9,10},{10,... | collective-permute-start | bytes 442376 | tf_op jit(solution)/shard_map/ppermute | solution.py:34
  6.3 0.0 collective-permute-start
  6.3 4.7 %collective-permute-done.1.refs_3_ = f32[96,384]{1,0:T(8,128)S(1)} collective-permute-done((f32[96,384]{1,0:T(8,128)S(1)}, f32[96,384]{1,0:T(8,128)S(1)}, u32[]{:S(2)}, u32[]{:S(2)}) %collective-permute-start.1) | collective-permute-done | bytes 147488 | tf_op jit(solution)/shard_map/ppermute | solution.py:34
  11.0 2.0 %collective-permute-start.2 = (f32[96,384]{1,0:T(8,128)S(1)}, f32[96,384]{1,0:T(8,128)S(1)}, u32[]{:S(2)}, u32[]{:S(2)}) collective-permute-start(f32[96,384]{1,0:T(8,128)S(1)} %collective-permute-done.1.refs_3_), channel_id=1, source_target_pairs={{0,1},{1,0},{2,3},{3,2},{4,5},{5,4},{6,7},{7,6},{8,9},{9,8},{10,11... | collective-permute-start | bytes 442376 | tf_op jit(solution)/shard_map/ppermute | solution.py:34
  13.0 0.6 %collective-permute-done.refs_1_ = f32[96,384]{1,0:T(8,128)S(1)} collective-permute-done((f32[96,384]{1,0:T(8,128)S(1)}, f32[96,384]{1,0:T(8,128)S(1)}, u32[]{:S(2)}, u32[]{:S(2)}) %collective-permute-start) | collective-permute-done | bytes 147488 | tf_op jit(solution)/shard_map/ppermute | solution.py:34
  13.6 3.0 %collective-permute-done.2.refs_2_ = f32[96,384]{1,0:T(8,128)S(1)} collective-permute-done((f32[96,384]{1,0:T(8,128)S(1)}, f32[96,384]{1,0:T(8,128)S(1)}, u32[]{:S(2)}, u32[]{:S(2)}) %collective-permute-start.2) | collective-permute-done | bytes 147488 | tf_op jit(solution)/shard_map/ppermute | solution.py:34
  16.6 0.0 copy-start
  16.6 0.4 %shard_map.83 = (f32[256,384]{1,0:T(8,128)S(1)}, f32[128,384]{1,0:T(8,128)S(1)}, f32[64,384]{1,0:T(8,128)S(1)}, f32[64,32]{1,0:T(8,128)S(1)}, f32[64,32]{1,0:T(8...) custom-call(f32[96,384]{1,0:T(8,128)S(1)} %shard_map.82.refs_0_, f32[96,384]{1,0:T(8,128)S(1)} %collective-permute-done.refs_1_, ...), custom_call_target="tpu_custom_call" | custom-call | flops 1000 | bytes 1000 | tf_op jit(solution)/shard_map/pallas_call | solution.py:45
  17.0 0.1 collective-permute-start.3
  17.1 1.6 %collective-permute-start.4 = (f32[128,384]{1,0:T(8,128)S(1)}, f32[128,384]{1,0:T(8,128)S(1)}, u32[]{:S(2)}, u32[]{:S(2)}) collective-permute-start(f32[128,384]{1,0:T(8,128)S(1)} %get-tuple-element.45), channel_id=1, source_target_pairs={{0,8},{4,12},{8,0},{12,4},{16,24},{20,28},{24,16},{28,20},{1,9},{5... | collective-permute-start | bytes 589832 | tf_op jit(solution)/shard_map/ppermute | solution.py:34
  18.6 1.5 %collective-permute-start.5 = (f32[64,384]{1,0:T(8,128)S(1)}, f32[64,384]{1,0:T(8,128)S(1)}, u32[]{:S(2)}, u32[]{:S(2)}) collective-permute-start(f32[64,384]{1,0:T(8,128)S(1)} %get-tuple-element.46), channel_id=1, source_target_pairs={{0,16},{4,20},{8,24},{12,28},{16,0},{20,4},{24,8},{28,12},{1,17},{... | collective-permute-start | bytes 294920 | tf_op jit(solution)/shard_map/ppermute | solution.py:34
  20.1 0.5 %collective-permute-start.6 = (f32[64,384]{1,0:T(8,128)S(1)}, f32[64,384]{1,0:T(8,128)S(1)}, u32[]{:S(2)}, u32[]{:S(2)}) collective-permute-start(f32[64,384]{1,0:T(8,128)S(1)} %get-tuple-element.46), channel_id=1, source_target_pairs={{0,24},{4,28},{8,16},{12,20},{16,8},{20,12},{24,0},{28,4},{1,25},{... | collective-permute-start | bytes 294920 | tf_op jit(solution)/shard_map/ppermute | solution.py:34
  20.6 0.0 collective-permute-done.3.refs_1_
  20.6 0.0 copy-done
  20.6 0.5 %shard_map.84 = (f32[256,384]{1,0:T(8,128)S(1)}, f32[32,64]{1,0:T(8,128)S(1)}, f32[64,32]{1,0:T(8,128)S(1)}) custom-call(s32[2,8,32]{2,1,0:T(8,128)S(1)} %copy-done, f32[256,384]{1,0:T(8,128)S(1)} %get-tuple-element.44.refs_0_, f32[256,384]{1,0:T(8,128)S(1)} %collective-permute-done.3.refs_1_), custom_call_target="tpu_custom_call" | custom-call | flops 1000 | bytes 1000 | tf_op jit(solution)/shard_map/pallas_call | solution.py:45
  21.1 0.1 slice.4.other.refs_7_
  21.2 0.0 copy-start.1
  21.2 0.2 shard_map.85.mine.refs_8_
  21.4 0.6 %copy-done.1 = f32[1,64,256]{2,1,0:T(8,128)S(1)} copy-done((f32[1,64,256]{2,1,0:T(8,128)S(1)}, f32[1,64,256]{2,1,0:T(8,128)}, u32[]{:S(2)}) %copy-start.1) | copy-done | bytes 65560
  22.1 0.3 shard_map.86
  22.4 2.7 %collective-permute-start.8 = (f32[64,128]{1,0:T(8,128)S(1)}, f32[64,128]{1,0:T(8,128)S(1)}, u32[]{:S(2)}, u32[]{:S(2)}) collective-permute-start(f32[64,128]{1,0:T(8,128)S(1)} %get-tuple-element.52), channel_id=1, source_target_pairs={{0,2},{1,3},{2,0},{3,1},{4,6},{5,7},{6,4},{7,5},{8,10},{9,11},{10,... | collective-permute-start | bytes 98312 | tf_op jit(solution)/shard_map/ppermute | solution.py:34
  25.1 1.5 %collective-permute-start.7 = (f32[64,32]{1,0:T(8,128)S(1)}, f32[64,32]{1,0:T(8,128)S(1)}, u32[]{:S(2)}, u32[]{:S(2)}) collective-permute-start(f32[64,32]{1,0:T(8,128)S(1)} %shard_map.85.mine.refs_8_), channel_id=1, source_target_pairs={{0,8},{4,12},{8,0},{12,4},{16,24},{20,28},{24,16},{28,20},{1,9},{5... | collective-permute-start | bytes 24584 | tf_op jit(solution)/shard_map/ppermute | solution.py:34
  26.6 0.9 %shard_map.87 = (f32[160,32]{1,0:T(8,128)S(1)}, f32[160,64]{1,0:T(8,128)S(1)}) custom-call(s32[2,8,32]{2,1,0:T(8,128)S(1)} %copy-done, f32[256,384]{1,0:T(8,128)S(1)} %get-tuple-element.53.whole), custom_call_target="tpu_custom_call" | custom-call | flops 1000 | bytes 1000 | tf_op jit(solution)/shard_map/pallas_call | solution.py:45
  27.5 0.0 collective-permute-done.5.refs_4_
  27.5 0.0 collective-permute-done.6.refs_6_
  27.5 0.0 collective-permute-done.4.refs_2_
  27.5 1.5 %collective-permute-done.7.other.refs_9_ = f32[64,32]{1,0:T(8,128)S(1)} collective-permute-done((f32[64,32]{1,0:T(8,128)S(1)}, f32[64,32]{1,0:T(8,128)S(1)}, u32[]{:S(2)}, u32[]{:S(2)}) %collective-permute-start.7) | collective-permute-done | bytes 8224 | tf_op jit(solution)/shard_map/ppermute | solution.py:34
  29.0 0.0 collective-permute-done.8.got
  29.0 0.0 collective-permute-start.9
  29.0 0.5 %collective-permute-start.10 = (f32[64,384]{1,0:T(8,128)S(1)}, f32[64,384]{1,0:T(8,128)S(1)}, u32[]{:S(2)}, u32[]{:S(2)}) collective-permute-start(f32[64,384]{1,0:T(8,128)S(1)} %collective-permute-done.5.refs_4_), channel_id=1, source_target_pairs={{0,4},{4,0},{8,12},{12,8},{16,20},{20,16},{24,28},{28,24},{1,5},{5... | collective-permute-start | bytes 294920 | tf_op jit(solution)/shard_map/ppermute | solution.py:34
  29.5 0.0 collective-permute-start.11
  29.5 0.9 %collective-permute-done.9.refs_3_ = f32[128,384]{1,0:T(8,128)S(1)} collective-permute-done((f32[128,384]{1,0:T(8,128)S(1)}, f32[128,384]{1,0:T(8,128)S(1)}, u32[]{:S(2)}, u32[]{:S(2)}) %collective-permute-start.9) | collective-permute-done | bytes 196640 | tf_op jit(solution)/shard_map/ppermute | solution.py:34
  30.5 0.5 %shard_map.88 = (f32[256,384]{1,0:T(8,128)S(1)}, f32[32,64]{1,0:T(8,128)S(1)}, f32[64,32]{1,0:T(8,128)S(1)}) custom-call(s32[2,8,32]{2,1,0:T(8,128)S(1)} %copy-done, f32[256,384]{1,0:T(8,128)S(1)} %get-tuple-element.44.refs_0_, f32[256,384]{1,0:T(8,128)S(1)} %collective-permute-done.3.refs_1_, f32[128,384]{1,0:T(8,128)S(1)} %collective-permute-done.4.refs_2_, ...), custom_call_target="tpu_custom_call" | custom-call | flops 1000 | bytes 1000 | tf_op jit(solution)/shard_map/pallas_call | solution.py:45
  31.0 0.2 shard_map.89.refs_10_
  31.2 0.2 shard_map.91
  31.3 1.4 %collective-permute-start.12 = (f32[64,64]{1,0:T(8,128)S(1)}, f32[64,64]{1,0:T(8,128)S(1)}, u32[]{:S(2)}, u32[]{:S(2)}) collective-permute-start(f32[64,64]{1,0:T(8,128)S(1)} %get-tuple-element.71), channel_id=1, source_target_pairs={{0,1},{1,0},{2,3},{3,2},{4,5},{5,4},{6,7},{7,6},{8,9},{9,8},{10,11... | collective-permute-start | bytes 49160 | tf_op jit(solution)/shard_map/ppermute | solution.py:34
  32.7 1.5 %collective-permute-start.13 = (f32[64,32]{1,0:T(8,128)S(1)}, f32[64,32]{1,0:T(8,128)S(1)}, u32[]{:S(2)}, u32[]{:S(2)}) collective-permute-start(f32[64,32]{1,0:T(8,128)S(1)} %shard_map.89.refs_10_), channel_id=1, source_target_pairs={{0,16},{4,20},{8,24},{12,28},{16,0},{20,4},{24,8},{28,12},{1,17},{... | collective-permute-start | bytes 24584 | tf_op jit(solution)/shard_map/ppermute | solution.py:34
  34.2 0.0 collective-permute-done.10.refs_5_
  34.2 0.0 collective-permute-done.11.refs_7_
  34.3 1.1 %shard_map.94 = (f32[256,384]{1,0:T(8,128)S(1)}, f32[32,32]{1,0:T(8,128)}, f32[64,32]{1,0:T(8,128)}) custom-call(s32[2,8,32]{2,1,0:T(8,128)S(1)} %copy-done, f32[256,384]{1,0:T(8,128)S(1)} %get-tuple-element.44.refs_0_, f32[256,384]{1,0:T(8,128)S(1)} %collective-permute-done.3.refs_1_, f32[128,384]{1,0:T(8,128)S(1)} %collective-permute-done.4.refs_2_, ...), custom_call_target="tpu_custom_call" | custom-call | flops 1000 | bytes 1000 | tf_op jit(solution)/shard_map/pallas_call | solution.py:45
  35.4 0.8 %shard_map.95 = (f32[128,32]{1,0:T(8,128)S(1)}, f32[128,64]{1,0:T(8,128)S(1)}) custom-call(s32[2,8,32]{2,1,0:T(8,128)S(1)} %copy-done, f32[256,384]{1,0:T(8,128)S(1)} %get-tuple-element.77.whole), custom_call_target="tpu_custom_call" | custom-call | flops 1000 | bytes 1000 | tf_op jit(solution)/shard_map/pallas_call | solution.py:45
  36.2 0.5 %shard_map.90 = (f32[256,384]{1,0:T(8,128)S(1)}, f32[32,64]{1,0:T(8,128)S(1)}, f32[64,32]{1,0:T(8,128)S(1)}) custom-call(s32[2,8,32]{2,1,0:T(8,128)S(1)} %copy-done, f32[256,384]{1,0:T(8,128)S(1)} %get-tuple-element.44.refs_0_, f32[256,384]{1,0:T(8,128)S(1)} %collective-permute-done.3.refs_1_, f32[128,384]{1,0:T(8,128)S(1)} %collective-permute-done.4.refs_2_, ...), custom_call_target="tpu_custom_call" | custom-call | flops 1000 | bytes 1000 | tf_op jit(solution)/shard_map/pallas_call | solution.py:45
  36.7 0.9 %shard_map.93 = (f32[160,32]{1,0:T(8,128)S(1)}, f32[160,64]{1,0:T(8,128)S(1)}) custom-call(s32[2,8,32]{2,1,0:T(8,128)S(1)} %copy-done, f32[256,384]{1,0:T(8,128)S(1)} %get-tuple-element.75.whole), custom_call_target="tpu_custom_call" | custom-call | flops 1000 | bytes 1000 | tf_op jit(solution)/shard_map/pallas_call | solution.py:45
  37.7 0.9 %shard_map.92 = (f32[160,32]{1,0:T(8,128)S(1)}, f32[160,64]{1,0:T(8,128)S(1)}) custom-call(s32[2,8,32]{2,1,0:T(8,128)S(1)} %copy-done, f32[256,384]{1,0:T(8,128)S(1)} %get-tuple-element.73.whole), custom_call_target="tpu_custom_call" | custom-call | flops 1000 | bytes 1000 | tf_op jit(solution)/shard_map/pallas_call | solution.py:45
  38.6 0.0 collective-permute-done.13.refs_11_
  38.6 0.0 collective-permute-done.12.refs_5_
  38.6 1.8 %shard_map.96 = f32[2,1,64,64]{3,2,1,0:T(8,128)} custom-call(f32[64,32]{1,0:T(8,128)S(1)} %get-tuple-element.64.refs_0_, f32[32,64]{1,0:T(8,128)S(1)} %get-tuple-element.65.refs_1_, f32[64,32]{1,0:T(8,128)S(1)} %get-tuple-element.66.refs_2_, f32[32,64]{1,0:T(8,128)S(1)} %get-tuple-element.67.refs_3_, f32[64,64]{1,0:T(8,128)S(1)} %get-tuple-element.70.refs_4_, ...), custom_call_target="tpu_custom_call" | custom-call | flops 1000 | bytes 1000 | tf_op jit(solution)/shard_map/pallas_call | solution.py:45
Async XLA Ops:
  1.2 9.8 %collective-permute-start.1 = (f32[96,384]{1,0:T(8,128)S(1)}, f32[96,384]{1,0:T(8,128)S(1)}, u32[]{:S(2)}, u32[]{:S(2)}) collective-permute-start(f32[96,384]{1,0:T(8,128)S(1)} %shard_map.82.refs_0_), channel_id=1, source_target_pairs={{0,3},{1,2},{2,1},{3,0},{4,7},{5,6},{6,5},{7,4},{8,11},{9,10},{10,... | collective-permute-start | bytes 442376 | tf_op jit(solution)/shard_map/ppermute | solution.py:34
  6.3 7.3 %collective-permute-start = (f32[96,384]{1,0:T(8,128)S(1)}, f32[96,384]{1,0:T(8,128)S(1)}, u32[]{:S(2)}, u32[]{:S(2)}) collective-permute-start(f32[96,384]{1,0:T(8,128)S(1)} %shard_map.82.refs_0_), channel_id=1, source_target_pairs={{0,1},{1,0},{2,3},{3,2},{4,5},{5,4},{6,7},{7,6},{8,9},{9,8},{10,11... | collective-permute-start | bytes 442376 | tf_op jit(solution)/shard_map/ppermute | solution.py:34
  11.0 5.5 %collective-permute-start.2 = (f32[96,384]{1,0:T(8,128)S(1)}, f32[96,384]{1,0:T(8,128)S(1)}, u32[]{:S(2)}, u32[]{:S(2)}) collective-permute-start(f32[96,384]{1,0:T(8,128)S(1)} %collective-permute-done.1.refs_3_), channel_id=1, source_target_pairs={{0,1},{1,0},{2,3},{3,2},{4,5},{5,4},{6,7},{7,6},{8,9},{9,8},{10,11... | collective-permute-start | bytes 442376 | tf_op jit(solution)/shard_map/ppermute | solution.py:34
  16.6 4.1 %copy-start = (s32[2,8,32]{2,1,0:T(8,128)S(1)}, s32[2,8,32]{2,1,0:T(8,128)}, u32[]{:S(2)}) copy-start(s32[2,8,32]{2,1,0:T(8,128)} %pattern.17) | copy-start | bytes 6148
  17.0 3.6 %collective-permute-start.3 = (f32[256,384]{1,0:T(8,128)S(1)}, f32[256,384]{1,0:T(8,128)S(1)}, u32[]{:S(2)}, u32[]{:S(2)}) collective-permute-start(f32[256,384]{1,0:T(8,128)S(1)} %get-tuple-element.44.refs_0_), channel_id=1, source_target_pairs={{0,4},{4,0},{8,12},{12,8},{16,20},{20,16},{24,28},{28,24},{1,5},{5... | collective-permute-start | bytes 1179656 | tf_op jit(solution)/shard_map/ppermute | solution.py:34
  17.1 10.4 %collective-permute-start.4 = (f32[128,384]{1,0:T(8,128)S(1)}, f32[128,384]{1,0:T(8,128)S(1)}, u32[]{:S(2)}, u32[]{:S(2)}) collective-permute-start(f32[128,384]{1,0:T(8,128)S(1)} %get-tuple-element.45), channel_id=1, source_target_pairs={{0,8},{4,12},{8,0},{12,4},{16,24},{20,28},{24,16},{28,20},{1,9},{5... | collective-permute-start | bytes 589832 | tf_op jit(solution)/shard_map/ppermute | solution.py:34
  18.6 8.9 %collective-permute-start.5 = (f32[64,384]{1,0:T(8,128)S(1)}, f32[64,384]{1,0:T(8,128)S(1)}, u32[]{:S(2)}, u32[]{:S(2)}) collective-permute-start(f32[64,384]{1,0:T(8,128)S(1)} %get-tuple-element.46), channel_id=1, source_target_pairs={{0,16},{4,20},{8,24},{12,28},{16,0},{20,4},{24,8},{28,12},{1,17},{... | collective-permute-start | bytes 294920 | tf_op jit(solution)/shard_map/ppermute | solution.py:34
  20.1 7.3 %collective-permute-start.6 = (f32[64,384]{1,0:T(8,128)S(1)}, f32[64,384]{1,0:T(8,128)S(1)}, u32[]{:S(2)}, u32[]{:S(2)}) collective-permute-start(f32[64,384]{1,0:T(8,128)S(1)} %get-tuple-element.46), channel_id=1, source_target_pairs={{0,24},{4,28},{8,16},{12,20},{16,8},{20,12},{24,0},{28,4},{1,25},{... | collective-permute-start | bytes 294920 | tf_op jit(solution)/shard_map/ppermute | solution.py:34
  21.2 0.9 %copy-start.1 = (f32[1,64,256]{2,1,0:T(8,128)S(1)}, f32[1,64,256]{2,1,0:T(8,128)}, u32[]{:S(2)}) copy-start(f32[1,64,256]{2,1,0:T(8,128)} %matrix.1) | copy-start | bytes 196612
  22.4 6.6 %collective-permute-start.8 = (f32[64,128]{1,0:T(8,128)S(1)}, f32[64,128]{1,0:T(8,128)S(1)}, u32[]{:S(2)}, u32[]{:S(2)}) collective-permute-start(f32[64,128]{1,0:T(8,128)S(1)} %get-tuple-element.52), channel_id=1, source_target_pairs={{0,2},{1,3},{2,0},{3,1},{4,6},{5,7},{6,4},{7,5},{8,10},{9,11},{10,... | collective-permute-start | bytes 98312 | tf_op jit(solution)/shard_map/ppermute | solution.py:34
  25.1 3.9 %collective-permute-start.7 = (f32[64,32]{1,0:T(8,128)S(1)}, f32[64,32]{1,0:T(8,128)S(1)}, u32[]{:S(2)}, u32[]{:S(2)}) collective-permute-start(f32[64,32]{1,0:T(8,128)S(1)} %shard_map.85.mine.refs_8_), channel_id=1, source_target_pairs={{0,8},{4,12},{8,0},{12,4},{16,24},{20,28},{24,16},{28,20},{1,9},{5... | collective-permute-start | bytes 24584 | tf_op jit(solution)/shard_map/ppermute | solution.py:34
  29.0 1.4 %collective-permute-start.9 = (f32[128,384]{1,0:T(8,128)S(1)}, f32[128,384]{1,0:T(8,128)S(1)}, u32[]{:S(2)}, u32[]{:S(2)}) collective-permute-start(f32[128,384]{1,0:T(8,128)S(1)} %collective-permute-done.4.refs_2_), channel_id=1, source_target_pairs={{0,4},{4,0},{8,12},{12,8},{16,20},{20,16},{24,28},{28,24},{1,5},{5... | collective-permute-start | bytes 589832 | tf_op jit(solution)/shard_map/ppermute | solution.py:34
  29.0 5.2 %collective-permute-start.10 = (f32[64,384]{1,0:T(8,128)S(1)}, f32[64,384]{1,0:T(8,128)S(1)}, u32[]{:S(2)}, u32[]{:S(2)}) collective-permute-start(f32[64,384]{1,0:T(8,128)S(1)} %collective-permute-done.5.refs_4_), channel_id=1, source_target_pairs={{0,4},{4,0},{8,12},{12,8},{16,20},{20,16},{24,28},{28,24},{1,5},{5... | collective-permute-start | bytes 294920 | tf_op jit(solution)/shard_map/ppermute | solution.py:34
  29.5 4.7 %collective-permute-start.11 = (f32[64,384]{1,0:T(8,128)S(1)}, f32[64,384]{1,0:T(8,128)S(1)}, u32[]{:S(2)}, u32[]{:S(2)}) collective-permute-start(f32[64,384]{1,0:T(8,128)S(1)} %collective-permute-done.6.refs_6_), channel_id=1, source_target_pairs={{0,4},{4,0},{8,12},{12,8},{16,20},{20,16},{24,28},{28,24},{1,5},{5... | collective-permute-start | bytes 294920 | tf_op jit(solution)/shard_map/ppermute | solution.py:34
  31.3 7.3 %collective-permute-start.12 = (f32[64,64]{1,0:T(8,128)S(1)}, f32[64,64]{1,0:T(8,128)S(1)}, u32[]{:S(2)}, u32[]{:S(2)}) collective-permute-start(f32[64,64]{1,0:T(8,128)S(1)} %get-tuple-element.71), channel_id=1, source_target_pairs={{0,1},{1,0},{2,3},{3,2},{4,5},{5,4},{6,7},{7,6},{8,9},{9,8},{10,11... | collective-permute-start | bytes 49160 | tf_op jit(solution)/shard_map/ppermute | solution.py:34
  32.7 5.9 %collective-permute-start.13 = (f32[64,32]{1,0:T(8,128)S(1)}, f32[64,32]{1,0:T(8,128)S(1)}, u32[]{:S(2)}, u32[]{:S(2)}) collective-permute-start(f32[64,32]{1,0:T(8,128)S(1)} %shard_map.89.refs_10_), channel_id=1, source_target_pairs={{0,16},{4,20},{8,24},{12,28},{16,0},{20,4},{24,8},{28,12},{1,17},{... | collective-permute-start | bytes 24584 | tf_op jit(solution)/shard_map/ppermute | solution.py:34

commit v3 on v0

--- a/solution.py
+++ b/solution.py
@@ -1,7 +1,276 @@
+import functools
 import jax
 import jax.numpy as jnp
 from jax import lax
+from jax.experimental import pallas as pl
+from jax.experimental.pallas import tpu as pltpu
 from jax.sharding import PartitionSpec as P
+
+def halves(value):
+    high = value.astype(jnp.bfloat16)
+    return high, (value - high.astype(jnp.float32)).astype(jnp.bfloat16)
+
+
+def product(left, right, side):
+    def term(one, two):
+        return lax.dot_general(
+            one, two, (((1,), (side,)), ((), ())), preferred_element_type=jnp.float32
+        )
+
+    (left_high, left_low), (right_high, right_low) = halves(left), halves(right)
+    return term(left_high, right_high) + (term(left_high, right_low) + term(left_low, right_high))
+
+
+def nn(left, right):
+    return product(left, right, 0)
+
+
+def nt(left, right):
+    return product(left, right, 1)
+
+
+def exchange(block, axis, mask):
+    count = lax.axis_size(axis)
+    return lax.ppermute(block, axis, [(src, src ^ mask) for src in range(count)])
+
+
+def call(kernel, outs, args, scratch=(), chip=True, cost=1000):
+    if chip:
+        args = [
+            pltpu.with_memory_space_constraint(arg, pltpu.VMEM)
+            if arg.ndim == 2
+            else arg
+            for arg in args
+        ]
+    return pl.pallas_call(
+        kernel,
+        out_shape=[
+            jax.ShapeDtypeStruct(out, jnp.float32)
+            if len(out) == 4
+            else pltpu.VMEM(*out)
+            if isinstance(out[0], tuple)
+            else pltpu.VMEM(out, jnp.float32)
+            for out in outs
+        ],
+        in_specs=[pl.BlockSpec(memory_space=pltpu.VMEM) for _ in args],
+        out_specs=[pl.BlockSpec(memory_space=pltpu.VMEM) for _ in outs],
+        scratch_shapes=list(scratch),
+        compiler_params=pltpu.CompilerParams(vmem_limit_bytes=8 << 20) if chip else None,
+        cost_estimate=pl.CostEstimate(flops=cost, bytes_accessed=cost, transcendentals=0),
+    )(*args)
+
+
+class Plan:
+    def __init__(self, groups, fronts, rhs, upd, rows):
+        self.groups, self.fronts, self.rhs, self.upd, self.rows = groups, fronts, rhs, upd, rows
+        self.depth = groups.bit_length() - 1
+        self.full = fronts * rows
+        self.width = self.full + 128
+        self.share, self.offset, self.base, self.blocks = {}, {}, {}, {}
+        base = 0
+        for level in range(1, self.depth + 2):
+            self.blocks[level] = 2 ** min(level, self.depth)
+            self.share[level] = rows // self.blocks[level]
+            self.offset[level] = rows - (rows >> level - 1)
+            self.base[level] = base
+            base += fronts * self.share[level]
+
+    def label(self, level, group):
+        if level > self.depth:
+            return jnp.int32(0)
+        return (group // 2**level) * 2**level + 2 ** (level - 1)
+
+    def child_ids(self, level, group, pattern):
+        if level == 1:
+            kind, labels = 0, (group, group ^ 1)
+        elif level > self.depth:
+            kind, labels = 1, (self.label(level - 1, group),)
+        else:
+            kind = 1
+            labels = tuple(self.label(level - 1, far) for far in (group, group ^ 2 ** (level - 1)))
+        return jnp.concatenate([pattern[pl.ds(kind * self.groups + label, 1), :] for label in labels], axis=1)
+
+
+def one_hot(ids, count, start=0):
+    rows = lax.broadcasted_iota(jnp.int32, (count, ids.shape[1]), 0) + start
+    return (rows == ids).astype(jnp.float32)
+
+
+def own_columns(plan, front, value):
+    rows = plan.rows
+    result = value[:, :rows]
+    for slot in range(1, plan.fronts):
+        result = jnp.where(front == slot, value[:, slot * rows : (slot + 1) * rows], result)
+    return result
+
+
+def place():
+    return lax.axis_index("front"), lax.axis_index("leaf")
+
+
+def pack_kernel(plan, pattern, lr, sr, li, si, lu, su, outer, out, ids):
+    full, rhs, upd, rows = plan.full, plan.rhs, plan.upd, plan.rows
+    front, _ = place()
+    ids[...] = pattern[...].reshape(ids.shape)
+    empty = jnp.zeros((upd, rows), jnp.float32)
+    out[:rows, :full] = si[0]
+    out[:rows, full:] = jnp.concatenate([sr[0], su[0], empty], axis=0).T
+    out[:rows, full + rhs + upd :] = nn(outer[...], one_hot(pattern[1, 0:1, :], rows, front * rows))
+    out[rows:, :full] = li[0]
+    out[rows:, full:] = jnp.concatenate([lr[0], lu[0], empty], axis=0).T
+
+
+def fold_rows(plan, rows_of):
+    step, full, edge = plan.rows, plan.full, plan.full + plan.rhs + plan.upd
+    pieces = [rows_of(front)[:, : (front + 1) * step] for front in (3, 2, 0, 1)]
+    pieces += [rows_of(front)[:, full:edge] for front in range(plan.fronts)]
+    return jnp.concatenate(pieces, axis=1)
+
+
+def unfold_rows(plan, folded):
+    step, full, edge = plan.rows, plan.full, plan.rhs + plan.upd
+    count = folded.shape[0]
+    starts = {3: 0, 2: full, 0: full + 3 * step, 1: 2 * full}
+    for front in range(plan.fronts):
+        wide = (front + 1) * step
+        side = 2 * full + 2 * step + front * edge
+        pieces = [folded[:, starts[front] : starts[front] + wide]]
+        if wide < full:
+            pieces.append(jnp.zeros((count, full - wide), jnp.float32))
+        pieces.append(folded[:, side : side + edge])
+        pieces.append(jnp.zeros((count, plan.width - full - edge), jnp.float32))
+        yield front, jnp.concatenate(pieces, axis=1)
+
+
+def spread_kernel(plan, *refs):
+    count = plan.fronts
+    packs = refs[:count]
+    all_part, late_part, high_part, picked, natural = refs[count:]
+    rows, edge = plan.rows, plan.full + plan.rhs + plan.upd
+    front, _ = place()
+    for slot in range(count):
+        at = pl.multiple_of((front ^ slot) * rows, rows)
+        natural[pl.ds(at, rows), :] = packs[slot][:rows, :]
+    total = packs[0][:rows, edge:]
+    for slot in range(1, count):
+        total = total + packs[slot][:rows, edge:]
+    picked[...] = total
+    at = 0
+    for level in range(1, plan.depth + 2):
+        offset, share = plan.offset[level], plan.share[level]
+        piece = fold_rows(
+            plan, lambda pos: natural[pos * rows + offset : pos * rows + offset + share, :]
+        )
+        all_part[at : at + share, :] = piece
+        if level >= 2:
+            late_part[at - plan.share[1] : at - plan.share[1] + share, :] = piece
+        if level >= 3:
+            low = at - plan.share[1] - plan.share[2]
+            high_part[low : low + share, :] = piece
+        at += share
+
+
+def leaf_kernel(plan, *refs):
+    count = plan.fronts
+    packs, (whole, ahead, update) = refs[:count], refs[count:]
+    front, _ = place()
+    rhs, upd, full, rows = plan.rhs, plan.upd, plan.full, plan.rows
+    for slot in range(count):
+        at = pl.multiple_of((front ^ slot) * rows, rows)
+        whole[pl.ds(at, rows), :] = packs[slot][rows:, :]
+    flipped = whole[:, full:].T
+    solved = nt(flipped[:rhs], whole[:, :full])
+    ahead[:rhs, :] = solved
+    ahead[rhs:, :] = flipped[rhs : rhs + upd]
+    update[:rhs, :upd] = nt(solved, flipped[rhs : rhs + upd])
+
+
+def assemble(plan, level, parts, whole):
+    blocks, share = plan.blocks[level], plan.share[level]
+    _, group = place()
+    for slot in range(blocks):
+        least = 1 if slot < 2 else 2 if slot < 4 else 3
+        first = sum(plan.share[below] for below in range(least, level))
+        inner = (group & (blocks - 1)) ^ slot
+        for front, piece in unfold_rows(plan, parts[slot][first : first + share, :]):
+            dest = pl.multiple_of(front * plan.rows + inner * share, share)
+            whole[pl.ds(dest, share), :] = piece
+
+
+def solve_level(plan, level, pattern, parts, whole):
+    front, group = place()
+    assemble(plan, level, parts, whole)
+    hot = one_hot(plan.child_ids(level, group, pattern), plan.full)
+    matrix = whole[:, : plan.full]
+    flipped = whole[:, plan.full :].T
+    right, block = flipped[: plan.rhs], flipped[plan.rhs : plan.rhs + plan.upd]
+    ahead = nt(jnp.concatenate([right, hot.T], axis=0), matrix)
+    both = nn(jnp.concatenate([ahead, block], axis=0), matrix)
+    result = [nn(both, hot[:, : plan.upd]), own_columns(plan, front, both)]
+    if level <= plan.depth:
+        fold = both[plan.rhs + hot.shape[1] :]
+        result = [nn(fold, hot), nt(right, fold)] + result
+    return result
+
+
+def level_kernel(plan, level, pattern, *refs):
+    parts, outs = refs[: plan.blocks[level]], refs[plan.blocks[level] :]
+    for out, value in zip(outs, solve_level(plan, level, pattern, parts, outs[-1])):
+        out[...] = value
+
+
+def upper_kernel(plan, pattern, leaf_all, leaf_ahead, top_s, *refs):
+    rhs, upd, group = plan.rhs, plan.upd, place()[1]
+    updates = [jnp.concatenate([refs[at][:rhs, :upd], refs[at + 1][:rhs, :upd]], axis=1) for at in (0, 2)]
+    near = refs[4][:rhs, :upd]
+    picks, columns = {1: refs[5][...], 2: refs[6][...]}, {1: refs[7][...], 2: refs[8][...]}
+    parts, (out, whole3, whole4) = refs[9:17], refs[17:]
+    cross, start, picks[3], columns[3] = solve_level(plan, 3, pattern, parts, whole3)
+    picks[4], columns[4] = solve_level(plan, 4, pattern, parts, whole4)
+    leaf_back = own_columns(plan, place()[0], nn(leaf_ahead[...], leaf_all[:, : plan.full]))
+    none = jnp.zeros((upd, upd), jnp.float32)
+    unit = one_hot(lax.broadcasted_iota(jnp.int32, (1, upd), 1), upd)
+
+    def step(terms, part):
+        known = jnp.concatenate([part[:rhs], jnp.zeros((upd, part.shape[1]), jnp.float32)], axis=0)
+        return known - nn(jnp.concatenate(terms, axis=1), part[rhs:])
+
+    gap = jnp.zeros((rhs, upd), jnp.float32)
+    both = jnp.concatenate(
+        [jnp.concatenate([near, gap], axis=1), jnp.concatenate([none, unit], axis=1)], axis=0
+    )
+    u3 = jnp.concatenate([start, none], axis=0) - nt(both, cross)
+    fixed = [jnp.concatenate([pair, jnp.zeros((upd, 2 * upd), jnp.float32)], axis=0) for pair in updates]
+    terms = {4: [u3, jnp.concatenate([top_s[...], none], axis=0)]}
+    terms[3] = [both, step(terms[4], picks[4])]
+    terms[2] = [fixed[1], step(terms[3], picks[3])]
+    terms[1] = [fixed[0], step(terms[2], picks[2])]
+    leaf_out = step([step(terms[1], picks[1])], leaf_back)
+    gap = jnp.zeros((rhs + upd, upd), jnp.float32)
+    chosen = jnp.concatenate([columns[4][: rhs + upd], none_wide(plan), columns[4][rhs + upd :]], axis=0)
+    weight = jnp.concatenate([terms[4][0], gap, terms[4][1]], axis=1)
+    for level in (3, 2, 1):
+        here = plan.label(level, group) == group
+        chosen = jnp.where(here, columns[level], chosen)
+        weight = jnp.where(here, jnp.concatenate(terms[level], axis=1), weight)
+    out[...] = jnp.concatenate([leaf_out, step([weight], chosen)], axis=1)
+
+
+def none_wide(plan):
+    return jnp.zeros((plan.upd, plan.rows), jnp.float32)
+
+
+def finish_kernel(plan, base, far, out):
+    rhs, upd, rows = plan.rhs, plan.upd, plan.rows
+    total = base[:rhs] + nn(far[:rhs, :upd], base[rhs:])
+    out[0, 0] = total[:, :rows]
+    out[1, 0] = total[:, rows:]
+
+
+def update_kernel(plan, start, cross, mine, other, out):
+    rhs, upd = plan.rhs, plan.upd
+    both = jnp.concatenate([mine[:rhs, :upd], other[:rhs, :upd]], axis=1)
+    out[:rhs, :upd] = start[...] - nt(both, cross[...])
 
 
 def partner(block, axis, distance):
@@ -30,7 +299,7 @@
     )
 
 
-def body(
+def general(
     leaf_rhs, sep_rhs, leaf_inverse, sep_inverse, leaf_block, sep_block, pattern, outer_solution
 ):
     group_count = lax.axis_size("leaf")
@@ -106,6 +375,87 @@
     return jnp.stack([leaf_x, sep_x])[:, None]
 
 
+def chain(
+    plan, leaf_rhs, sep_rhs, leaf_inverse, sep_inverse, leaf_block, sep_block, pattern, outer
+):
+    full, rows, rhs, upd, width = plan.full, plan.rows, plan.rhs, plan.upd, plan.width
+
+    def kernel(body, outs, *args, extra=(), **kw):
+        return call(functools.partial(body, plan, *extra), outs, args, **kw)
+
+    pack, ids = kernel(
+        pack_kernel,
+        [(2 * rows, width), ((pattern.shape[0] * pattern.shape[1], upd), jnp.int32)],
+        pattern, leaf_rhs, sep_rhs, leaf_inverse, sep_inverse, leaf_block, sep_block, outer,
+        chip=False,
+    )
+    across = exchange(pack, "front", 3)
+    beside = exchange(pack, "front", 1)
+    beyond = exchange(across, "front", 1)
+    wide = 4 * full
+    all_part, late_part, high_part, top_s = kernel(
+        spread_kernel,
+        [
+            (rows, wide),
+            (rows - plan.share[1], wide),
+            (plan.share[3] + plan.share[4], wide),
+            (rhs, upd),
+        ],
+        pack, beside, beyond, across,
+        scratch=[pltpu.VMEM((full, width), jnp.float32)],
+    )
+    all_core = exchange(all_part, "leaf", 1)
+    by_x = exchange(late_part, "leaf", 2)
+    by_y = exchange(high_part, "leaf", 4)
+    by_xy = exchange(high_part, "leaf", 6)
+    leaf_all, leaf_ahead, u0 = kernel(
+        leaf_kernel,
+        [(full, width), (rhs + upd, full), (rhs + 8, 128)],
+        pack, beside, beyond, across,
+    )
+    u0_far = exchange(u0, "leaf", 1)
+
+    def level_of(level, *parts):
+        tall = rhs + 3 * upd
+        return kernel(
+            level_kernel,
+            [(upd, 2 * upd), (rhs, upd), (tall, upd), (tall, rows)],
+            ids, *parts,
+            extra=(level,),
+            scratch=[pltpu.VMEM((full, width), jnp.float32)],
+        )
+
+    cross1, start1, picks1, columns1 = level_of(1, all_part, all_core)
+    (u1,) = kernel(update_kernel, [(rhs + 8, 128)], start1, cross1, u0, u0_far)
+    u1_far = exchange(u1, "leaf", 2)
+    by_x, by_y, by_xy, u1_far = lax.optimization_barrier((by_x, by_y, by_xy, u1_far))
+    by_x_core = exchange(by_x, "leaf", 1)
+    by_y_core, by_xy_core = exchange(by_y, "leaf", 1), exchange(by_xy, "leaf", 1)
+    cross2, start2, picks2, columns2 = level_of(2, all_part, all_core, by_x, by_x_core)
+    (u2,) = kernel(update_kernel, [(rhs + 8, 128)], start2, cross2, u1, u1_far)
+    u2_far = exchange(u2, "leaf", 4)
+    by_y, _ = lax.optimization_barrier((by_y, u2))
+    (base,) = kernel(
+        upper_kernel,
+        [(rhs + upd, 2 * rows)],
+        ids, leaf_all, leaf_ahead, top_s, u0, u0_far, u1, u1_far, u2,
+        picks1, picks2, columns1, columns2,
+        all_part, all_core, by_x, by_x_core, by_y, by_y_core, by_xy, by_xy_core,
+        scratch=[pltpu.VMEM((full, width), jnp.float32)] * 2,
+    )
+    (out,) = kernel(finish_kernel, [(2, 1, rhs, rows)], base, u2_far)
+    return out
+
+
+def body(*args):
+    groups, fronts = lax.axis_size("leaf"), lax.axis_size("front")
+    rhs, rows, upd = args[0].shape[1], args[0].shape[2], args[4].shape[1]
+    plan = Plan(groups, fronts, rhs, upd, rows)
+    if (groups, fronts) == (8, 4) and rows == 64 and rhs == 64 and upd == 32:
+        return chain(plan, *args)
+    return general(*args)
+
+
 def solution(mesh):
     placed = (
         P("leaf", None, "front"),

time: 696 us -> 37.3 us (0.05)
  waiting for transfers between devices: 565 us -> 13.7 us
  blocking collectives: 83.1 us -> 0 us
  local copies, waits for them, and re-layouts: 16.8 us -> 0 us
  between operations: 13.6 us -> 0.08 us
  matrix products: 12.1 us -> 0 us
  starting transfers between devices: 3.61 us -> 15.7 us
  Pallas kernels: 0 us -> 7.68 us
    psum x4 -> x0, waiting for transfers between devices: 464 us -> none  [block_sum(): return lax.psum(term, ('leaf', 'front'))]
    unnamed x14 -> x0, waiting for transfers between devices: 92.4 us -> none
    all_gather x6 -> x0, blocking collectives: 83.1 us -> none  [the longest x4 53.7 us: block_sum(): return lax.all_gather(piece, 'front', axis=1, tiled=True)]
    ppermute x6 -> x13, starting transfers between devices: 3.27 us -> 15.7 us  [exchange(): lax.ppermute(block, axis, [(src, src ^ mask) for src in range(count)])]
    unnamed x31 -> x0, local copies, waits for them, and re-layouts: 9.82 us -> none
    dot_general x20 -> x0, matrix products: 8.97 us -> none  [the longest x11 5.28 us: times_rows(): jnp.dot(vectors, matrix, precision=lax.Precision.HIGHEST, preferred_eleme...]
    pallas_call x0 -> x9, Pallas kernels: none -> 7.68 us  [call(): pl.pallas_call(kernel, out_shape=[jax.ShapeDtypeStruct(out, jnp.float32)...]
  transfers between devices with their start and end apart: 15 -> 13, of which waited for: 15 -> 7; matrix products, arithmetic and copies ran while one was open for 0% -> 0% of each run, Pallas kernels for 0% -> 15%
where the time goes in v3:
time: 37.3 us; the launch traced here: 37.1 us
  starting transfers between devices  15.7 us (42%)
  waiting for transfers between devices  13.7 us (37%)
  Pallas kernels  7.68 us (21%)
    ppermute x13, starting transfers between devices, exchange(): lax.ppermute(block, axis, [(src, src ^ mask) for src in range(count)])  15.7 us
    ppermute x13, waiting for transfers between devices, exchange(): lax.ppermute(block, axis, [(src, src ^ mask) for src in range(count)])  13.7 us
    pallas_call x9, Pallas kernels, call(): pl.pallas_call(kernel, out_shape=[jax.ShapeDtypeStruct(out, jnp.float32)...  7.68 us
  transfers between devices with their start and end apart: 13, of which 7 were waited for; matrix products, arithmetic and copies ran while one was open for 0% of the time, Pallas kernels for 15%

profile of v3, /device:TPU:0, one launch (start us, length us, event | category | flops | bytes accessed | tf_op | source)
XLA Modules:
  0.0 37.1 jit_solution(13456266827298970183)
XLA Ops:
  0.0 1.2 %shard_map.82 = (f32[128,384]{1,0:T(8,128)S(1)}, s32[16,32]{1,0:T(8,128)S(1)}) custom-call(s32[2,8,32]{2,1,0:T(8,128)} %pattern.1, f32[1,64,64]{2,1,0:T(8,128)} %lr.1, f32[1,64,64]{2,1,0:T(8,128)} %sr.1, f32[1,64,256]{2,1,0:T(8,128)} %li.1, f32[1,64,256]{2,1,0:T(8,128)} %si.1, f32[1,32,64]{2,1,0:T(8,128)} %lu.1, f32[1,32,64]{2,1,0:T(8,128)} %su.1, ...), custom_call_target="tpu_custom_call" | custom-call | flops 1000 | bytes 1000 | tf_op jit(solution)/shard_map/pallas_call | solution.py:45
  1.2 5.1 %collective-permute-start.1 = (f32[128,384]{1,0:T(8,128)S(1)}, f32[128,384]{1,0:T(8,128)S(1)}, u32[]{:S(2)}, u32[]{:S(2)}) collective-permute-start(f32[128,384]{1,0:T(8,128)S(1)} %get-tuple-element.28.refs_0_), channel_id=1, source_target_pairs={{0,3},{1,2},{2,1},{3,0},{4,7},{5,6},{6,5},{7,4},{8,11},{9,10},{10,... | collective-permute-start | bytes 589832 | tf_op jit(solution)/shard_map/ppermute | solution.py:34
  6.3 0.0 collective-permute-start
  6.3 5.8 %collective-permute-done.1.refs_3_ = f32[128,384]{1,0:T(8,128)S(1)} collective-permute-done((f32[128,384]{1,0:T(8,128)S(1)}, f32[128,384]{1,0:T(8,128)S(1)}, u32[]{:S(2)}, u32[]{:S(2)}) %collective-permute-start.1) | collective-permute-done | bytes 196640 | tf_op jit(solution)/shard_map/ppermute | solution.py:34
  12.1 3.1 %collective-permute-start.2 = (f32[128,384]{1,0:T(8,128)S(1)}, f32[128,384]{1,0:T(8,128)S(1)}, u32[]{:S(2)}, u32[]{:S(2)}) collective-permute-start(f32[128,384]{1,0:T(8,128)S(1)} %collective-permute-done.1.refs_3_), channel_id=1, source_target_pairs={{0,1},{1,0},{2,3},{3,2},{4,5},{5,4},{6,7},{7,6},{8,9},{9,8},{10,11... | collective-permute-start | bytes 589832 | tf_op jit(solution)/shard_map/ppermute | solution.py:34
  15.1 0.5 %collective-permute-done.refs_1_ = f32[128,384]{1,0:T(8,128)S(1)} collective-permute-done((f32[128,384]{1,0:T(8,128)S(1)}, f32[128,384]{1,0:T(8,128)S(1)}, u32[]{:S(2)}, u32[]{:S(2)}) %collective-permute-start) | collective-permute-done | bytes 196640 | tf_op jit(solution)/shard_map/ppermute | solution.py:34
  15.6 4.1 %collective-permute-done.2.refs_2_ = f32[128,384]{1,0:T(8,128)S(1)} collective-permute-done((f32[128,384]{1,0:T(8,128)S(1)}, f32[128,384]{1,0:T(8,128)S(1)}, u32[]{:S(2)}, u32[]{:S(2)}) %collective-permute-start.2) | collective-permute-done | bytes 196640 | tf_op jit(solution)/shard_map/ppermute | solution.py:34
  19.7 0.1 shard_map.84
  19.9 0.1 collective-permute-start.4
  20.0 1.6 %collective-permute-start.5 = (f32[32,1024]{1,0:T(8,128)S(1)}, f32[32,1024]{1,0:T(8,128)S(1)}, u32[]{:S(2)}, u32[]{:S(2)}) collective-permute-start(f32[32,1024]{1,0:T(8,128)S(1)} %get-tuple-element.36), channel_id=1, source_target_pairs={{0,8},{4,12},{8,0},{12,4},{16,24},{20,28},{24,16},{28,20},{1,9},{5... | collective-permute-start | bytes 393224 | tf_op jit(solution)/shard_map/ppermute | solution.py:34
  21.5 0.4 %shard_map.83 = (f32[256,384]{1,0:T(8,128)S(1)}, f32[96,256]{1,0:T(8,128)S(1)}, f32[72,128]{1,0:T(8,128)S(1)}) custom-call(f32[128,384]{1,0:T(8,128)S(1)} %get-tuple-element.28.refs_0_, f32[128,384]{1,0:T(8,128)S(1)} %collective-permute-done.refs_1_, f32[128,384]{1,0:T(8,128)S(1)} %collective-permute-done.2.refs_2_, ...), custom_call_target="tpu_custom_call" | custom-call | flops 1000 | bytes 1000 | tf_op jit(solution)/shard_map/pallas_call | solution.py:45
  22.0 0.2 collective-permute-start.3
  22.2 1.5 %collective-permute-start.7 = (f32[16,1024]{1,0:T(8,128)S(1)}, f32[16,1024]{1,0:T(8,128)S(1)}, u32[]{:S(2)}, u32[]{:S(2)}) collective-permute-start(f32[16,1024]{1,0:T(8,128)S(1)} %get-tuple-element.37), channel_id=1, source_target_pairs={{0,24},{4,28},{8,16},{12,20},{16,8},{20,12},{24,0},{28,4},{1,25},{... | collective-permute-start | bytes 196616 | tf_op jit(solution)/shard_map/ppermute | solution.py:34
  23.7 0.5 %collective-permute-start.6 = (f32[16,1024]{1,0:T(8,128)S(1)}, f32[16,1024]{1,0:T(8,128)S(1)}, u32[]{:S(2)}, u32[]{:S(2)}) collective-permute-start(f32[16,1024]{1,0:T(8,128)S(1)} %get-tuple-element.37), channel_id=1, source_target_pairs={{0,16},{4,20},{8,24},{12,28},{16,0},{20,4},{24,8},{28,12},{1,17},{... | collective-permute-start | bytes 196616 | tf_op jit(solution)/shard_map/ppermute | solution.py:34
  24.2 0.0 collective-permute-done.4.refs_1_.refs_10_
  24.2 1.0 %shard_map.85 = (f32[32,64]{1,0:T(8,128)S(1)}, f32[64,32]{1,0:T(8,128)S(1)}, f32[160,32]{1,0:T(8,128)S(1)}, f32[160,64]{1,0:T(8,128)S(1)}) custom-call(s32[16,32]{1,0:T(8,128)S(1)} %get-tuple-element.27.pattern, f32[64,1024]{1,0:T(8,128)S(1)} %get-tuple-element.33.refs_0_.refs_9_, f32[64,1024]{1,0:T(8,128)S(1)} %collective-permute-done.4.refs_1_.refs_10_), custom_call_target="tpu_custom_call" | custom-call | flops 1000 | bytes 1000 | tf_op jit(solution)/shard_map/pallas_call | solution.py:45
  25.2 0.0 collective-permute-done.3.other.refs_1_
  25.2 0.2 shard_map.86.mine.refs_2_
  25.4 1.6 %collective-permute-start.8 = (f32[72,128]{1,0:T(8,128)S(1)}, f32[72,128]{1,0:T(8,128)S(1)}, u32[]{:S(2)}, u32[]{:S(2)}) collective-permute-start(f32[72,128]{1,0:T(8,128)S(1)} %shard_map.86.mine.refs_2_), channel_id=1, source_target_pairs={{0,8},{4,12},{8,0},{12,4},{16,24},{20,28},{24,16},{28,20},{1,9},{5... | collective-permute-start | bytes 110600 | tf_op jit(solution)/shard_map/ppermute | solution.py:34
  26.9 1.4 %collective-permute-done.7.refs_15_ = f32[16,1024]{1,0:T(8,128)S(1)} collective-permute-done((f32[16,1024]{1,0:T(8,128)S(1)}, f32[16,1024]{1,0:T(8,128)S(1)}, u32[]{:S(2)}, u32[]{:S(2)}) %collective-permute-start.7) | collective-permute-done | bytes 65568 | tf_op jit(solution)/shard_map/ppermute | solution.py:34
  28.4 0.8 %collective-permute-done.6.refs_13_ = f32[16,1024]{1,0:T(8,128)S(1)} collective-permute-done((f32[16,1024]{1,0:T(8,128)S(1)}, f32[16,1024]{1,0:T(8,128)S(1)}, u32[]{:S(2)}, u32[]{:S(2)}) %collective-permute-start.6) | collective-permute-done | bytes 65568 | tf_op jit(solution)/shard_map/ppermute | solution.py:34
  29.1 0.0 collective-permute-done.5.refs_2_.refs_11_
  29.1 0.3 collective-permute-done.8.other.refs_3_
  29.4 0.0 collective-permute-start.9
  29.4 0.5 %collective-permute-start.10 = (f32[16,1024]{1,0:T(8,128)S(1)}, f32[16,1024]{1,0:T(8,128)S(1)}, u32[]{:S(2)}, u32[]{:S(2)}) collective-permute-start(f32[16,1024]{1,0:T(8,128)S(1)} %collective-permute-done.6.refs_13_), channel_id=1, source_target_pairs={{0,4},{4,0},{8,12},{12,8},{16,20},{20,16},{24,28},{28,24},{1,5},{5... | collective-permute-start | bytes 196616 | tf_op jit(solution)/shard_map/ppermute | solution.py:34
  29.9 0.0 collective-permute-start.11
  29.9 0.8 %collective-permute-done.9.refs_3_.refs_12_ = f32[32,1024]{1,0:T(8,128)S(1)} collective-permute-done((f32[32,1024]{1,0:T(8,128)S(1)}, f32[32,1024]{1,0:T(8,128)S(1)}, u32[]{:S(2)}, u32[]{:S(2)}) %collective-permute-start.9) | collective-permute-done | bytes 131104 | tf_op jit(solution)/shard_map/ppermute | solution.py:34
  30.7 1.0 %shard_map.87 = (f32[32,64]{1,0:T(8,128)S(1)}, f32[64,32]{1,0:T(8,128)S(1)}, f32[160,32]{1,0:T(8,128)S(1)}, f32[160,64]{1,0:T(8,128)S(1)}) custom-call(s32[16,32]{1,0:T(8,128)S(1)} %get-tuple-element.27.pattern, f32[64,1024]{1,0:T(8,128)S(1)} %get-tuple-element.33.refs_0_.refs_9_, f32[64,1024]{1,0:T(8,128)S(1)} %collective-permute-done.4.refs_1_.refs_10_, ...), custom_call_target="tpu_custom_call" | custom-call | flops 1000 | bytes 1000 | tf_op jit(solution)/shard_map/pallas_call | solution.py:45
  31.7 0.2 shard_map.88.refs_4_
  31.9 1.6 %collective-permute-start.12 = (f32[72,128]{1,0:T(8,128)S(1)}, f32[72,128]{1,0:T(8,128)S(1)}, u32[]{:S(2)}, u32[]{:S(2)}) collective-permute-start(f32[72,128]{1,0:T(8,128)S(1)} %shard_map.88.refs_4_), channel_id=1, source_target_pairs={{0,16},{4,20},{8,24},{12,28},{16,0},{20,4},{24,8},{28,12},{1,17},{... | collective-permute-start | bytes 110600 | tf_op jit(solution)/shard_map/ppermute | solution.py:34
  33.5 0.0 collective-permute-done.10.refs_14_
  33.5 0.0 collective-permute-done.11.refs_16_
  33.5 2.7 %shard_map.89.base = f32[96,128]{1,0:T(8,128)S(1)} custom-call(s32[16,32]{1,0:T(8,128)S(1)} %get-tuple-element.27.pattern, f32[256,384]{1,0:T(8,128)S(1)} %get-tuple-element.29.leaf_all, f32[96,256]{1,0:T(8,128)S(1)} %get-tuple-element.30.leaf_ahead, f32[64,32]{1,0:T(8,128)S(1)} %get-tuple-element.31.top_s, f32[72,128]{1,0:T(8,128)S(1)} %get-tuple-element.32.mine.refs_0_, ...), custom_call_target="tpu_custom_call" | custom-call | flops 1000 | bytes 1000 | tf_op jit(solution)/shard_map/pallas_call | solution.py:45
  36.3 0.0 collective-permute-done.12.far
  36.3 0.8 %shard_map.90 = f32[2,1,64,64]{3,2,1,0:T(8,128)} custom-call(f32[96,128]{1,0:T(8,128)S(1)} %shard_map.89.base, f32[72,128]{1,0:T(8,128)S(1)} %collective-permute-done.12.far), custom_call_target="tpu_custom_call" | custom-call | flops 1000 | bytes 1000 | tf_op jit(solution)/shard_map/pallas_call | solution.py:45
Async XLA Ops:
  1.2 10.9 %collective-permute-start.1 = (f32[128,384]{1,0:T(8,128)S(1)}, f32[128,384]{1,0:T(8,128)S(1)}, u32[]{:S(2)}, u32[]{:S(2)}) collective-permute-start(f32[128,384]{1,0:T(8,128)S(1)} %get-tuple-element.28.refs_0_), channel_id=1, source_target_pairs={{0,3},{1,2},{2,1},{3,0},{4,7},{5,6},{6,5},{7,4},{8,11},{9,10},{10,... | collective-permute-start | bytes 589832 | tf_op jit(solution)/shard_map/ppermute | solution.py:34
  6.3 9.3 %collective-permute-start = (f32[128,384]{1,0:T(8,128)S(1)}, f32[128,384]{1,0:T(8,128)S(1)}, u32[]{:S(2)}, u32[]{:S(2)}) collective-permute-start(f32[128,384]{1,0:T(8,128)S(1)} %get-tuple-element.28.refs_0_), channel_id=1, source_target_pairs={{0,1},{1,0},{2,3},{3,2},{4,5},{5,4},{6,7},{7,6},{8,9},{9,8},{10,11... | collective-permute-start | bytes 589832 | tf_op jit(solution)/shard_map/ppermute | solution.py:34
  12.1 7.7 %collective-permute-start.2 = (f32[128,384]{1,0:T(8,128)S(1)}, f32[128,384]{1,0:T(8,128)S(1)}, u32[]{:S(2)}, u32[]{:S(2)}) collective-permute-start(f32[128,384]{1,0:T(8,128)S(1)} %collective-permute-done.1.refs_3_), channel_id=1, source_target_pairs={{0,1},{1,0},{2,3},{3,2},{4,5},{5,4},{6,7},{7,6},{8,9},{9,8},{10,11... | collective-permute-start | bytes 589832 | tf_op jit(solution)/shard_map/ppermute | solution.py:34
  19.9 4.3 %collective-permute-start.4 = (f32[64,1024]{1,0:T(8,128)S(1)}, f32[64,1024]{1,0:T(8,128)S(1)}, u32[]{:S(2)}, u32[]{:S(2)}) collective-permute-start(f32[64,1024]{1,0:T(8,128)S(1)} %get-tuple-element.33.refs_0_.refs_9_), channel_id=1, source_target_pairs={{0,4},{4,0},{8,12},{12,8},{16,20},{20,16},{24,28},{28,24},{1,5},{5... | collective-permute-start | bytes 786440 | tf_op jit(solution)/shard_map/ppermute | solution.py:34
  20.0 9.2 %collective-permute-start.5 = (f32[32,1024]{1,0:T(8,128)S(1)}, f32[32,1024]{1,0:T(8,128)S(1)}, u32[]{:S(2)}, u32[]{:S(2)}) collective-permute-start(f32[32,1024]{1,0:T(8,128)S(1)} %get-tuple-element.36), channel_id=1, source_target_pairs={{0,8},{4,12},{8,0},{12,4},{16,24},{20,28},{24,16},{28,20},{1,9},{5... | collective-permute-start | bytes 393224 | tf_op jit(solution)/shard_map/ppermute | solution.py:34
  22.0 3.2 %collective-permute-start.3 = (f32[72,128]{1,0:T(8,128)S(1)}, f32[72,128]{1,0:T(8,128)S(1)}, u32[]{:S(2)}, u32[]{:S(2)}) collective-permute-start(f32[72,128]{1,0:T(8,128)S(1)} %get-tuple-element.32.mine.refs_0_), channel_id=1, source_target_pairs={{0,4},{4,0},{8,12},{12,8},{16,20},{20,16},{24,28},{28,24},{1,5},{5... | collective-permute-start | bytes 110600 | tf_op jit(solution)/shard_map/ppermute | solution.py:34
  22.2 6.2 %collective-permute-start.7 = (f32[16,1024]{1,0:T(8,128)S(1)}, f32[16,1024]{1,0:T(8,128)S(1)}, u32[]{:S(2)}, u32[]{:S(2)}) collective-permute-start(f32[16,1024]{1,0:T(8,128)S(1)} %get-tuple-element.37), channel_id=1, source_target_pairs={{0,24},{4,28},{8,16},{12,20},{16,8},{20,12},{24,0},{28,4},{1,25},{... | collective-permute-start | bytes 196616 | tf_op jit(solution)/shard_map/ppermute | solution.py:34
  23.7 5.5 %collective-permute-start.6 = (f32[16,1024]{1,0:T(8,128)S(1)}, f32[16,1024]{1,0:T(8,128)S(1)}, u32[]{:S(2)}, u32[]{:S(2)}) collective-permute-start(f32[16,1024]{1,0:T(8,128)S(1)} %get-tuple-element.37), channel_id=1, source_target_pairs={{0,16},{4,20},{8,24},{12,28},{16,0},{20,4},{24,8},{28,12},{1,17},{... | collective-permute-start | bytes 196616 | tf_op jit(solution)/shard_map/ppermute | solution.py:34
  25.4 4.0 %collective-permute-start.8 = (f32[72,128]{1,0:T(8,128)S(1)}, f32[72,128]{1,0:T(8,128)S(1)}, u32[]{:S(2)}, u32[]{:S(2)}) collective-permute-start(f32[72,128]{1,0:T(8,128)S(1)} %shard_map.86.mine.refs_2_), channel_id=1, source_target_pairs={{0,8},{4,12},{8,0},{12,4},{16,24},{20,28},{24,16},{28,20},{1,9},{5... | collective-permute-start | bytes 110600 | tf_op jit(solution)/shard_map/ppermute | solution.py:34
  29.4 1.3 %collective-permute-start.9 = (f32[32,1024]{1,0:T(8,128)S(1)}, f32[32,1024]{1,0:T(8,128)S(1)}, u32[]{:S(2)}, u32[]{:S(2)}) collective-permute-start(f32[32,1024]{1,0:T(8,128)S(1)} %collective-permute-done.5.refs_2_.refs_11_), channel_id=1, source_target_pairs={{0,4},{4,0},{8,12},{12,8},{16,20},{20,16},{24,28},{28,24},{1,5},{5... | collective-permute-start | bytes 393224 | tf_op jit(solution)/shard_map/ppermute | solution.py:34
  29.4 4.1 %collective-permute-start.10 = (f32[16,1024]{1,0:T(8,128)S(1)}, f32[16,1024]{1,0:T(8,128)S(1)}, u32[]{:S(2)}, u32[]{:S(2)}) collective-permute-start(f32[16,1024]{1,0:T(8,128)S(1)} %collective-permute-done.6.refs_13_), channel_id=1, source_target_pairs={{0,4},{4,0},{8,12},{12,8},{16,20},{20,16},{24,28},{28,24},{1,5},{5... | collective-permute-start | bytes 196616 | tf_op jit(solution)/shard_map/ppermute | solution.py:34
  29.9 3.6 %collective-permute-start.11 = (f32[16,1024]{1,0:T(8,128)S(1)}, f32[16,1024]{1,0:T(8,128)S(1)}, u32[]{:S(2)}, u32[]{:S(2)}) collective-permute-start(f32[16,1024]{1,0:T(8,128)S(1)} %collective-permute-done.7.refs_15_), channel_id=1, source_target_pairs={{0,4},{4,0},{8,12},{12,8},{16,20},{20,16},{24,28},{28,24},{1,5},{5... | collective-permute-start | bytes 196616 | tf_op jit(solution)/shard_map/ppermute | solution.py:34
  31.9 4.3 %collective-permute-start.12 = (f32[72,128]{1,0:T(8,128)S(1)}, f32[72,128]{1,0:T(8,128)S(1)}, u32[]{:S(2)}, u32[]{:S(2)}) collective-permute-start(f32[72,128]{1,0:T(8,128)S(1)} %shard_map.88.refs_4_), channel_id=1, source_target_pairs={{0,16},{4,20},{8,24},{12,28},{16,0},{20,4},{24,8},{28,12},{1,17},{... | collective-permute-start | bytes 110600 | tf_op jit(solution)/shard_map/ppermute | solution.py:34

commit v4 on v3

--- a/solution.py
+++ b/solution.py
@@ -104,6 +104,16 @@
     return result
 
 
+def dense(value):
+    count = value.shape[0] // 4
+    return jnp.concatenate([value[pos * count : (pos + 1) * count] for pos in range(4)], axis=1)
+
+
+def undense(value):
+    count = value.shape[1] // 4
+    return jnp.concatenate([value[:, pos * count : (pos + 1) * count] for pos in range(4)], axis=0)
+
+
 def place():
     return lax.axis_index("front"), lax.axis_index("leaf")
 
@@ -115,9 +125,9 @@
     empty = jnp.zeros((upd, rows), jnp.float32)
     out[:rows, :full] = si[0]
     out[:rows, full:] = jnp.concatenate([sr[0], su[0], empty], axis=0).T
-    out[:rows, full + rhs + upd :] = nn(outer[...], one_hot(pattern[1, 0:1, :], rows, front * rows))
     out[rows:, :full] = li[0]
     out[rows:, full:] = jnp.concatenate([lr[0], lu[0], empty], axis=0).T
+    out[:rhs, full + rhs + upd :] = nn(outer[...], one_hot(pattern[1, 0:1, :], rows, front * rows))
 
 
 def fold_rows(plan, rows_of):
@@ -142,32 +152,39 @@
         yield front, jnp.concatenate(pieces, axis=1)
 
 
+def fold_levels(plan, packs, low, levels, natural):
+    front, _ = place()
+    count, base = natural.shape[0] // plan.fronts, plan.offset[levels[0]]
+    for slot, pack in enumerate(packs):
+        at = pl.multiple_of((front ^ slot) * count, count)
+        natural[pl.ds(at, count), :] = pack[low[slot] : low[slot] + count, :]
+    for level in levels:
+        offset, share = plan.offset[level] - base, plan.share[level]
+        yield offset, fold_rows(
+            plan, lambda pos: natural[pos * count + offset : pos * count + offset + share, :]
+        )
+
+
 def spread_kernel(plan, *refs):
-    count = plan.fronts
-    packs = refs[:count]
-    all_part, late_part, high_part, picked, natural = refs[count:]
-    rows, edge = plan.rows, plan.full + plan.rhs + plan.upd
-    front, _ = place()
-    for slot in range(count):
-        at = pl.multiple_of((front ^ slot) * rows, rows)
-        natural[pl.ds(at, rows), :] = packs[slot][:rows, :]
-    total = packs[0][:rows, edge:]
-    for slot in range(1, count):
-        total = total + packs[slot][:rows, edge:]
+    packs = refs[: plan.fronts]
+    all_part, late_part, high_part, picked, natural = refs[plan.fronts :]
+    edge = plan.full + plan.rhs + plan.upd
+    total = packs[0][: plan.rhs, edge:]
+    for pack in packs[1:]:
+        total = total + pack[: plan.rhs, edge:]
     picked[...] = total
-    at = 0
-    for level in range(1, plan.depth + 2):
-        offset, share = plan.offset[level], plan.share[level]
-        piece = fold_rows(
-            plan, lambda pos: natural[pos * rows + offset : pos * rows + offset + share, :]
-        )
-        all_part[at : at + share, :] = piece
-        if level >= 2:
-            late_part[at - plan.share[1] : at - plan.share[1] + share, :] = piece
-        if level >= 3:
-            low = at - plan.share[1] - plan.share[2]
-            high_part[low : low + share, :] = piece
-        at += share
+    levels = range(1, plan.depth + 2)
+    for at, piece in fold_levels(plan, packs, [0] * 4, levels, natural):
+        for out, level in ((all_part, 1), (late_part, 2), (high_part, 3)):
+            low = at - plan.offset[level]
+            if low >= 0:
+                out[low : low + piece.shape[0], :] = piece
+
+
+def far_kernel(plan, high, all_core, out):
+    count = high.shape[0]
+    out[:count, :] = high[...]
+    out[count:, :] = all_core[plan.offset[3] :, :]
 
 
 def leaf_kernel(plan, *refs):
@@ -175,59 +192,101 @@
     packs, (whole, ahead, update) = refs[:count], refs[count:]
     front, _ = place()
     rhs, upd, full, rows = plan.rhs, plan.upd, plan.full, plan.rows
+    low = rows
     for slot in range(count):
         at = pl.multiple_of((front ^ slot) * rows, rows)
-        whole[pl.ds(at, rows), :] = packs[slot][rows:, :]
+        whole[pl.ds(at, rows), :] = packs[slot][low : low + rows, :]
     flipped = whole[:, full:].T
     solved = nt(flipped[:rhs], whole[:, :full])
     ahead[:rhs, :] = solved
     ahead[rhs:, :] = flipped[rhs : rhs + upd]
-    update[:rhs, :upd] = nt(solved, flipped[rhs : rhs + upd])
+    update[...] = dense(nt(solved, flipped[rhs : rhs + upd]))
 
 
 def assemble(plan, level, parts, whole):
     blocks, share = plan.blocks[level], plan.share[level]
     _, group = place()
-    for slot in range(blocks):
-        least = 1 if slot < 2 else 2 if slot < 4 else 3
-        first = sum(plan.share[below] for below in range(least, level))
+    for ref, first, slot in parts:
         inner = (group & (blocks - 1)) ^ slot
-        for front, piece in unfold_rows(plan, parts[slot][first : first + share, :]):
+        for front, piece in unfold_rows(plan, ref[first : first + share, :]):
             dest = pl.multiple_of(front * plan.rows + inner * share, share)
             whole[pl.ds(dest, share), :] = piece
 
 
-def solve_level(plan, level, pattern, parts, whole):
+def upper_parts(plan, level, refs):
+    own, own_core, by_x, by_x_core, far, far_core = refs
+    _, group = place()
+    at = plan.offset[level] - plan.offset[3]
+    late = at + plan.share[2]
+    half = plan.share[3] + plan.share[4]
+    parts = [(own, plan.offset[level], 0), (own_core, plan.offset[level], 1)]
+    parts += [(by_x, late, 2), (by_x_core, late, 3)]
+    side = 4 + 2 * (group & 1)
+    parts += [(far, at, side), (far, half + at, side ^ 1)]
+    return parts + [(far_core, at, side ^ 3), (far_core, half + at, side ^ 2)]
+
+
+def lead_level(plan, level, pattern, parts, whole):
+    assemble(plan, level, parts, whole)
+    flipped = whole[:, plan.full :].T
+    right, block = flipped[: plan.rhs], flipped[plan.rhs : plan.rhs + plan.upd]
+    fold = nn(block, whole[:, : plan.full])
+    hot = one_hot(plan.child_ids(level, place()[1], pattern), plan.full)
+    return nn(fold, hot), nt(right, fold)
+
+
+def back_level(plan, level, pattern, whole):
     front, group = place()
-    assemble(plan, level, parts, whole)
+    rhs = plan.rhs
     hot = one_hot(plan.child_ids(level, group, pattern), plan.full)
     matrix = whole[:, : plan.full]
     flipped = whole[:, plan.full :].T
-    right, block = flipped[: plan.rhs], flipped[plan.rhs : plan.rhs + plan.upd]
+    right, block = flipped[:rhs], flipped[rhs : rhs + plan.upd]
     ahead = nt(jnp.concatenate([right, hot.T], axis=0), matrix)
-    both = nn(jnp.concatenate([ahead, block], axis=0), matrix)
-    result = [nn(both, hot[:, : plan.upd]), own_columns(plan, front, both)]
-    if level <= plan.depth:
-        fold = both[plan.rhs + hot.shape[1] :]
-        result = [nn(fold, hot), nt(right, fold)] + result
-    return result
-
-
-def level_kernel(plan, level, pattern, *refs):
-    parts, outs = refs[: plan.blocks[level]], refs[plan.blocks[level] :]
-    for out, value in zip(outs, solve_level(plan, level, pattern, parts, outs[-1])):
-        out[...] = value
-
-
-def upper_kernel(plan, pattern, leaf_all, leaf_ahead, top_s, *refs):
+    stacked = jnp.concatenate([ahead, block], axis=0)
+    result = [nt(stacked, ahead[rhs : rhs + plan.upd]), nn(stacked, own_columns(plan, front, matrix))]
+    if level > plan.depth:
+        return result
+    return [nt(block, ahead[rhs:]), nt(ahead[:rhs], block)] + result
+
+
+def lead_kernel(plan, level, pattern, *refs):
+    blocks = plan.blocks[level]
+    parts = [
+        (ref, plan.offset[level] if slot < 2 else 0, slot) for slot, ref in enumerate(refs[:blocks])
+    ]
+    whole, cross, start = refs[blocks:]
+    cross[...], start[...] = lead_level(plan, level, pattern, parts, whole)
+
+
+def lower_kernel(plan, pattern, whole, leaf_all, leaf_ahead, near, far, own_part, leaf_part):
+    rhs, upd = plan.rhs, plan.upd
+    known = jnp.concatenate([undense(near[...]), undense(far[...])], axis=1)
+    _, _, picks, columns = back_level(plan, 1, pattern, whole)
+    leaf_back = nn(leaf_ahead[...], own_columns(plan, place()[0], leaf_all[:, : plan.full]))
+    both = jnp.concatenate([columns, picks], axis=1)
+    base = both[:rhs] - nn(known, both[rhs : rhs + 2 * upd])
+    slope = both[rhs + 2 * upd :]
+    own_part[:rhs] = base[:, : plan.rows]
+    own_part[rhs : rhs + 2 * upd] = jnp.zeros((2 * upd, plan.rows), jnp.float32)
+    own_part[rhs + 2 * upd :] = slope[:, : plan.rows]
+    through = jnp.concatenate([base[:, plan.rows :], -slope[:, plan.rows :]], axis=0)
+    through = nn(through, leaf_back[rhs:])
+    leaf_part[:rhs] = leaf_back[:rhs] - through[:rhs]
+    leaf_part[rhs:] = through[rhs:]
+
+
+def upper_kernel(plan, pattern, leaf_part, top_s, *refs):
     rhs, upd, group = plan.rhs, plan.upd, place()[1]
-    updates = [jnp.concatenate([refs[at][:rhs, :upd], refs[at + 1][:rhs, :upd]], axis=1) for at in (0, 2)]
-    near = refs[4][:rhs, :upd]
-    picks, columns = {1: refs[5][...], 2: refs[6][...]}, {1: refs[7][...], 2: refs[8][...]}
-    parts, (out, whole3, whole4) = refs[9:17], refs[17:]
-    cross, start, picks[3], columns[3] = solve_level(plan, 3, pattern, parts, whole3)
-    picks[4], columns[4] = solve_level(plan, 4, pattern, parts, whole4)
-    leaf_back = own_columns(plan, place()[0], nn(leaf_ahead[...], leaf_all[:, : plan.full]))
+    known = jnp.concatenate([undense(refs[0][...]), undense(refs[1][...])], axis=1)
+    near = undense(refs[2][...])
+    picks, columns = {}, {1: refs[3][...]}
+    sources, (out, whole3, whole4) = refs[5:11], refs[11:]
+    assemble(plan, 3, upper_parts(plan, 3, sources), whole3)
+    assemble(plan, 4, upper_parts(plan, 4, sources), whole4)
+    cross, start, picks[3], columns[3] = back_level(plan, 3, pattern, whole3)
+    picks[4], columns[4] = back_level(plan, 4, pattern, whole4)
+    _, _, picks[2], columns[2] = back_level(plan, 2, pattern, refs[4])
     none = jnp.zeros((upd, upd), jnp.float32)
     unit = one_hot(lax.broadcasted_iota(jnp.int32, (1, upd), 1), upd)
 
@@ -240,12 +299,13 @@
         [jnp.concatenate([near, gap], axis=1), jnp.concatenate([none, unit], axis=1)], axis=0
     )
     u3 = jnp.concatenate([start, none], axis=0) - nt(both, cross)
-    fixed = [jnp.concatenate([pair, jnp.zeros((upd, 2 * upd), jnp.float32)], axis=0) for pair in updates]
+    fixed = jnp.concatenate([known, jnp.zeros((upd, 2 * upd), jnp.float32)], axis=0)
     terms = {4: [u3, jnp.concatenate([top_s[...], none], axis=0)]}
     terms[3] = [both, step(terms[4], picks[4])]
-    terms[2] = [fixed[1], step(terms[3], picks[3])]
-    terms[1] = [fixed[0], step(terms[2], picks[2])]
-    leaf_out = step([step(terms[1], picks[1])], leaf_back)
+    terms[2] = [fixed, step(terms[3], picks[3])]
+    last = step(terms[2], picks[2])
+    terms[1] = [jnp.zeros((rhs + upd, 2 * upd), jnp.float32), last]
+    leaf_out = step([last], leaf_part)
     gap = jnp.zeros((rhs + upd, upd), jnp.float32)
     chosen = jnp.concatenate([columns[4][: rhs + upd], none_wide(plan), columns[4][rhs + upd :]], axis=0)
     weight = jnp.concatenate([terms[4][0], gap, terms[4][1]], axis=1)
@@ -262,15 +322,14 @@
 
 def finish_kernel(plan, base, far, out):
     rhs, upd, rows = plan.rhs, plan.upd, plan.rows
-    total = base[:rhs] + nn(far[:rhs, :upd], base[rhs:])
+    total = base[:rhs] + nn(undense(far[...]), base[rhs:])
     out[0, 0] = total[:, :rows]
     out[1, 0] = total[:, rows:]
 
 
 def update_kernel(plan, start, cross, mine, other, out):
-    rhs, upd = plan.rhs, plan.upd
-    both = jnp.concatenate([mine[:rhs, :upd], other[:rhs, :upd]], axis=1)
-    out[:rhs, :upd] = start[...] - nt(both, cross[...])
+    both = jnp.concatenate([undense(mine[...]), undense(other[...])], axis=1)
+    out[...] = dense(start[...] - nt(both, cross[...]))
 
 
 def partner(block, axis, distance):
@@ -406,41 +465,47 @@
     )
     all_core = exchange(all_part, "leaf", 1)
     by_x = exchange(late_part, "leaf", 2)
-    by_y = exchange(high_part, "leaf", 4)
-    by_xy = exchange(high_part, "leaf", 6)
+    leaf_beyond, _ = lax.optimization_barrier((beyond, top_s))
     leaf_all, leaf_ahead, u0 = kernel(
         leaf_kernel,
-        [(full, width), (rhs + upd, full), (rhs + 8, 128)],
-        pack, beside, beyond, across,
+        [(full, width), (rhs + upd, full), (rhs // 4, 4 * upd)],
+        pack, beside, leaf_beyond, across,
     )
     u0_far = exchange(u0, "leaf", 1)
-
-    def level_of(level, *parts):
-        tall = rhs + 3 * upd
+    high_part, _ = lax.optimization_barrier((high_part, u0))
+    (far_part,) = kernel(far_kernel, [(2 * high_part.shape[0], wide)], high_part, all_core)
+    far = lax.ppermute(far_part, "leaf", [(src, src ^ (6 if src % 2 else 4)) for src in range(plan.groups)])
+    def lead_of(level, *parts):
         return kernel(
-            level_kernel,
-            [(upd, 2 * upd), (rhs, upd), (tall, upd), (tall, rows)],
+            lead_kernel,
+            [(full, width), (upd, 2 * upd), (rhs, upd)],
             ids, *parts,
             extra=(level,),
-            scratch=[pltpu.VMEM((full, width), jnp.float32)],
         )
 
-    cross1, start1, picks1, columns1 = level_of(1, all_part, all_core)
-    (u1,) = kernel(update_kernel, [(rhs + 8, 128)], start1, cross1, u0, u0_far)
+    whole1, cross1, start1 = lead_of(1, all_part, all_core)
+    (u1,) = kernel(update_kernel, [(rhs // 4, 4 * upd)], start1, cross1, u0, u0_far)
     u1_far = exchange(u1, "leaf", 2)
-    by_x, by_y, by_xy, u1_far = lax.optimization_barrier((by_x, by_y, by_xy, u1_far))
+
+    whole1, _ = lax.optimization_barrier((whole1, u1))
+    own_part, leaf_part = kernel(
+        lower_kernel,
+        [(rhs + 3 * upd, rows), (rhs + upd, rows)],
+        ids, whole1, leaf_all, leaf_ahead, u0, u0_far,
+    )
+    by_x, far, u1_far, own_part = lax.optimization_barrier((by_x, far, u1_far, own_part))
     by_x_core = exchange(by_x, "leaf", 1)
-    by_y_core, by_xy_core = exchange(by_y, "leaf", 1), exchange(by_xy, "leaf", 1)
-    cross2, start2, picks2, columns2 = level_of(2, all_part, all_core, by_x, by_x_core)
-    (u2,) = kernel(update_kernel, [(rhs + 8, 128)], start2, cross2, u1, u1_far)
+    far_core = exchange(far, "leaf", 1)
+    whole2, cross2, start2 = lead_of(2, all_part, all_core, by_x, by_x_core)
+    (u2,) = kernel(
+        update_kernel, [(rhs // 4, 4 * upd)], start2, cross2, u1, u1_far
+    )
     u2_far = exchange(u2, "leaf", 4)
-    by_y, _ = lax.optimization_barrier((by_y, u2))
     (base,) = kernel(
         upper_kernel,
         [(rhs + upd, 2 * rows)],
-        ids, leaf_all, leaf_ahead, top_s, u0, u0_far, u1, u1_far, u2,
-        picks1, picks2, columns1, columns2,
-        all_part, all_core, by_x, by_x_core, by_y, by_y_core, by_xy, by_xy_core,
+        ids, leaf_part, top_s, u1, u1_far, u2, own_part, whole2,
+        all_part, all_core, by_x, by_x_core, far, far_core,
         scratch=[pltpu.VMEM((full, width), jnp.float32)] * 2,
     )
     (out,) = kernel(finish_kernel, [(2, 1, rhs, rows)], base, u2_far)

time: 37.3 us -> 35.8 us (0.960)
  starting transfers between devices: 15.7 us -> 14.4 us
  waiting for transfers between devices: 13.7 us -> 13 us
  Pallas kernels: 7.68 us -> 8.19 us
    ppermute x13 -> x10, starting transfers between devices: 15.7 us -> 12.8 us  [exchange(): lax.ppermute(block, axis, [(src, src ^ mask) for src in range(count)])]
    ppermute x0 -> x1, starting transfers between devices: none -> 1.58 us  [chain(): lax.ppermute(far_part, 'leaf', [(src, src ^ (6 if src % 2 else 4)) for sr...]
    ppermute x13 -> x10, waiting for transfers between devices: 13.7 us -> 13 us  [exchange(): lax.ppermute(block, axis, [(src, src ^ mask) for src in range(count)])]
    pallas_call x9 -> x11, Pallas kernels: 7.68 us -> 8.19 us  [call(): pl.pallas_call(kernel, out_shape=[jax.ShapeDtypeStruct(out, jnp.float32)...]
  transfers between devices with their start and end apart: 13 -> 11, of which waited for: 7 -> 6; matrix products, arithmetic and copies ran while one was open for 0% -> 0% of each run, Pallas kernels for 15% -> 17%
where the time goes in v4:
time: 35.8 us; the launch traced here: 35.7 us
  starting transfers between devices  14.4 us (40%)
  waiting for transfers between devices  13 us (36%)
  Pallas kernels  8.19 us (23%)
    ppermute x10, waiting for transfers between devices, exchange(): lax.ppermute(block, axis, [(src, src ^ mask) for src in range(count)])  13 us
    ppermute x10, starting transfers between devices, exchange(): lax.ppermute(block, axis, [(src, src ^ mask) for src in range(count)])  12.8 us
    pallas_call x11, Pallas kernels, call(): pl.pallas_call(kernel, out_shape=[jax.ShapeDtypeStruct(out, jnp.float32)...  8.19 us
    ppermute x1, starting transfers between devices, chain(): lax.ppermute(far_part, 'leaf', [(src, src ^ (6 if src % 2 else 4)) for sr...  1.58 us
  transfers between devices with their start and end apart: 11, of which 6 were waited for; matrix products, arithmetic and copies ran while one was open for 0% of the time, Pallas kernels for 17%

profile of v4, /device:TPU:0, one launch (start us, length us, event | category | flops | bytes accessed | tf_op | source)
XLA Modules:
  0.0 35.7 jit_solution(14279140223642680335)
XLA Ops:
  0.0 1.2 %shard_map.82 = (f32[128,384]{1,0:T(8,128)S(1)}, s32[16,32]{1,0:T(8,128)S(1)}) custom-call(s32[2,8,32]{2,1,0:T(8,128)} %pattern.1, f32[1,64,64]{2,1,0:T(8,128)} %lr.1, f32[1,64,64]{2,1,0:T(8,128)} %sr.1, f32[1,64,256]{2,1,0:T(8,128)} %li.1, f32[1,64,256]{2,1,0:T(8,128)} %si.1, f32[1,32,64]{2,1,0:T(8,128)} %lu.1, f32[1,32,64]{2,1,0:T(8,128)} %su.1, ...), custom_call_target="tpu_custom_call" | custom-call | flops 1000 | bytes 1000 | tf_op jit(solution)/shard_map/pallas_call | solution.py:45
  1.2 5.1 %collective-permute-start.1 = (f32[128,384]{1,0:T(8,128)S(1)}, f32[128,384]{1,0:T(8,128)S(1)}, u32[]{:S(2)}, u32[]{:S(2)}) collective-permute-start(f32[128,384]{1,0:T(8,128)S(1)} %get-tuple-element.30.refs_0_), channel_id=1, source_target_pairs={{0,3},{1,2},{2,1},{3,0},{4,7},{5,6},{6,5},{7,4},{8,11},{9,10},{10,... | collective-permute-start | bytes 589832 | tf_op jit(solution)/shard_map/ppermute | solution.py:34
  6.3 0.0 collective-permute-start
  6.3 5.8 %collective-permute-done.1.refs_3_ = f32[128,384]{1,0:T(8,128)S(1)} collective-permute-done((f32[128,384]{1,0:T(8,128)S(1)}, f32[128,384]{1,0:T(8,128)S(1)}, u32[]{:S(2)}, u32[]{:S(2)}) %collective-permute-start.1) | collective-permute-done | bytes 196640 | tf_op jit(solution)/shard_map/ppermute | solution.py:34
  12.1 3.1 %collective-permute-start.2 = (f32[128,384]{1,0:T(8,128)S(1)}, f32[128,384]{1,0:T(8,128)S(1)}, u32[]{:S(2)}, u32[]{:S(2)}) collective-permute-start(f32[128,384]{1,0:T(8,128)S(1)} %collective-permute-done.1.refs_3_), channel_id=1, source_target_pairs={{0,1},{1,0},{2,3},{3,2},{4,5},{5,4},{6,7},{7,6},{8,9},{9,8},{10,11... | collective-permute-start | bytes 589832 | tf_op jit(solution)/shard_map/ppermute | solution.py:34
  15.1 0.5 %collective-permute-done.refs_1_ = f32[128,384]{1,0:T(8,128)S(1)} collective-permute-done((f32[128,384]{1,0:T(8,128)S(1)}, f32[128,384]{1,0:T(8,128)S(1)}, u32[]{:S(2)}, u32[]{:S(2)}) %collective-permute-start) | collective-permute-done | bytes 196640 | tf_op jit(solution)/shard_map/ppermute | solution.py:34
  15.6 4.1 %collective-permute-done.2.refs_2_ = f32[128,384]{1,0:T(8,128)S(1)} collective-permute-done((f32[128,384]{1,0:T(8,128)S(1)}, f32[128,384]{1,0:T(8,128)S(1)}, u32[]{:S(2)}, u32[]{:S(2)}) %collective-permute-start.2) | collective-permute-done | bytes 196640 | tf_op jit(solution)/shard_map/ppermute | solution.py:34
  19.7 0.1 shard_map.83
  19.9 0.1 collective-permute-start.3
  20.0 0.5 %shard_map.85 = (f32[256,384]{1,0:T(8,128)S(1)}, f32[96,256]{1,0:T(8,128)S(1)}, f32[16,128]{1,0:T(8,128)S(1)}) custom-call(f32[128,384]{1,0:T(8,128)S(1)} %get-tuple-element.30.refs_0_, f32[128,384]{1,0:T(8,128)S(1)} %collective-permute-done.refs_1_, f32[128,384]{1,0:T(8,128)S(1)} %collective-permute-done.2.refs_2_, ...), custom_call_target="tpu_custom_call" | custom-call | flops 1000 | bytes 1000 | tf_op jit(solution)/shard_map/pallas_call | solution.py:45
  20.4 1.6 %collective-permute-start.5 = (f32[32,1024]{1,0:T(8,128)S(1)}, f32[32,1024]{1,0:T(8,128)S(1)}, u32[]{:S(2)}, u32[]{:S(2)}) collective-permute-start(f32[32,1024]{1,0:T(8,128)S(1)} %get-tuple-element.42), channel_id=1, source_target_pairs={{0,8},{4,12},{8,0},{12,4},{16,24},{20,28},{24,16},{28,20},{1,9},{5... | collective-permute-start | bytes 393224 | tf_op jit(solution)/shard_map/ppermute | solution.py:34
  22.0 0.0 collective-permute-done.3.refs_1_.all_core.refs_6_
  22.0 1.6 %collective-permute-start.6 = (f32[32,1024]{1,0:T(8,128)S(1)}, f32[32,1024]{1,0:T(8,128)S(1)}, u32[]{:S(2)}, u32[]{:S(2)}) collective-permute-start(f32[32,1024]{1,0:T(8,128)S(1)} %shard_map.88), channel_id=1, source_target_pairs={{0,16},{4,28},{8,24},{12,20},{16,0},{20,12},{24,8},{28,4},{1,17},{... | collective-permute-start | bytes 393224 | tf_op jit(solution)/shard_map/ppermute | solution.py:477
  23.6 0.3 collective-permute-start.4
  23.9 0.6 %shard_map.84 = (f32[256,384]{1,0:T(8,128)S(1)}, f32[32,64]{1,0:T(8,128)S(1)}, f32[64,32]{1,0:T(8,128)S(1)}) custom-call(s32[16,32]{1,0:T(8,128)S(1)} %get-tuple-element.29.pattern, f32[64,1024]{1,0:T(8,128)S(1)} %get-tuple-element.31.refs_0_.refs_5_, f32[64,1024]{1,0:T(8,128)S(1)} %collective-permute-done.3.refs_1_.all_core.refs_6_), custom_call_target="tpu_custom_call" | custom-call | flops 1000 | bytes 1000 | tf_op jit(solution)/shard_map/pallas_call | solution.py:45
  24.5 0.3 collective-permute-done.4.other.far
  24.8 0.3 shard_map.86.mine.refs_0_
  25.1 1.1 %collective-permute-start.7 = (f32[16,128]{1,0:T(8,128)S(1)}, f32[16,128]{1,0:T(8,128)S(1)}, u32[]{:S(2)}, u32[]{:S(2)}) collective-permute-start(f32[16,128]{1,0:T(8,128)S(1)} %shard_map.86.mine.refs_0_), channel_id=1, source_target_pairs={{0,8},{4,12},{8,0},{12,4},{16,24},{20,28},{24,16},{28,20},{1,9},{5... | collective-permute-start | bytes 24584 | tf_op jit(solution)/shard_map/ppermute | solution.py:34
  26.2 1.1 %shard_map.87 = (f32[160,64]{1,0:T(8,128)S(1)}, f32[96,64]{1,0:T(8,128)S(1)}) custom-call(s32[16,32]{1,0:T(8,128)S(1)} %get-tuple-element.29.pattern, f32[256,384]{1,0:T(8,128)S(1)} %get-tuple-element.38.whole, f32[256,384]{1,0:T(8,128)S(1)} %get-tuple-element.39.leaf_all, f32[96,256]{1,0:T(8,128)S(1)} %get-tuple-element.40.leaf_ahead, ...), custom_call_target="tpu_custom_call" | custom-call | flops 1000 | bytes 1000 | tf_op jit(solution)/shard_map/pallas_call | solution.py:45
  27.3 0.0 collective-permute-done.5.refs_2_.refs_7_
  27.3 1.4 %collective-permute-done.7.other.refs_1_ = f32[16,128]{1,0:T(8,128)S(1)} collective-permute-done((f32[16,128]{1,0:T(8,128)S(1)}, f32[16,128]{1,0:T(8,128)S(1)}, u32[]{:S(2)}, u32[]{:S(2)}) %collective-permute-start.7) | collective-permute-done | bytes 8224 | tf_op jit(solution)/shard_map/ppermute | solution.py:34
  28.8 0.0 collective-permute-done.6.refs_9_
  28.8 0.0 collective-permute-start.8
  28.8 0.5 %collective-permute-start.9 = (f32[32,1024]{1,0:T(8,128)S(1)}, f32[32,1024]{1,0:T(8,128)S(1)}, u32[]{:S(2)}, u32[]{:S(2)}) collective-permute-start(f32[32,1024]{1,0:T(8,128)S(1)} %collective-permute-done.6.refs_9_), channel_id=1, source_target_pairs={{0,4},{4,0},{8,12},{12,8},{16,20},{20,16},{24,28},{28,24},{1,5},{5... | collective-permute-start | bytes 393224 | tf_op jit(solution)/shard_map/ppermute | solution.py:34
  29.3 0.8 %collective-permute-done.8.refs_3_.refs_8_ = f32[32,1024]{1,0:T(8,128)S(1)} collective-permute-done((f32[32,1024]{1,0:T(8,128)S(1)}, f32[32,1024]{1,0:T(8,128)S(1)}, u32[]{:S(2)}, u32[]{:S(2)}) %collective-permute-start.8) | collective-permute-done | bytes 131104 | tf_op jit(solution)/shard_map/ppermute | solution.py:34
  30.1 0.6 %shard_map.89 = (f32[256,384]{1,0:T(8,128)S(1)}, f32[32,64]{1,0:T(8,128)S(1)}, f32[64,32]{1,0:T(8,128)S(1)}) custom-call(s32[16,32]{1,0:T(8,128)S(1)} %get-tuple-element.29.pattern, f32[64,1024]{1,0:T(8,128)S(1)} %get-tuple-element.31.refs_0_.refs_5_, f32[64,1024]{1,0:T(8,128)S(1)} %collective-permute-done.3.refs_1_.all_core.refs_6_, ...), custom_call_target="tpu_custom_call" | custom-call | flops 1000 | bytes 1000 | tf_op jit(solution)/shard_map/pallas_call | solution.py:45
  30.7 0.4 shard_map.90.refs_2_
  31.1 1.2 %collective-permute-start.10 = (f32[16,128]{1,0:T(8,128)S(1)}, f32[16,128]{1,0:T(8,128)S(1)}, u32[]{:S(2)}, u32[]{:S(2)}) collective-permute-start(f32[16,128]{1,0:T(8,128)S(1)} %shard_map.90.refs_2_), channel_id=1, source_target_pairs={{0,16},{4,20},{8,24},{12,28},{16,0},{20,4},{24,8},{28,12},{1,17},{... | collective-permute-start | bytes 24584 | tf_op jit(solution)/shard_map/ppermute | solution.py:34
  32.3 0.0 collective-permute-done.9.refs_10_
  32.3 2.5 %shard_map.91.base = f32[96,128]{1,0:T(8,128)S(1)} custom-call(s32[16,32]{1,0:T(8,128)S(1)} %get-tuple-element.29.pattern, f32[96,64]{1,0:T(8,128)S(1)} %get-tuple-element.41.leaf_part, f32[64,32]{1,0:T(8,128)S(1)} %get-tuple-element.35.top_s, f32[16,128]{1,0:T(8,128)S(1)} %shard_map.86.mine.refs_0_, f32[16,128]{1,0:T(8,128)S(1)} %collective-permute-done.7.other.refs_1_, ...), custom_call_target="tpu_custom_call" | custom-call | flops 1000 | bytes 1000 | tf_op jit(solution)/shard_map/pallas_call | solution.py:45
  34.8 0.0 collective-permute-done.10.far
  34.8 0.9 %shard_map.92 = f32[2,1,64,64]{3,2,1,0:T(8,128)} custom-call(f32[96,128]{1,0:T(8,128)S(1)} %shard_map.91.base, f32[16,128]{1,0:T(8,128)S(1)} %collective-permute-done.10.far), custom_call_target="tpu_custom_call" | custom-call | flops 1000 | bytes 1000 | tf_op jit(solution)/shard_map/pallas_call | solution.py:45
  (1 shorter events, 0.0 us)
Async XLA Ops:
  1.2 10.9 %collective-permute-start.1 = (f32[128,384]{1,0:T(8,128)S(1)}, f32[128,384]{1,0:T(8,128)S(1)}, u32[]{:S(2)}, u32[]{:S(2)}) collective-permute-start(f32[128,384]{1,0:T(8,128)S(1)} %get-tuple-element.30.refs_0_), channel_id=1, source_target_pairs={{0,3},{1,2},{2,1},{3,0},{4,7},{5,6},{6,5},{7,4},{8,11},{9,10},{10,... | collective-permute-start | bytes 589832 | tf_op jit(solution)/shard_map/ppermute | solution.py:34
  6.3 9.3 %collective-permute-start = (f32[128,384]{1,0:T(8,128)S(1)}, f32[128,384]{1,0:T(8,128)S(1)}, u32[]{:S(2)}, u32[]{:S(2)}) collective-permute-start(f32[128,384]{1,0:T(8,128)S(1)} %get-tuple-element.30.refs_0_), channel_id=1, source_target_pairs={{0,1},{1,0},{2,3},{3,2},{4,5},{5,4},{6,7},{7,6},{8,9},{9,8},{10,11... | collective-permute-start | bytes 589832 | tf_op jit(solution)/shard_map/ppermute | solution.py:34
  12.1 7.7 %collective-permute-start.2 = (f32[128,384]{1,0:T(8,128)S(1)}, f32[128,384]{1,0:T(8,128)S(1)}, u32[]{:S(2)}, u32[]{:S(2)}) collective-permute-start(f32[128,384]{1,0:T(8,128)S(1)} %collective-permute-done.1.refs_3_), channel_id=1, source_target_pairs={{0,1},{1,0},{2,3},{3,2},{4,5},{5,4},{6,7},{7,6},{8,9},{9,8},{10,11... | collective-permute-start | bytes 589832 | tf_op jit(solution)/shard_map/ppermute | solution.py:34
  19.9 2.1 %collective-permute-start.3 = (f32[64,1024]{1,0:T(8,128)S(1)}, f32[64,1024]{1,0:T(8,128)S(1)}, u32[]{:S(2)}, u32[]{:S(2)}) collective-permute-start(f32[64,1024]{1,0:T(8,128)S(1)} %get-tuple-element.31.refs_0_.refs_5_), channel_id=1, source_target_pairs={{0,4},{4,0},{8,12},{12,8},{16,20},{20,16},{24,28},{28,24},{1,5},{5... | collective-permute-start | bytes 786440 | tf_op jit(solution)/shard_map/ppermute | solution.py:34
  20.4 6.9 %collective-permute-start.5 = (f32[32,1024]{1,0:T(8,128)S(1)}, f32[32,1024]{1,0:T(8,128)S(1)}, u32[]{:S(2)}, u32[]{:S(2)}) collective-permute-start(f32[32,1024]{1,0:T(8,128)S(1)} %get-tuple-element.42), channel_id=1, source_target_pairs={{0,8},{4,12},{8,0},{12,4},{16,24},{20,28},{24,16},{28,20},{1,9},{5... | collective-permute-start | bytes 393224 | tf_op jit(solution)/shard_map/ppermute | solution.py:34
  22.0 6.8 %collective-permute-start.6 = (f32[32,1024]{1,0:T(8,128)S(1)}, f32[32,1024]{1,0:T(8,128)S(1)}, u32[]{:S(2)}, u32[]{:S(2)}) collective-permute-start(f32[32,1024]{1,0:T(8,128)S(1)} %shard_map.88), channel_id=1, source_target_pairs={{0,16},{4,28},{8,24},{12,20},{16,0},{20,12},{24,8},{28,4},{1,17},{... | collective-permute-start | bytes 393224 | tf_op jit(solution)/shard_map/ppermute | solution.py:477
  23.6 1.2 %collective-permute-start.4 = (f32[16,128]{1,0:T(8,128)S(1)}, f32[16,128]{1,0:T(8,128)S(1)}, u32[]{:S(2)}, u32[]{:S(2)}) collective-permute-start(f32[16,128]{1,0:T(8,128)S(1)} %get-tuple-element.37.mine.near), channel_id=1, source_target_pairs={{0,4},{4,0},{8,12},{12,8},{16,20},{20,16},{24,28},{28,24},{1,5},{5... | collective-permute-start | bytes 24584 | tf_op jit(solution)/shard_map/ppermute | solution.py:34
  25.1 3.7 %collective-permute-start.7 = (f32[16,128]{1,0:T(8,128)S(1)}, f32[16,128]{1,0:T(8,128)S(1)}, u32[]{:S(2)}, u32[]{:S(2)}) collective-permute-start(f32[16,128]{1,0:T(8,128)S(1)} %shard_map.86.mine.refs_0_), channel_id=1, source_target_pairs={{0,8},{4,12},{8,0},{12,4},{16,24},{20,28},{24,16},{28,20},{1,9},{5... | collective-permute-start | bytes 24584 | tf_op jit(solution)/shard_map/ppermute | solution.py:34
  28.8 1.3 %collective-permute-start.8 = (f32[32,1024]{1,0:T(8,128)S(1)}, f32[32,1024]{1,0:T(8,128)S(1)}, u32[]{:S(2)}, u32[]{:S(2)}) collective-permute-start(f32[32,1024]{1,0:T(8,128)S(1)} %collective-permute-done.5.refs_2_.refs_7_), channel_id=1, source_target_pairs={{0,4},{4,0},{8,12},{12,8},{16,20},{20,16},{24,28},{28,24},{1,5},{5... | collective-permute-start | bytes 393224 | tf_op jit(solution)/shard_map/ppermute | solution.py:34
  28.8 3.5 %collective-permute-start.9 = (f32[32,1024]{1,0:T(8,128)S(1)}, f32[32,1024]{1,0:T(8,128)S(1)}, u32[]{:S(2)}, u32[]{:S(2)}) collective-permute-start(f32[32,1024]{1,0:T(8,128)S(1)} %collective-permute-done.6.refs_9_), channel_id=1, source_target_pairs={{0,4},{4,0},{8,12},{12,8},{16,20},{20,16},{24,28},{28,24},{1,5},{5... | collective-permute-start | bytes 393224 | tf_op jit(solution)/shard_map/ppermute | solution.py:34
  31.1 3.7 %collective-permute-start.10 = (f32[16,128]{1,0:T(8,128)S(1)}, f32[16,128]{1,0:T(8,128)S(1)}, u32[]{:S(2)}, u32[]{:S(2)}) collective-permute-start(f32[16,128]{1,0:T(8,128)S(1)} %shard_map.90.refs_2_), channel_id=1, source_target_pairs={{0,16},{4,20},{8,24},{12,28},{16,0},{20,4},{24,8},{28,12},{1,17},{... | collective-permute-start | bytes 24584 | tf_op jit(solution)/shard_map/ppermute | solution.py:34

commit v5 on v4

--- a/solution.py
+++ b/solution.py
@@ -119,15 +119,25 @@
 
 
 def pack_kernel(plan, pattern, lr, sr, li, si, lu, su, outer, out, ids):
-    full, rhs, upd, rows = plan.full, plan.rhs, plan.upd, plan.rows
+    full, rows, half = plan.full, plan.rows, plan.rhs // 2
+    ids[...] = pattern[...].reshape(ids.shape)
+    out[:rows, :full] = si[0]
+    out[:rows, full:] = jnp.concatenate([sr[0], su[0], outer[:half]], axis=0).T
+    out[rows:, :full] = li[0]
+    out[rows:, full:] = jnp.concatenate([lr[0], lu[0], outer[half:]], axis=0).T
+
+
+def outer_kernel(plan, pattern, *refs):
+    packs, (picked, natural) = refs[: plan.fronts], refs[plan.fronts :]
     front, _ = place()
-    ids[...] = pattern[...].reshape(ids.shape)
-    empty = jnp.zeros((upd, rows), jnp.float32)
-    out[:rows, :full] = si[0]
-    out[:rows, full:] = jnp.concatenate([sr[0], su[0], empty], axis=0).T
-    out[rows:, :full] = li[0]
-    out[rows:, full:] = jnp.concatenate([lr[0], lu[0], empty], axis=0).T
-    out[:rhs, full + rhs + upd :] = nn(outer[...], one_hot(pattern[1, 0:1, :], rows, front * rows))
+    rows, full, edge = plan.rows, plan.full, plan.rhs + plan.upd
+    for slot, pack in enumerate(packs):
+        at = pl.multiple_of((front ^ slot) * rows, rows)
+        natural[pl.ds(at, rows), :128] = pack[:rows, full:]
+        natural[pl.ds(at, rows), 128:] = pack[rows:, full:]
+    turned = natural[...].T
+    outer = jnp.concatenate([turned[edge:128], turned[128 + edge :]], axis=0)
+    picked[...] = nn(outer, one_hot(pattern[plan.groups : plan.groups + 1, :], full))
 
 
 def fold_rows(plan, rows_of):
@@ -167,12 +177,7 @@
 
 def spread_kernel(plan, *refs):
     packs = refs[: plan.fronts]
-    all_part, late_part, high_part, picked, natural = refs[plan.fronts :]
-    edge = plan.full + plan.rhs + plan.upd
-    total = packs[0][: plan.rhs, edge:]
-    for pack in packs[1:]:
-        total = total + pack[: plan.rhs, edge:]
-    picked[...] = total
+    all_part, late_part, high_part, natural = refs[plan.fronts :]
     levels = range(1, plan.depth + 2)
     for at, piece in fold_levels(plan, packs, [0] * 4, levels, natural):
         for out, level in ((all_part, 1), (late_part, 2), (high_part, 3)):
@@ -452,20 +457,19 @@
     beside = exchange(pack, "front", 1)
     beyond = exchange(across, "front", 1)
     wide = 4 * full
-    all_part, late_part, high_part, top_s = kernel(
+    all_part, late_part, high_part = kernel(
         spread_kernel,
         [
             (rows, wide),
             (rows - plan.share[1], wide),
             (plan.share[3] + plan.share[4], wide),
-            (rhs, upd),
         ],
         pack, beside, beyond, across,
         scratch=[pltpu.VMEM((full, width), jnp.float32)],
     )
     all_core = exchange(all_part, "leaf", 1)
     by_x = exchange(late_part, "leaf", 2)
-    leaf_beyond, _ = lax.optimization_barrier((beyond, top_s))
+    leaf_beyond, _ = lax.optimization_barrier((beyond, all_part))
     leaf_all, leaf_ahead, u0 = kernel(
         leaf_kernel,
         [(full, width), (rhs + upd, full), (rhs // 4, 4 * upd)],
@@ -493,7 +497,16 @@
         [(rhs + 3 * upd, rows), (rhs + upd, rows)],
         ids, whole1, leaf_all, leaf_ahead, u0, u0_far,
     )
-    by_x, far, u1_far, own_part = lax.optimization_barrier((by_x, far, u1_far, own_part))
+    spare_beyond, _ = lax.optimization_barrier((beyond, u1))
+    (top_s,) = kernel(
+        outer_kernel,
+        [(rhs, upd)],
+        ids, pack, beside, spare_beyond, across,
+        scratch=[pltpu.VMEM((full, 256), jnp.float32)],
+    )
+    by_x, far, u1_far, own_part, top_s = lax.optimization_barrier(
+        (by_x, far, u1_far, own_part, top_s)
+    )
     by_x_core = exchange(by_x, "leaf", 1)
     far_core = exchange(far, "leaf", 1)
     whole2, cross2, start2 = lead_of(2, all_part, all_core, by_x, by_x_core)

time: 35.8 us -> 35.7 us (level)
    pallas_call x11 -> x12, Pallas kernels: 8.19 us -> 8.34 us  [call(): pl.pallas_call(kernel, out_shape=[jax.ShapeDtypeStruct(out, jnp.float32)...]
  transfers between devices with their start and end apart: 11 -> 11, of which waited for: 6 -> 7; matrix products, arithmetic and copies ran while one was open for 0% -> 0% of each run, Pallas kernels for 17% -> 18%
where the time goes in v5:
time: 35.7 us; the launch traced here: 35.6 us
  starting transfers between devices  14.3 us (40%)
  waiting for transfers between devices  12.8 us (36%)
  Pallas kernels  8.34 us (23%)
    ppermute x10, waiting for transfers between devices, exchange(): lax.ppermute(block, axis, [(src, src ^ mask) for src in range(count)])  12.8 us
    ppermute x10, starting transfers between devices, exchange(): lax.ppermute(block, axis, [(src, src ^ mask) for src in range(count)])  12.7 us
    pallas_call x12, Pallas kernels, call(): pl.pallas_call(kernel, out_shape=[jax.ShapeDtypeStruct(out, jnp.float32)...  8.34 us
    ppermute x1, starting transfers between devices, chain(): lax.ppermute(far_part, 'leaf', [(src, src ^ (6 if src % 2 else 4)) for sr...  1.59 us
  transfers between devices with their start and end apart: 11, of which 7 were waited for; matrix products, arithmetic and copies ran while one was open for 0% of the time, Pallas kernels for 18%

profile of v5, /device:TPU:0, one launch (start us, length us, event | category | flops | bytes accessed | tf_op | source)
XLA Modules:
  0.0 35.6 jit_solution(8040333742622962068)
XLA Ops:
  0.0 1.0 %shard_map.82 = (f32[128,384]{1,0:T(8,128)S(1)}, s32[16,32]{1,0:T(8,128)S(1)}) custom-call(s32[2,8,32]{2,1,0:T(8,128)} %pattern.1, f32[1,64,64]{2,1,0:T(8,128)} %lr.1, f32[1,64,64]{2,1,0:T(8,128)} %sr.1, f32[1,64,256]{2,1,0:T(8,128)} %li.1, f32[1,64,256]{2,1,0:T(8,128)} %si.1, f32[1,32,64]{2,1,0:T(8,128)} %lu.1, f32[1,32,64]{2,1,0:T(8,128)} %su.1, ...), custom_call_target="tpu_custom_call" | custom-call | flops 1000 | bytes 1000 | tf_op jit(solution)/shard_map/pallas_call | solution.py:45
  1.0 5.1 %collective-permute-start.1 = (f32[128,384]{1,0:T(8,128)S(1)}, f32[128,384]{1,0:T(8,128)S(1)}, u32[]{:S(2)}, u32[]{:S(2)}) collective-permute-start(f32[128,384]{1,0:T(8,128)S(1)} %get-tuple-element.31.refs_0_), channel_id=1, source_target_pairs={{0,3},{1,2},{2,1},{3,0},{4,7},{5,6},{6,5},{7,4},{8,11},{9,10},{10,... | collective-permute-start | bytes 589832 | tf_op jit(solution)/shard_map/ppermute | solution.py:34
  6.2 0.0 collective-permute-start
  6.2 5.8 %collective-permute-done.1.refs_3_ = f32[128,384]{1,0:T(8,128)S(1)} collective-permute-done((f32[128,384]{1,0:T(8,128)S(1)}, f32[128,384]{1,0:T(8,128)S(1)}, u32[]{:S(2)}, u32[]{:S(2)}) %collective-permute-start.1) | collective-permute-done | bytes 196640 | tf_op jit(solution)/shard_map/ppermute | solution.py:34
  11.9 3.1 %collective-permute-start.2 = (f32[128,384]{1,0:T(8,128)S(1)}, f32[128,384]{1,0:T(8,128)S(1)}, u32[]{:S(2)}, u32[]{:S(2)}) collective-permute-start(f32[128,384]{1,0:T(8,128)S(1)} %collective-permute-done.1.refs_3_), channel_id=1, source_target_pairs={{0,1},{1,0},{2,3},{3,2},{4,5},{5,4},{6,7},{7,6},{8,9},{9,8},{10,11... | collective-permute-start | bytes 589832 | tf_op jit(solution)/shard_map/ppermute | solution.py:34
  15.0 0.5 %collective-permute-done.refs_1_ = f32[128,384]{1,0:T(8,128)S(1)} collective-permute-done((f32[128,384]{1,0:T(8,128)S(1)}, f32[128,384]{1,0:T(8,128)S(1)}, u32[]{:S(2)}, u32[]{:S(2)}) %collective-permute-start) | collective-permute-done | bytes 196640 | tf_op jit(solution)/shard_map/ppermute | solution.py:34
  15.5 4.1 %collective-permute-done.2.refs_2_ = f32[128,384]{1,0:T(8,128)S(1)} collective-permute-done((f32[128,384]{1,0:T(8,128)S(1)}, f32[128,384]{1,0:T(8,128)S(1)}, u32[]{:S(2)}, u32[]{:S(2)}) %collective-permute-start.2) | collective-permute-done | bytes 196640 | tf_op jit(solution)/shard_map/ppermute | solution.py:34
  19.6 0.1 shard_map.83
  19.7 0.1 collective-permute-start.3
  19.8 1.6 %collective-permute-start.5 = (f32[32,1024]{1,0:T(8,128)S(1)}, f32[32,1024]{1,0:T(8,128)S(1)}, u32[]{:S(2)}, u32[]{:S(2)}) collective-permute-start(f32[32,1024]{1,0:T(8,128)S(1)} %get-tuple-element.42), channel_id=1, source_target_pairs={{0,8},{4,12},{8,0},{12,4},{16,24},{20,28},{24,16},{28,20},{1,9},{5... | collective-permute-start | bytes 393224 | tf_op jit(solution)/shard_map/ppermute | solution.py:34
  21.4 0.5 %shard_map.85 = (f32[256,384]{1,0:T(8,128)S(1)}, f32[96,256]{1,0:T(8,128)S(1)}, f32[16,128]{1,0:T(8,128)S(1)}) custom-call(f32[128,384]{1,0:T(8,128)S(1)} %get-tuple-element.31.refs_0_, f32[128,384]{1,0:T(8,128)S(1)} %collective-permute-done.refs_1_, f32[128,384]{1,0:T(8,128)S(1)} %collective-permute-done.2.refs_2_, ...), custom_call_target="tpu_custom_call" | custom-call | flops 1000 | bytes 1000 | tf_op jit(solution)/shard_map/pallas_call | solution.py:45
  21.8 0.1 collective-permute-done.3.refs_1_.all_core.refs_6_
  21.9 1.6 %collective-permute-start.6 = (f32[32,1024]{1,0:T(8,128)S(1)}, f32[32,1024]{1,0:T(8,128)S(1)}, u32[]{:S(2)}, u32[]{:S(2)}) collective-permute-start(f32[32,1024]{1,0:T(8,128)S(1)} %shard_map.88), channel_id=1, source_target_pairs={{0,16},{4,28},{8,24},{12,20},{16,0},{20,12},{24,8},{28,4},{1,17},{... | collective-permute-start | bytes 393224 | tf_op jit(solution)/shard_map/ppermute | solution.py:481
  23.5 0.2 collective-permute-start.4
  23.7 0.6 %shard_map.84 = (f32[256,384]{1,0:T(8,128)S(1)}, f32[32,64]{1,0:T(8,128)S(1)}, f32[64,32]{1,0:T(8,128)S(1)}) custom-call(s32[16,32]{1,0:T(8,128)S(1)} %get-tuple-element.30.pattern, f32[64,1024]{1,0:T(8,128)S(1)} %get-tuple-element.32.refs_0_.refs_5_, f32[64,1024]{1,0:T(8,128)S(1)} %collective-permute-done.3.refs_1_.all_core.refs_6_), custom_call_target="tpu_custom_call" | custom-call | flops 1000 | bytes 1000 | tf_op jit(solution)/shard_map/pallas_call | solution.py:45
  24.3 0.4 %collective-permute-done.4.other.far = f32[16,128]{1,0:T(8,128)S(1)} collective-permute-done((f32[16,128]{1,0:T(8,128)S(1)}, f32[16,128]{1,0:T(8,128)S(1)}, u32[]{:S(2)}, u32[]{:S(2)}) %collective-permute-start.4) | collective-permute-done | bytes 8224 | tf_op jit(solution)/shard_map/ppermute | solution.py:34
  24.7 0.3 shard_map.86.mine.refs_0_
  25.0 1.0 %collective-permute-start.7 = (f32[16,128]{1,0:T(8,128)S(1)}, f32[16,128]{1,0:T(8,128)S(1)}, u32[]{:S(2)}, u32[]{:S(2)}) collective-permute-start(f32[16,128]{1,0:T(8,128)S(1)} %shard_map.86.mine.refs_0_), channel_id=1, source_target_pairs={{0,8},{4,12},{8,0},{12,4},{16,24},{20,28},{24,16},{28,20},{1,9},{5... | collective-permute-start | bytes 24584 | tf_op jit(solution)/shard_map/ppermute | solution.py:34
  26.0 0.3 shard_map.89.top_s
  26.3 1.2 %shard_map.87 = (f32[160,64]{1,0:T(8,128)S(1)}, f32[96,64]{1,0:T(8,128)S(1)}) custom-call(s32[16,32]{1,0:T(8,128)S(1)} %get-tuple-element.30.pattern, f32[256,384]{1,0:T(8,128)S(1)} %get-tuple-element.38.whole, f32[256,384]{1,0:T(8,128)S(1)} %get-tuple-element.39.leaf_all, f32[96,256]{1,0:T(8,128)S(1)} %get-tuple-element.40.leaf_ahead, ...), custom_call_target="tpu_custom_call" | custom-call | flops 1000 | bytes 1000 | tf_op jit(solution)/shard_map/pallas_call | solution.py:45
  27.5 0.0 collective-permute-done.5.refs_2_.refs_7_
  27.5 1.2 %collective-permute-done.7.other.refs_1_ = f32[16,128]{1,0:T(8,128)S(1)} collective-permute-done((f32[16,128]{1,0:T(8,128)S(1)}, f32[16,128]{1,0:T(8,128)S(1)}, u32[]{:S(2)}, u32[]{:S(2)}) %collective-permute-start.7) | collective-permute-done | bytes 8224 | tf_op jit(solution)/shard_map/ppermute | solution.py:34
  28.7 0.0 collective-permute-done.6.refs_9_
  28.7 0.0 collective-permute-start.8
  28.7 0.5 %collective-permute-start.9 = (f32[32,1024]{1,0:T(8,128)S(1)}, f32[32,1024]{1,0:T(8,128)S(1)}, u32[]{:S(2)}, u32[]{:S(2)}) collective-permute-start(f32[32,1024]{1,0:T(8,128)S(1)} %collective-permute-done.6.refs_9_), channel_id=1, source_target_pairs={{0,4},{4,0},{8,12},{12,8},{16,20},{20,16},{24,28},{28,24},{1,5},{5... | collective-permute-start | bytes 393224 | tf_op jit(solution)/shard_map/ppermute | solution.py:34
  29.2 0.8 %collective-permute-done.8.refs_3_.refs_8_ = f32[32,1024]{1,0:T(8,128)S(1)} collective-permute-done((f32[32,1024]{1,0:T(8,128)S(1)}, f32[32,1024]{1,0:T(8,128)S(1)}, u32[]{:S(2)}, u32[]{:S(2)}) %collective-permute-start.8) | collective-permute-done | bytes 131104 | tf_op jit(solution)/shard_map/ppermute | solution.py:34
  30.0 0.6 %shard_map.90 = (f32[256,384]{1,0:T(8,128)S(1)}, f32[32,64]{1,0:T(8,128)S(1)}, f32[64,32]{1,0:T(8,128)S(1)}) custom-call(s32[16,32]{1,0:T(8,128)S(1)} %get-tuple-element.30.pattern, f32[64,1024]{1,0:T(8,128)S(1)} %get-tuple-element.32.refs_0_.refs_5_, f32[64,1024]{1,0:T(8,128)S(1)} %collective-permute-done.3.refs_1_.all_core.refs_6_, ...), custom_call_target="tpu_custom_call" | custom-call | flops 1000 | bytes 1000 | tf_op jit(solution)/shard_map/pallas_call | solution.py:45
  30.6 0.4 shard_map.91.refs_2_
  31.0 1.2 %collective-permute-start.10 = (f32[16,128]{1,0:T(8,128)S(1)}, f32[16,128]{1,0:T(8,128)S(1)}, u32[]{:S(2)}, u32[]{:S(2)}) collective-permute-start(f32[16,128]{1,0:T(8,128)S(1)} %shard_map.91.refs_2_), channel_id=1, source_target_pairs={{0,16},{4,20},{8,24},{12,28},{16,0},{20,4},{24,8},{28,12},{1,17},{... | collective-permute-start | bytes 24584 | tf_op jit(solution)/shard_map/ppermute | solution.py:34
  32.2 0.0 collective-permute-done.9.refs_10_
  32.2 2.5 %shard_map.92.base = f32[96,128]{1,0:T(8,128)S(1)} custom-call(s32[16,32]{1,0:T(8,128)S(1)} %get-tuple-element.30.pattern, f32[96,64]{1,0:T(8,128)S(1)} %get-tuple-element.41.leaf_part, f32[64,32]{1,0:T(8,128)S(1)} %shard_map.89.top_s, f32[16,128]{1,0:T(8,128)S(1)} %shard_map.86.mine.refs_0_, f32[16,128]{1,0:T(8,128)S(1)} %collective-permute-done.7.other.refs_1_, ...), custom_call_target="tpu_custom_call" | custom-call | flops 1000 | bytes 1000 | tf_op jit(solution)/shard_map/pallas_call | solution.py:45
  34.7 0.0 collective-permute-done.10.far
  34.7 0.9 %shard_map.93 = f32[2,1,64,64]{3,2,1,0:T(8,128)} custom-call(f32[96,128]{1,0:T(8,128)S(1)} %shard_map.92.base, f32[16,128]{1,0:T(8,128)S(1)} %collective-permute-done.10.far), custom_call_target="tpu_custom_call" | custom-call | flops 1000 | bytes 1000 | tf_op jit(solution)/shard_map/pallas_call | solution.py:45
  (1 shorter events, 0.0 us)
Async XLA Ops:
  1.0 10.9 %collective-permute-start.1 = (f32[128,384]{1,0:T(8,128)S(1)}, f32[128,384]{1,0:T(8,128)S(1)}, u32[]{:S(2)}, u32[]{:S(2)}) collective-permute-start(f32[128,384]{1,0:T(8,128)S(1)} %get-tuple-element.31.refs_0_), channel_id=1, source_target_pairs={{0,3},{1,2},{2,1},{3,0},{4,7},{5,6},{6,5},{7,4},{8,11},{9,10},{10,... | collective-permute-start | bytes 589832 | tf_op jit(solution)/shard_map/ppermute | solution.py:34
  6.2 9.3 %collective-permute-start = (f32[128,384]{1,0:T(8,128)S(1)}, f32[128,384]{1,0:T(8,128)S(1)}, u32[]{:S(2)}, u32[]{:S(2)}) collective-permute-start(f32[128,384]{1,0:T(8,128)S(1)} %get-tuple-element.31.refs_0_), channel_id=1, source_target_pairs={{0,1},{1,0},{2,3},{3,2},{4,5},{5,4},{6,7},{7,6},{8,9},{9,8},{10,11... | collective-permute-start | bytes 589832 | tf_op jit(solution)/shard_map/ppermute | solution.py:34
  11.9 7.7 %collective-permute-start.2 = (f32[128,384]{1,0:T(8,128)S(1)}, f32[128,384]{1,0:T(8,128)S(1)}, u32[]{:S(2)}, u32[]{:S(2)}) collective-permute-start(f32[128,384]{1,0:T(8,128)S(1)} %collective-permute-done.1.refs_3_), channel_id=1, source_target_pairs={{0,1},{1,0},{2,3},{3,2},{4,5},{5,4},{6,7},{7,6},{8,9},{9,8},{10,11... | collective-permute-start | bytes 589832 | tf_op jit(solution)/shard_map/ppermute | solution.py:34
  19.7 2.2 %collective-permute-start.3 = (f32[64,1024]{1,0:T(8,128)S(1)}, f32[64,1024]{1,0:T(8,128)S(1)}, u32[]{:S(2)}, u32[]{:S(2)}) collective-permute-start(f32[64,1024]{1,0:T(8,128)S(1)} %get-tuple-element.32.refs_0_.refs_5_), channel_id=1, source_target_pairs={{0,4},{4,0},{8,12},{12,8},{16,20},{20,16},{24,28},{28,24},{1,5},{5... | collective-permute-start | bytes 786440 | tf_op jit(solution)/shard_map/ppermute | solution.py:34
  19.8 7.7 %collective-permute-start.5 = (f32[32,1024]{1,0:T(8,128)S(1)}, f32[32,1024]{1,0:T(8,128)S(1)}, u32[]{:S(2)}, u32[]{:S(2)}) collective-permute-start(f32[32,1024]{1,0:T(8,128)S(1)} %get-tuple-element.42), channel_id=1, source_target_pairs={{0,8},{4,12},{8,0},{12,4},{16,24},{20,28},{24,16},{28,20},{1,9},{5... | collective-permute-start | bytes 393224 | tf_op jit(solution)/shard_map/ppermute | solution.py:34
  21.9 6.8 %collective-permute-start.6 = (f32[32,1024]{1,0:T(8,128)S(1)}, f32[32,1024]{1,0:T(8,128)S(1)}, u32[]{:S(2)}, u32[]{:S(2)}) collective-permute-start(f32[32,1024]{1,0:T(8,128)S(1)} %shard_map.88), channel_id=1, source_target_pairs={{0,16},{4,28},{8,24},{12,20},{16,0},{20,12},{24,8},{28,4},{1,17},{... | collective-permute-start | bytes 393224 | tf_op jit(solution)/shard_map/ppermute | solution.py:481
  23.5 1.2 %collective-permute-start.4 = (f32[16,128]{1,0:T(8,128)S(1)}, f32[16,128]{1,0:T(8,128)S(1)}, u32[]{:S(2)}, u32[]{:S(2)}) collective-permute-start(f32[16,128]{1,0:T(8,128)S(1)} %get-tuple-element.37.mine.near), channel_id=1, source_target_pairs={{0,4},{4,0},{8,12},{12,8},{16,20},{20,16},{24,28},{28,24},{1,5},{5... | collective-permute-start | bytes 24584 | tf_op jit(solution)/shard_map/ppermute | solution.py:34
  25.0 3.7 %collective-permute-start.7 = (f32[16,128]{1,0:T(8,128)S(1)}, f32[16,128]{1,0:T(8,128)S(1)}, u32[]{:S(2)}, u32[]{:S(2)}) collective-permute-start(f32[16,128]{1,0:T(8,128)S(1)} %shard_map.86.mine.refs_0_), channel_id=1, source_target_pairs={{0,8},{4,12},{8,0},{12,4},{16,24},{20,28},{24,16},{28,20},{1,9},{5... | collective-permute-start | bytes 24584 | tf_op jit(solution)/shard_map/ppermute | solution.py:34
  28.7 1.3 %collective-permute-start.8 = (f32[32,1024]{1,0:T(8,128)S(1)}, f32[32,1024]{1,0:T(8,128)S(1)}, u32[]{:S(2)}, u32[]{:S(2)}) collective-permute-start(f32[32,1024]{1,0:T(8,128)S(1)} %collective-permute-done.5.refs_2_.refs_7_), channel_id=1, source_target_pairs={{0,4},{4,0},{8,12},{12,8},{16,20},{20,16},{24,28},{28,24},{1,5},{5... | collective-permute-start | bytes 393224 | tf_op jit(solution)/shard_map/ppermute | solution.py:34
  28.7 3.5 %collective-permute-start.9 = (f32[32,1024]{1,0:T(8,128)S(1)}, f32[32,1024]{1,0:T(8,128)S(1)}, u32[]{:S(2)}, u32[]{:S(2)}) collective-permute-start(f32[32,1024]{1,0:T(8,128)S(1)} %collective-permute-done.6.refs_9_), channel_id=1, source_target_pairs={{0,4},{4,0},{8,12},{12,8},{16,20},{20,16},{24,28},{28,24},{1,5},{5... | collective-permute-start | bytes 393224 | tf_op jit(solution)/shard_map/ppermute | solution.py:34
  31.0 3.7 %collective-permute-start.10 = (f32[16,128]{1,0:T(8,128)S(1)}, f32[16,128]{1,0:T(8,128)S(1)}, u32[]{:S(2)}, u32[]{:S(2)}) collective-permute-start(f32[16,128]{1,0:T(8,128)S(1)} %shard_map.91.refs_2_), channel_id=1, source_target_pairs={{0,16},{4,20},{8,24},{12,28},{16,0},{20,4},{24,8},{28,12},{1,17},{... | collective-permute-start | bytes 24584 | tf_op jit(solution)/shard_map/ppermute | solution.py:34

commit v6 on v5

--- a/solution.py
+++ b/solution.py
@@ -118,13 +118,44 @@
     return lax.axis_index("front"), lax.axis_index("leaf")
 
 
-def pack_kernel(plan, pattern, lr, sr, li, si, lu, su, outer, out, ids):
-    full, rows, half = plan.full, plan.rows, plan.rhs // 2
+def pack_kernel(plan, pattern, lr, sr, li, si, lu, su, outer, out, main, ids):
+    cut, full, rows, half = plan.full // 2, plan.full, plan.rows, plan.rhs // 2
     ids[...] = pattern[...].reshape(ids.shape)
-    out[:rows, :full] = si[0]
-    out[:rows, full:] = jnp.concatenate([sr[0], su[0], outer[:half]], axis=0).T
-    out[rows:, :full] = li[0]
-    out[rows:, full:] = jnp.concatenate([lr[0], lu[0], outer[half:]], axis=0).T
+    for low, inverse, pieces in (
+        (0, si, (sr[0], su[0], outer[:half])),
+        (rows, li, (lr[0], lu[0], outer[half:])),
+    ):
+        side = jnp.concatenate(pieces, axis=0).T
+        out[low : low + rows, :cut] = inverse[0, :, :cut]
+        out[low : low + rows, cut:full] = side
+        out[low : low + rows, full:] = inverse[0, :, cut:]
+        main[low : low + rows, :cut] = inverse[0, :, :cut]
+        main[low : low + rows, cut:] = side
+
+
+def onward_kernel(plan, pack, across, main, right):
+    full = plan.full
+    main[...] = across[:, :full]
+    right[...] = jnp.where(place()[0] < plan.fronts // 2, across[:, full:], pack[:, full:])
+
+
+def whole_rows(plan, packs, low, whole):
+    front, _ = place()
+    cut, full, rows = plan.full // 2, plan.full, plan.rows
+    pack, _, _, across, second = packs
+    rest = second[low : low + rows, :]
+    lower = front < plan.fronts // 2
+    rights = (
+        pack[low : low + rows, full:],
+        jnp.where(lower, 0.0, rest),
+        jnp.where(lower, rest, 0.0),
+        across[low : low + rows, full:],
+    )
+    for slot in range(plan.fronts):
+        at = pl.multiple_of((front ^ slot) * rows, rows)
+        whole[pl.ds(at, rows), :cut] = packs[slot][low : low + rows, :cut]
+        whole[pl.ds(at, rows), cut:full] = rights[slot]
+        whole[pl.ds(at, rows), full:] = packs[slot][low : low + rows, cut:full]
 
 
 def outer_kernel(plan, pattern, *refs):
@@ -133,8 +164,8 @@
     rows, full, edge = plan.rows, plan.full, plan.rhs + plan.upd
     for slot, pack in enumerate(packs):
         at = pl.multiple_of((front ^ slot) * rows, rows)
-        natural[pl.ds(at, rows), :128] = pack[:rows, full:]
-        natural[pl.ds(at, rows), 128:] = pack[rows:, full:]
+        natural[pl.ds(at, rows), :128] = pack[:rows, full // 2 : full]
+        natural[pl.ds(at, rows), 128:] = pack[rows:, full // 2 : full]
     turned = natural[...].T
     outer = jnp.concatenate([turned[edge:128], turned[128 + edge :]], axis=0)
     picked[...] = nn(outer, one_hot(pattern[plan.groups : plan.groups + 1, :], full))
@@ -162,24 +193,20 @@
         yield front, jnp.concatenate(pieces, axis=1)
 
 
-def fold_levels(plan, packs, low, levels, natural):
-    front, _ = place()
-    count, base = natural.shape[0] // plan.fronts, plan.offset[levels[0]]
-    for slot, pack in enumerate(packs):
-        at = pl.multiple_of((front ^ slot) * count, count)
-        natural[pl.ds(at, count), :] = pack[low[slot] : low[slot] + count, :]
-    for level in levels:
-        offset, share = plan.offset[level] - base, plan.share[level]
+def fold_levels(plan, packs, natural):
+    whole_rows(plan, packs, 0, natural)
+    rows = plan.rows
+    for level in range(1, plan.depth + 2):
+        offset, share = plan.offset[level], plan.share[level]
         yield offset, fold_rows(
-            plan, lambda pos: natural[pos * count + offset : pos * count + offset + share, :]
+            plan, lambda pos: natural[pos * rows + offset : pos * rows + offset + share, :]
         )
 
 
 def spread_kernel(plan, *refs):
-    packs = refs[: plan.fronts]
-    all_part, late_part, high_part, natural = refs[plan.fronts :]
-    levels = range(1, plan.depth + 2)
-    for at, piece in fold_levels(plan, packs, [0] * 4, levels, natural):
+    packs = refs[: plan.fronts + 1]
+    all_part, late_part, high_part, natural = refs[plan.fronts + 1 :]
+    for at, piece in fold_levels(plan, packs, natural):
         for out, level in ((all_part, 1), (late_part, 2), (high_part, 3)):
             low = at - plan.offset[level]
             if low >= 0:
@@ -193,14 +220,9 @@
 
 
 def leaf_kernel(plan, *refs):
-    count = plan.fronts
-    packs, (whole, ahead, update) = refs[:count], refs[count:]
-    front, _ = place()
-    rhs, upd, full, rows = plan.rhs, plan.upd, plan.full, plan.rows
-    low = rows
-    for slot in range(count):
-        at = pl.multiple_of((front ^ slot) * rows, rows)
-        whole[pl.ds(at, rows), :] = packs[slot][low : low + rows, :]
+    packs, (whole, ahead, update) = refs[: plan.fronts + 1], refs[plan.fronts + 1 :]
+    rhs, upd, full = plan.rhs, plan.upd, plan.full
+    whole_rows(plan, packs, plan.rows, whole)
     flipped = whole[:, full:].T
     solved = nt(flipped[:rhs], whole[:, :full])
     ahead[:rhs, :] = solved
@@ -447,15 +469,23 @@
     def kernel(body, outs, *args, extra=(), **kw):
         return call(functools.partial(body, plan, *extra), outs, args, **kw)
 
-    pack, ids = kernel(
+    pack, main, ids = kernel(
         pack_kernel,
-        [(2 * rows, width), ((pattern.shape[0] * pattern.shape[1], upd), jnp.int32)],
+        [
+            (2 * rows, width),
+            (2 * rows, full),
+            ((pattern.shape[0] * pattern.shape[1], upd), jnp.int32),
+        ],
         pattern, leaf_rhs, sep_rhs, leaf_inverse, sep_inverse, leaf_block, sep_block, outer,
         chip=False,
     )
     across = exchange(pack, "front", 3)
-    beside = exchange(pack, "front", 1)
-    beyond = exchange(across, "front", 1)
+    beside = exchange(main, "front", 1)
+    onward, onward_second = kernel(
+        onward_kernel, [(2 * rows, full), (2 * rows, full // 2)], pack, across
+    )
+    beyond = exchange(onward, "front", 1)
+    second = exchange(onward_second, "front", 1)
     wide = 4 * full
     all_part, late_part, high_part = kernel(
         spread_kernel,
@@ -464,7 +494,7 @@
             (rows - plan.share[1], wide),
             (plan.share[3] + plan.share[4], wide),
         ],
-        pack, beside, beyond, across,
+        pack, beside, beyond, across, second,
         scratch=[pltpu.VMEM((full, width), jnp.float32)],
     )
     all_core = exchange(all_part, "leaf", 1)
@@ -473,7 +503,7 @@
     leaf_all, leaf_ahead, u0 = kernel(
         leaf_kernel,
         [(full, width), (rhs + upd, full), (rhs // 4, 4 * upd)],
-        pack, beside, leaf_beyond, across,
+        pack, beside, leaf_beyond, across, second,
     )
     u0_far = exchange(u0, "leaf", 1)
     high_part, _ = lax.optimization_barrier((high_part, u0))

time: 35.7 us -> 35.4 us (level)
  waiting for transfers between devices: 12.8 us -> 12.3 us
    ppermute x10 -> x11, waiting for transfers between devices: 12.8 us -> 12.3 us  [exchange(): lax.ppermute(block, axis, [(src, src ^ mask) for src in range(count)])]
    ppermute x10 -> x11, starting transfers between devices: 12.7 us -> 13 us  [exchange(): lax.ppermute(block, axis, [(src, src ^ mask) for src in range(count)])]
    pallas_call x12 -> x13, Pallas kernels: 8.34 us -> 8.36 us  [call(): pl.pallas_call(kernel, out_shape=[jax.ShapeDtypeStruct(out, jnp.float32)...]
  transfers between devices with their start and end apart: 11 -> 12, of which waited for: 7 -> 5; matrix products, arithmetic and copies ran while one was open for 0% -> 0% of each run, Pallas kernels for 18% -> 18%
where the time goes in v6:
time: 35.4 us; the launch traced here: 35.3 us
  starting transfers between devices  14.6 us (41%)
  waiting for transfers between devices  12.3 us (35%)
  Pallas kernels  8.36 us (24%)
    ppermute x11, starting transfers between devices, exchange(): lax.ppermute(block, axis, [(src, src ^ mask) for src in range(count)])  13 us
    ppermute x11, waiting for transfers between devices, exchange(): lax.ppermute(block, axis, [(src, src ^ mask) for src in range(count)])  12.3 us
    pallas_call x13, Pallas kernels, call(): pl.pallas_call(kernel, out_shape=[jax.ShapeDtypeStruct(out, jnp.float32)...  8.36 us
    ppermute x1, starting transfers between devices, chain(): lax.ppermute(far_part, 'leaf', [(src, src ^ (6 if src % 2 else 4)) for sr...  1.58 us
  transfers between devices with their start and end apart: 12, of which 5 were waited for; matrix products, arithmetic and copies ran while one was open for 0% of the time, Pallas kernels for 18%

profile of v6, /device:TPU:0, one launch (start us, length us, event | category | flops | bytes accessed | tf_op | source)
XLA Modules:
  0.0 35.3 jit_solution(14596470816150522713)
XLA Ops:
  0.0 1.0 %shard_map.82 = (f32[128,384]{1,0:T(8,128)S(1)}, f32[128,256]{1,0:T(8,128)S(1)}, s32[16,32]{1,0:T(8,128)S(1)}) custom-call(s32[2,8,32]{2,1,0:T(8,128)} %pattern.1, f32[1,64,64]{2,1,0:T(8,128)} %lr.1, f32[1,64,64]{2,1,0:T(8,128)} %sr.1, f32[1,64,256]{2,1,0:T(8,128)} %li.1, f32[1,64,256]{2,1,0:T(8,128)} %si.1, f32[1,32,64]{2,1,0:T(8,128)} %lu.1, ...), custom_call_target="tpu_custom_call" | custom-call | flops 1000 | bytes 1000 | tf_op jit(solution)/shard_map/pallas_call | solution.py:45
  1.0 5.1 %collective-permute-start.1 = (f32[128,384]{1,0:T(8,128)S(1)}, f32[128,384]{1,0:T(8,128)S(1)}, u32[]{:S(2)}, u32[]{:S(2)}) collective-permute-start(f32[128,384]{1,0:T(8,128)S(1)} %get-tuple-element.34.pack.refs_0_), channel_id=1, source_target_pairs={{0,3},{1,2},{2,1},{3,0},{4,7},{5,6},{6,5},{7,4},{8,11},{9,10},{10,... | collective-permute-start | bytes 589832 | tf_op jit(solution)/shard_map/ppermute | solution.py:34
  6.2 0.0 collective-permute-start
  6.2 5.8 %collective-permute-done.1.across.refs_3_ = f32[128,384]{1,0:T(8,128)S(1)} collective-permute-done((f32[128,384]{1,0:T(8,128)S(1)}, f32[128,384]{1,0:T(8,128)S(1)}, u32[]{:S(2)}, u32[]{:S(2)}) %collective-permute-start.1) | collective-permute-done | bytes 196640 | tf_op jit(solution)/shard_map/ppermute | solution.py:34
  12.0 3.1 %collective-permute-start.2 = (f32[128,256]{1,0:T(8,128)S(1)}, f32[128,256]{1,0:T(8,128)S(1)}, u32[]{:S(2)}, u32[]{:S(2)}) collective-permute-start(f32[128,256]{1,0:T(8,128)S(1)} %get-tuple-element.36), channel_id=1, source_target_pairs={{0,1},{1,0},{2,3},{3,2},{4,5},{5,4},{6,7},{7,6},{8,9},{9,8},{10,11... | collective-permute-start | bytes 393224 | tf_op jit(solution)/shard_map/ppermute | solution.py:34
  15.1 0.1 collective-permute-start.3
  15.1 0.0 collective-permute-done.refs_1_
  15.2 4.2 %collective-permute-done.3.refs_4_ = f32[128,128]{1,0:T(8,128)S(1)} collective-permute-done((f32[128,128]{1,0:T(8,128)S(1)}, f32[128,128]{1,0:T(8,128)S(1)}, u32[]{:S(2)}, u32[]{:S(2)}) %collective-permute-start.3) | collective-permute-done | bytes 65568 | tf_op jit(solution)/shard_map/ppermute | solution.py:34
  19.3 0.0 collective-permute-done.2.refs_2_
  19.3 0.1 shard_map.84
  19.5 0.1 collective-permute-start.4
  19.6 0.5 %shard_map.86 = (f32[256,384]{1,0:T(8,128)S(1)}, f32[96,256]{1,0:T(8,128)S(1)}, f32[16,128]{1,0:T(8,128)S(1)}) custom-call(f32[128,384]{1,0:T(8,128)S(1)} %get-tuple-element.34.pack.refs_0_, f32[128,256]{1,0:T(8,128)S(1)} %collective-permute-done.refs_1_, f32[128,256]{1,0:T(8,128)S(1)} %collective-permute-done.2.refs_2_, ...), custom_call_target="tpu_custom_call" | custom-call | flops 1000 | bytes 1000 | tf_op jit(solution)/shard_map/pallas_call | solution.py:45
  20.1 1.6 %collective-permute-start.6 = (f32[32,1024]{1,0:T(8,128)S(1)}, f32[32,1024]{1,0:T(8,128)S(1)}, u32[]{:S(2)}, u32[]{:S(2)}) collective-permute-start(f32[32,1024]{1,0:T(8,128)S(1)} %get-tuple-element.48), channel_id=1, source_target_pairs={{0,8},{4,12},{8,0},{12,4},{16,24},{20,28},{24,16},{28,20},{1,9},{5... | collective-permute-start | bytes 393224 | tf_op jit(solution)/shard_map/ppermute | solution.py:34
  21.6 0.0 collective-permute-done.4.refs_1_.all_core.refs_6_
  21.6 1.6 %collective-permute-start.7 = (f32[32,1024]{1,0:T(8,128)S(1)}, f32[32,1024]{1,0:T(8,128)S(1)}, u32[]{:S(2)}, u32[]{:S(2)}) collective-permute-start(f32[32,1024]{1,0:T(8,128)S(1)} %shard_map.89), channel_id=1, source_target_pairs={{0,16},{4,28},{8,24},{12,20},{16,0},{20,12},{24,8},{28,4},{1,17},{... | collective-permute-start | bytes 393224 | tf_op jit(solution)/shard_map/ppermute | solution.py:511
  23.2 0.3 collective-permute-start.5
  23.5 0.6 %shard_map.85 = (f32[256,384]{1,0:T(8,128)S(1)}, f32[32,64]{1,0:T(8,128)S(1)}, f32[64,32]{1,0:T(8,128)S(1)}) custom-call(s32[16,32]{1,0:T(8,128)S(1)} %get-tuple-element.33.pattern, f32[64,1024]{1,0:T(8,128)S(1)} %get-tuple-element.38.refs_0_.refs_5_, f32[64,1024]{1,0:T(8,128)S(1)} %collective-permute-done.4.refs_1_.all_core.refs_6_), custom_call_target="tpu_custom_call" | custom-call | flops 1000 | bytes 1000 | tf_op jit(solution)/shard_map/pallas_call | solution.py:45
  24.1 0.3 collective-permute-done.5.other.far
  24.4 0.3 shard_map.87.mine.refs_0_
  24.7 1.1 %collective-permute-start.8 = (f32[16,128]{1,0:T(8,128)S(1)}, f32[16,128]{1,0:T(8,128)S(1)}, u32[]{:S(2)}, u32[]{:S(2)}) collective-permute-start(f32[16,128]{1,0:T(8,128)S(1)} %shard_map.87.mine.refs_0_), channel_id=1, source_target_pairs={{0,8},{4,12},{8,0},{12,4},{16,24},{20,28},{24,16},{28,20},{1,9},{5... | collective-permute-start | bytes 24584 | tf_op jit(solution)/shard_map/ppermute | solution.py:34
  25.8 0.3 shard_map.90.top_s
  26.1 1.2 %shard_map.88 = (f32[160,64]{1,0:T(8,128)S(1)}, f32[96,64]{1,0:T(8,128)S(1)}) custom-call(s32[16,32]{1,0:T(8,128)S(1)} %get-tuple-element.33.pattern, f32[256,384]{1,0:T(8,128)S(1)} %get-tuple-element.44.whole, f32[256,384]{1,0:T(8,128)S(1)} %get-tuple-element.45.leaf_all, f32[96,256]{1,0:T(8,128)S(1)} %get-tuple-element.46.leaf_ahead, ...), custom_call_target="tpu_custom_call" | custom-call | flops 1000 | bytes 1000 | tf_op jit(solution)/shard_map/pallas_call | solution.py:45
  27.3 0.0 collective-permute-done.6.refs_2_.refs_7_
  27.3 1.1 %collective-permute-done.8.other.refs_1_ = f32[16,128]{1,0:T(8,128)S(1)} collective-permute-done((f32[16,128]{1,0:T(8,128)S(1)}, f32[16,128]{1,0:T(8,128)S(1)}, u32[]{:S(2)}, u32[]{:S(2)}) %collective-permute-start.8) | collective-permute-done | bytes 8224 | tf_op jit(solution)/shard_map/ppermute | solution.py:34
  28.4 0.0 collective-permute-done.7.refs_9_
  28.4 0.0 collective-permute-start.9
  28.4 0.5 %collective-permute-start.10 = (f32[32,1024]{1,0:T(8,128)S(1)}, f32[32,1024]{1,0:T(8,128)S(1)}, u32[]{:S(2)}, u32[]{:S(2)}) collective-permute-start(f32[32,1024]{1,0:T(8,128)S(1)} %collective-permute-done.7.refs_9_), channel_id=1, source_target_pairs={{0,4},{4,0},{8,12},{12,8},{16,20},{20,16},{24,28},{28,24},{1,5},{5... | collective-permute-start | bytes 393224 | tf_op jit(solution)/shard_map/ppermute | solution.py:34
  28.9 0.8 %collective-permute-done.9.refs_3_.refs_8_ = f32[32,1024]{1,0:T(8,128)S(1)} collective-permute-done((f32[32,1024]{1,0:T(8,128)S(1)}, f32[32,1024]{1,0:T(8,128)S(1)}, u32[]{:S(2)}, u32[]{:S(2)}) %collective-permute-start.9) | collective-permute-done | bytes 131104 | tf_op jit(solution)/shard_map/ppermute | solution.py:34
  29.7 0.6 %shard_map.91 = (f32[256,384]{1,0:T(8,128)S(1)}, f32[32,64]{1,0:T(8,128)S(1)}, f32[64,32]{1,0:T(8,128)S(1)}) custom-call(s32[16,32]{1,0:T(8,128)S(1)} %get-tuple-element.33.pattern, f32[64,1024]{1,0:T(8,128)S(1)} %get-tuple-element.38.refs_0_.refs_5_, f32[64,1024]{1,0:T(8,128)S(1)} %collective-permute-done.4.refs_1_.all_core.refs_6_, ...), custom_call_target="tpu_custom_call" | custom-call | flops 1000 | bytes 1000 | tf_op jit(solution)/shard_map/pallas_call | solution.py:45
  30.3 0.4 shard_map.92.refs_2_
  30.7 1.2 %collective-permute-start.11 = (f32[16,128]{1,0:T(8,128)S(1)}, f32[16,128]{1,0:T(8,128)S(1)}, u32[]{:S(2)}, u32[]{:S(2)}) collective-permute-start(f32[16,128]{1,0:T(8,128)S(1)} %shard_map.92.refs_2_), channel_id=1, source_target_pairs={{0,16},{4,20},{8,24},{12,28},{16,0},{20,4},{24,8},{28,12},{1,17},{... | collective-permute-start | bytes 24584 | tf_op jit(solution)/shard_map/ppermute | solution.py:34
  31.9 0.0 collective-permute-done.10.refs_10_
  31.9 2.5 %shard_map.93.base = f32[96,128]{1,0:T(8,128)S(1)} custom-call(s32[16,32]{1,0:T(8,128)S(1)} %get-tuple-element.33.pattern, f32[96,64]{1,0:T(8,128)S(1)} %get-tuple-element.47.leaf_part, f32[64,32]{1,0:T(8,128)S(1)} %shard_map.90.top_s, f32[16,128]{1,0:T(8,128)S(1)} %shard_map.87.mine.refs_0_, f32[16,128]{1,0:T(8,128)S(1)} %collective-permute-done.8.other.refs_1_, ...), custom_call_target="tpu_custom_call" | custom-call | flops 1000 | bytes 1000 | tf_op jit(solution)/shard_map/pallas_call | solution.py:45
  34.4 0.0 collective-permute-done.11.far
  34.4 0.9 %shard_map.94 = f32[2,1,64,64]{3,2,1,0:T(8,128)} custom-call(f32[96,128]{1,0:T(8,128)S(1)} %shard_map.93.base, f32[16,128]{1,0:T(8,128)S(1)} %collective-permute-done.11.far), custom_call_target="tpu_custom_call" | custom-call | flops 1000 | bytes 1000 | tf_op jit(solution)/shard_map/pallas_call | solution.py:45
  (2 shorter events, 0.0 us)
Async XLA Ops:
  1.0 10.9 %collective-permute-start.1 = (f32[128,384]{1,0:T(8,128)S(1)}, f32[128,384]{1,0:T(8,128)S(1)}, u32[]{:S(2)}, u32[]{:S(2)}) collective-permute-start(f32[128,384]{1,0:T(8,128)S(1)} %get-tuple-element.34.pack.refs_0_), channel_id=1, source_target_pairs={{0,3},{1,2},{2,1},{3,0},{4,7},{5,6},{6,5},{7,4},{8,11},{9,10},{10,... | collective-permute-start | bytes 589832 | tf_op jit(solution)/shard_map/ppermute | solution.py:34
  6.2 9.0 %collective-permute-start = (f32[128,256]{1,0:T(8,128)S(1)}, f32[128,256]{1,0:T(8,128)S(1)}, u32[]{:S(2)}, u32[]{:S(2)}) collective-permute-start(f32[128,256]{1,0:T(8,128)S(1)} %get-tuple-element.35), channel_id=1, source_target_pairs={{0,1},{1,0},{2,3},{3,2},{4,5},{5,4},{6,7},{7,6},{8,9},{9,8},{10,11... | collective-permute-start | bytes 393224 | tf_op jit(solution)/shard_map/ppermute | solution.py:34
  12.0 7.4 %collective-permute-start.2 = (f32[128,256]{1,0:T(8,128)S(1)}, f32[128,256]{1,0:T(8,128)S(1)}, u32[]{:S(2)}, u32[]{:S(2)}) collective-permute-start(f32[128,256]{1,0:T(8,128)S(1)} %get-tuple-element.36), channel_id=1, source_target_pairs={{0,1},{1,0},{2,3},{3,2},{4,5},{5,4},{6,7},{7,6},{8,9},{9,8},{10,11... | collective-permute-start | bytes 393224 | tf_op jit(solution)/shard_map/ppermute | solution.py:34
  15.1 4.3 %collective-permute-start.3 = (f32[128,128]{1,0:T(8,128)S(1)}, f32[128,128]{1,0:T(8,128)S(1)}, u32[]{:S(2)}, u32[]{:S(2)}) collective-permute-start(f32[128,128]{1,0:T(8,128)S(1)} %get-tuple-element.37), channel_id=1, source_target_pairs={{0,1},{1,0},{2,3},{3,2},{4,5},{5,4},{6,7},{7,6},{8,9},{9,8},{10,11... | collective-permute-start | bytes 196616 | tf_op jit(solution)/shard_map/ppermute | solution.py:34
  19.5 2.1 %collective-permute-start.4 = (f32[64,1024]{1,0:T(8,128)S(1)}, f32[64,1024]{1,0:T(8,128)S(1)}, u32[]{:S(2)}, u32[]{:S(2)}) collective-permute-start(f32[64,1024]{1,0:T(8,128)S(1)} %get-tuple-element.38.refs_0_.refs_5_), channel_id=1, source_target_pairs={{0,4},{4,0},{8,12},{12,8},{16,20},{20,16},{24,28},{28,24},{1,5},{5... | collective-permute-start | bytes 786440 | tf_op jit(solution)/shard_map/ppermute | solution.py:34
  20.1 7.2 %collective-permute-start.6 = (f32[32,1024]{1,0:T(8,128)S(1)}, f32[32,1024]{1,0:T(8,128)S(1)}, u32[]{:S(2)}, u32[]{:S(2)}) collective-permute-start(f32[32,1024]{1,0:T(8,128)S(1)} %get-tuple-element.48), channel_id=1, source_target_pairs={{0,8},{4,12},{8,0},{12,4},{16,24},{20,28},{24,16},{28,20},{1,9},{5... | collective-permute-start | bytes 393224 | tf_op jit(solution)/shard_map/ppermute | solution.py:34
  21.6 6.8 %collective-permute-start.7 = (f32[32,1024]{1,0:T(8,128)S(1)}, f32[32,1024]{1,0:T(8,128)S(1)}, u32[]{:S(2)}, u32[]{:S(2)}) collective-permute-start(f32[32,1024]{1,0:T(8,128)S(1)} %shard_map.89), channel_id=1, source_target_pairs={{0,16},{4,28},{8,24},{12,20},{16,0},{20,12},{24,8},{28,4},{1,17},{... | collective-permute-start | bytes 393224 | tf_op jit(solution)/shard_map/ppermute | solution.py:511
  23.2 1.2 %collective-permute-start.5 = (f32[16,128]{1,0:T(8,128)S(1)}, f32[16,128]{1,0:T(8,128)S(1)}, u32[]{:S(2)}, u32[]{:S(2)}) collective-permute-start(f32[16,128]{1,0:T(8,128)S(1)} %get-tuple-element.43.mine.near), channel_id=1, source_target_pairs={{0,4},{4,0},{8,12},{12,8},{16,20},{20,16},{24,28},{28,24},{1,5},{5... | collective-permute-start | bytes 24584 | tf_op jit(solution)/shard_map/ppermute | solution.py:34
  24.7 3.7 %collective-permute-start.8 = (f32[16,128]{1,0:T(8,128)S(1)}, f32[16,128]{1,0:T(8,128)S(1)}, u32[]{:S(2)}, u32[]{:S(2)}) collective-permute-start(f32[16,128]{1,0:T(8,128)S(1)} %shard_map.87.mine.refs_0_), channel_id=1, source_target_pairs={{0,8},{4,12},{8,0},{12,4},{16,24},{20,28},{24,16},{28,20},{1,9},{5... | collective-permute-start | bytes 24584 | tf_op jit(solution)/shard_map/ppermute | solution.py:34
  28.4 1.3 %collective-permute-start.9 = (f32[32,1024]{1,0:T(8,128)S(1)}, f32[32,1024]{1,0:T(8,128)S(1)}, u32[]{:S(2)}, u32[]{:S(2)}) collective-permute-start(f32[32,1024]{1,0:T(8,128)S(1)} %collective-permute-done.6.refs_2_.refs_7_), channel_id=1, source_target_pairs={{0,4},{4,0},{8,12},{12,8},{16,20},{20,16},{24,28},{28,24},{1,5},{5... | collective-permute-start | bytes 393224 | tf_op jit(solution)/shard_map/ppermute | solution.py:34
  28.4 3.5 %collective-permute-start.10 = (f32[32,1024]{1,0:T(8,128)S(1)}, f32[32,1024]{1,0:T(8,128)S(1)}, u32[]{:S(2)}, u32[]{:S(2)}) collective-permute-start(f32[32,1024]{1,0:T(8,128)S(1)} %collective-permute-done.7.refs_9_), channel_id=1, source_target_pairs={{0,4},{4,0},{8,12},{12,8},{16,20},{20,16},{24,28},{28,24},{1,5},{5... | collective-permute-start | bytes 393224 | tf_op jit(solution)/shard_map/ppermute | solution.py:34
  30.7 3.7 %collective-permute-start.11 = (f32[16,128]{1,0:T(8,128)S(1)}, f32[16,128]{1,0:T(8,128)S(1)}, u32[]{:S(2)}, u32[]{:S(2)}) collective-permute-start(f32[16,128]{1,0:T(8,128)S(1)} %shard_map.92.refs_2_), channel_id=1, source_target_pairs={{0,16},{4,20},{8,24},{12,28},{16,0},{20,4},{24,8},{28,12},{1,17},{... | collective-permute-start | bytes 24584 | tf_op jit(solution)/shard_map/ppermute | solution.py:34

commit v7 on v6

--- a/solution.py
+++ b/solution.py
@@ -216,18 +216,22 @@
 def far_kernel(plan, high, all_core, out):
     count = high.shape[0]
     out[:count, :] = high[...]
-    out[count:, :] = all_core[plan.offset[3] :, :]
+    out[count:, :] = all_core[plan.offset[3] :, : out.shape[1]]
 
 
 def leaf_kernel(plan, *refs):
-    packs, (whole, ahead, update) = refs[: plan.fronts + 1], refs[plan.fronts + 1 :]
+    packs, (all_part, whole, ahead, update, message) = refs[: plan.fronts + 1], refs[plan.fronts + 1 :]
     rhs, upd, full = plan.rhs, plan.upd, plan.full
     whole_rows(plan, packs, plan.rows, whole)
     flipped = whole[:, full:].T
     solved = nt(flipped[:rhs], whole[:, :full])
     ahead[:rhs, :] = solved
     ahead[rhs:, :] = flipped[rhs : rhs + upd]
-    update[...] = dense(nt(solved, flipped[rhs : rhs + upd]))
+    result = dense(nt(solved, flipped[rhs : rhs + upd]))
+    update[...] = result
+    wide = all_part.shape[1]
+    message[:, :wide] = all_part[...]
+    message[: result.shape[0], wide:] = result
 
 
 def assemble(plan, level, parts, whole):
@@ -352,6 +356,13 @@
     total = base[:rhs] + nn(undense(far[...]), base[rhs:])
     out[0, 0] = total[:, :rows]
     out[1, 0] = total[:, rows:]
+
+
+def first_update_kernel(plan, start, cross, mine, message, out, other):
+    count, wide = mine.shape
+    other[...] = message[:count, message.shape[1] - wide :]
+    both = jnp.concatenate([undense(mine[...]), undense(other[...])], axis=1)
+    out[...] = dense(start[...] - nt(both, cross[...]))
 
 
 def update_kernel(plan, start, cross, mine, other, out):
@@ -497,15 +508,19 @@
         pack, beside, beyond, across, second,
         scratch=[pltpu.VMEM((full, width), jnp.float32)],
     )
-    all_core = exchange(all_part, "leaf", 1)
     by_x = exchange(late_part, "leaf", 2)
     leaf_beyond, _ = lax.optimization_barrier((beyond, all_part))
-    leaf_all, leaf_ahead, u0 = kernel(
+    leaf_all, leaf_ahead, u0, message = kernel(
         leaf_kernel,
-        [(full, width), (rhs + upd, full), (rhs // 4, 4 * upd)],
-        pack, beside, leaf_beyond, across, second,
-    )
-    u0_far = exchange(u0, "leaf", 1)
+        [
+            (full, width),
+            (rhs + upd, full),
+            (rhs // 4, 4 * upd),
+            (rows, wide + 4 * upd),
+        ],
+        pack, beside, leaf_beyond, across, second, all_part,
+    )
+    all_core = exchange(message, "leaf", 1)
     high_part, _ = lax.optimization_barrier((high_part, u0))
     (far_part,) = kernel(far_kernel, [(2 * high_part.shape[0], wide)], high_part, all_core)
     far = lax.ppermute(far_part, "leaf", [(src, src ^ (6 if src % 2 else 4)) for src in range(plan.groups)])
@@ -518,7 +533,9 @@
         )
 
     whole1, cross1, start1 = lead_of(1, all_part, all_core)
-    (u1,) = kernel(update_kernel, [(rhs // 4, 4 * upd)], start1, cross1, u0, u0_far)
+    u1, u0_far = kernel(
+        first_update_kernel, [(rhs // 4, 4 * upd)] * 2, start1, cross1, u0, all_core
+    )
     u1_far = exchange(u1, "leaf", 2)
 
     whole1, _ = lax.optimization_barrier((whole1, u1))

time: 35.4 us -> 35.4 us (level)
  waiting for transfers between devices: 12.3 us -> 11.6 us
  starting transfers between devices: 14.6 us -> 15.2 us
    ppermute x11 -> x10, waiting for transfers between devices: 12.3 us -> 11.6 us  [exchange(): lax.ppermute(block, axis, [(src, src ^ mask) for src in range(count)])]
    ppermute x11 -> x10, starting transfers between devices: 13 us -> 13.6 us  [exchange(): lax.ppermute(block, axis, [(src, src ^ mask) for src in range(count)])]
  transfers between devices with their start and end apart: 12 -> 11, of which waited for: 5 -> 4; matrix products, arithmetic and copies ran while one was open for 0% -> 0% of each run, Pallas kernels for 18% -> 16%
where the time goes in v7:
time: 35.4 us; the launch traced here: 35.3 us
  starting transfers between devices  15.2 us (43%)
  waiting for transfers between devices  11.6 us (33%)
  Pallas kernels  8.43 us (24%)
    ppermute x10, starting transfers between devices, exchange(): lax.ppermute(block, axis, [(src, src ^ mask) for src in range(count)])  13.6 us
    ppermute x10, waiting for transfers between devices, exchange(): lax.ppermute(block, axis, [(src, src ^ mask) for src in range(count)])  11.6 us
    pallas_call x13, Pallas kernels, call(): pl.pallas_call(kernel, out_shape=[jax.ShapeDtypeStruct(out, jnp.float32)...  8.43 us
    ppermute x1, starting transfers between devices, chain(): lax.ppermute(far_part, 'leaf', [(src, src ^ (6 if src % 2 else 4)) for sr...  1.58 us
  transfers between devices with their start and end apart: 11, of which 4 were waited for; matrix products, arithmetic and copies ran while one was open for 0% of the time, Pallas kernels for 16%

profile of v7, /device:TPU:0, one launch (start us, length us, event | category | flops | bytes accessed | tf_op | source)
XLA Modules:
  0.0 35.3 jit_solution(14654558293524996710)
XLA Ops:
  0.0 1.0 %shard_map.82 = (f32[128,384]{1,0:T(8,128)S(1)}, f32[128,256]{1,0:T(8,128)S(1)}, s32[16,32]{1,0:T(8,128)S(1)}) custom-call(s32[2,8,32]{2,1,0:T(8,128)} %pattern.1, f32[1,64,64]{2,1,0:T(8,128)} %lr.1, f32[1,64,64]{2,1,0:T(8,128)} %sr.1, f32[1,64,256]{2,1,0:T(8,128)} %li.1, f32[1,64,256]{2,1,0:T(8,128)} %si.1, f32[1,32,64]{2,1,0:T(8,128)} %lu.1, ...), custom_call_target="tpu_custom_call" | custom-call | flops 1000 | bytes 1000 | tf_op jit(solution)/shard_map/pallas_call | solution.py:45
  1.0 5.1 %collective-permute-start.1 = (f32[128,384]{1,0:T(8,128)S(1)}, f32[128,384]{1,0:T(8,128)S(1)}, u32[]{:S(2)}, u32[]{:S(2)}) collective-permute-start(f32[128,384]{1,0:T(8,128)S(1)} %get-tuple-element.37.pack.refs_0_), channel_id=1, source_target_pairs={{0,3},{1,2},{2,1},{3,0},{4,7},{5,6},{6,5},{7,4},{8,11},{9,10},{10,... | collective-permute-start | bytes 589832 | tf_op jit(solution)/shard_map/ppermute | solution.py:34
  6.2 0.0 collective-permute-start
  6.2 5.8 %collective-permute-done.1.across.refs_3_ = f32[128,384]{1,0:T(8,128)S(1)} collective-permute-done((f32[128,384]{1,0:T(8,128)S(1)}, f32[128,384]{1,0:T(8,128)S(1)}, u32[]{:S(2)}, u32[]{:S(2)}) %collective-permute-start.1) | collective-permute-done | bytes 196640 | tf_op jit(solution)/shard_map/ppermute | solution.py:34
  12.0 3.1 %collective-permute-start.2 = (f32[128,256]{1,0:T(8,128)S(1)}, f32[128,256]{1,0:T(8,128)S(1)}, u32[]{:S(2)}, u32[]{:S(2)}) collective-permute-start(f32[128,256]{1,0:T(8,128)S(1)} %get-tuple-element.39), channel_id=1, source_target_pairs={{0,1},{1,0},{2,3},{3,2},{4,5},{5,4},{6,7},{7,6},{8,9},{9,8},{10,11... | collective-permute-start | bytes 393224 | tf_op jit(solution)/shard_map/ppermute | solution.py:34
  15.1 0.1 collective-permute-start.3
  15.1 0.0 collective-permute-done.refs_1_
  15.2 4.2 %collective-permute-done.3.refs_4_ = f32[128,128]{1,0:T(8,128)S(1)} collective-permute-done((f32[128,128]{1,0:T(8,128)S(1)}, f32[128,128]{1,0:T(8,128)S(1)}, u32[]{:S(2)}, u32[]{:S(2)}) %collective-permute-start.3) | collective-permute-done | bytes 65568 | tf_op jit(solution)/shard_map/ppermute | solution.py:34
  19.3 0.0 collective-permute-done.2.refs_2_
  19.3 0.1 shard_map.84
  19.5 0.5 %shard_map.85 = (f32[256,384]{1,0:T(8,128)S(1)}, f32[96,256]{1,0:T(8,128)S(1)}, f32[16,128]{1,0:T(8,128)S(1)}, f32[64,1152]{1,0:T(8,128)S(1)}) custom-call(f32[128,384]{1,0:T(8,128)S(1)} %get-tuple-element.37.pack.refs_0_, f32[128,256]{1,0:T(8,128)S(1)} %collective-permute-done.refs_1_, f32[128,256]{1,0:T(8,128)S(1)} %collective-permute-done.2.refs_2_, ...), custom_call_target="tpu_custom_call" | custom-call | flops 1000 | bytes 1000 | tf_op jit(solution)/shard_map/pallas_call | solution.py:45
  20.0 0.0 collective-permute-start.4
  20.1 1.6 %collective-permute-start.5 = (f32[32,1024]{1,0:T(8,128)S(1)}, f32[32,1024]{1,0:T(8,128)S(1)}, u32[]{:S(2)}, u32[]{:S(2)}) collective-permute-start(f32[32,1024]{1,0:T(8,128)S(1)} %get-tuple-element.54), channel_id=1, source_target_pairs={{0,8},{4,12},{8,0},{12,4},{16,24},{20,28},{24,16},{28,20},{1,9},{5... | collective-permute-start | bytes 393224 | tf_op jit(solution)/shard_map/ppermute | solution.py:34
  21.6 0.0 collective-permute-done.4.refs_1_.message.all_core.refs_6_
  21.6 1.6 %collective-permute-start.6 = (f32[32,1024]{1,0:T(8,128)S(1)}, f32[32,1024]{1,0:T(8,128)S(1)}, u32[]{:S(2)}, u32[]{:S(2)}) collective-permute-start(f32[32,1024]{1,0:T(8,128)S(1)} %shard_map.89), channel_id=1, source_target_pairs={{0,16},{4,28},{8,24},{12,20},{16,0},{20,12},{24,8},{28,4},{1,17},{... | collective-permute-start | bytes 393224 | tf_op jit(solution)/shard_map/ppermute | solution.py:526
  23.2 0.6 %shard_map.86 = (f32[256,384]{1,0:T(8,128)S(1)}, f32[32,64]{1,0:T(8,128)S(1)}, f32[64,32]{1,0:T(8,128)S(1)}) custom-call(s32[16,32]{1,0:T(8,128)S(1)} %get-tuple-element.36.pattern, f32[64,1024]{1,0:T(8,128)S(1)} %get-tuple-element.41.refs_5_.refs_0_, f32[64,1152]{1,0:T(8,128)S(1)} %collective-permute-done.4.refs_1_.message.all_core.refs_6_), custom_call_target="tpu_custom_call" | custom-call | flops 1000 | bytes 1000 | tf_op jit(solution)/shard_map/pallas_call | solution.py:45
  23.8 0.4 %shard_map.87 = (f32[16,128]{1,0:T(8,128)S(1)}, f32[16,128]{1,0:T(8,128)S(1)}) custom-call(f32[64,32]{1,0:T(8,128)S(1)} %get-tuple-element.45.start, f32[32,64]{1,0:T(8,128)S(1)} %get-tuple-element.46.cross, f32[16,128]{1,0:T(8,128)S(1)} %get-tuple-element.47.mine.near, f32[64,1152]{1,0:T(8,128)S(1)} %collective-permute-done.4.refs_1_.message.all_core.refs_6_), custom_call_target="tpu_custom_call" | custom-call | flops 1000 | bytes 1000 | tf_op jit(solution)/shard_map/pallas_call | solution.py:45
  24.2 1.5 %collective-permute-start.7 = (f32[16,128]{1,0:T(8,128)S(1)}, f32[16,128]{1,0:T(8,128)S(1)}, u32[]{:S(2)}, u32[]{:S(2)}) collective-permute-start(f32[16,128]{1,0:T(8,128)S(1)} %get-tuple-element.48.mine.refs_0_), channel_id=1, source_target_pairs={{0,8},{4,12},{8,0},{12,4},{16,24},{20,28},{24,16},{28,20},{1,9},{5... | collective-permute-start | bytes 24584 | tf_op jit(solution)/shard_map/ppermute | solution.py:34
  25.7 1.2 %shard_map.88 = (f32[160,64]{1,0:T(8,128)S(1)}, f32[96,64]{1,0:T(8,128)S(1)}) custom-call(s32[16,32]{1,0:T(8,128)S(1)} %get-tuple-element.36.pattern, f32[256,384]{1,0:T(8,128)S(1)} %get-tuple-element.49.whole, f32[256,384]{1,0:T(8,128)S(1)} %get-tuple-element.50.leaf_all, f32[96,256]{1,0:T(8,128)S(1)} %get-tuple-element.51.leaf_ahead, ...), custom_call_target="tpu_custom_call" | custom-call | flops 1000 | bytes 1000 | tf_op jit(solution)/shard_map/pallas_call | solution.py:45
  26.8 0.3 shard_map.90.top_s
  27.1 0.0 collective-permute-done.5.refs_2_.refs_7_
  27.1 0.7 %collective-permute-done.7.other.refs_1_ = f32[16,128]{1,0:T(8,128)S(1)} collective-permute-done((f32[16,128]{1,0:T(8,128)S(1)}, f32[16,128]{1,0:T(8,128)S(1)}, u32[]{:S(2)}, u32[]{:S(2)}) %collective-permute-start.7) | collective-permute-done | bytes 8224 | tf_op jit(solution)/shard_map/ppermute | solution.py:34
  27.8 0.0 collective-permute-done.6.refs_9_
  27.8 0.4 %collective-permute-start.8 = (f32[32,1024]{1,0:T(8,128)S(1)}, f32[32,1024]{1,0:T(8,128)S(1)}, u32[]{:S(2)}, u32[]{:S(2)}) collective-permute-start(f32[32,1024]{1,0:T(8,128)S(1)} %collective-permute-done.5.refs_2_.refs_7_), channel_id=1, source_target_pairs={{0,4},{4,0},{8,12},{12,8},{16,20},{20,16},{24,28},{28,24},{1,5},{5... | collective-permute-start | bytes 393224 | tf_op jit(solution)/shard_map/ppermute | solution.py:34
  28.2 0.1 collective-permute-start.9
  28.3 0.9 %collective-permute-done.8.refs_3_.refs_8_ = f32[32,1024]{1,0:T(8,128)S(1)} collective-permute-done((f32[32,1024]{1,0:T(8,128)S(1)}, f32[32,1024]{1,0:T(8,128)S(1)}, u32[]{:S(2)}, u32[]{:S(2)}) %collective-permute-start.8) | collective-permute-done | bytes 131104 | tf_op jit(solution)/shard_map/ppermute | solution.py:34
  29.2 0.6 %shard_map.91 = (f32[256,384]{1,0:T(8,128)S(1)}, f32[32,64]{1,0:T(8,128)S(1)}, f32[64,32]{1,0:T(8,128)S(1)}) custom-call(s32[16,32]{1,0:T(8,128)S(1)} %get-tuple-element.36.pattern, f32[64,1024]{1,0:T(8,128)S(1)} %get-tuple-element.41.refs_5_.refs_0_, f32[64,1152]{1,0:T(8,128)S(1)} %collective-permute-done.4.refs_1_.message.all_core.refs_6_, ...), custom_call_target="tpu_custom_call" | custom-call | flops 1000 | bytes 1000 | tf_op jit(solution)/shard_map/pallas_call | solution.py:45
  29.8 0.4 shard_map.92.refs_2_
  30.2 1.7 %collective-permute-start.10 = (f32[16,128]{1,0:T(8,128)S(1)}, f32[16,128]{1,0:T(8,128)S(1)}, u32[]{:S(2)}, u32[]{:S(2)}) collective-permute-start(f32[16,128]{1,0:T(8,128)S(1)} %shard_map.92.refs_2_), channel_id=1, source_target_pairs={{0,16},{4,20},{8,24},{12,28},{16,0},{20,4},{24,8},{28,12},{1,17},{... | collective-permute-start | bytes 24584 | tf_op jit(solution)/shard_map/ppermute | solution.py:34
  31.9 0.0 collective-permute-done.9.refs_10_
  31.9 2.5 %shard_map.93.base = f32[96,128]{1,0:T(8,128)S(1)} custom-call(s32[16,32]{1,0:T(8,128)S(1)} %get-tuple-element.36.pattern, f32[96,64]{1,0:T(8,128)S(1)} %get-tuple-element.53.leaf_part, f32[64,32]{1,0:T(8,128)S(1)} %shard_map.90.top_s, f32[16,128]{1,0:T(8,128)S(1)} %get-tuple-element.48.mine.refs_0_, f32[16,128]{1,0:T(8,128)S(1)} %collective-permute-done.7.other.refs_1_, ...), custom_call_target="tpu_custom_call" | custom-call | flops 1000 | bytes 1000 | tf_op jit(solution)/shard_map/pallas_call | solution.py:45
  34.4 0.0 collective-permute-done.10.far
  34.4 0.9 %shard_map.94 = f32[2,1,64,64]{3,2,1,0:T(8,128)} custom-call(f32[96,128]{1,0:T(8,128)S(1)} %shard_map.93.base, f32[16,128]{1,0:T(8,128)S(1)} %collective-permute-done.10.far), custom_call_target="tpu_custom_call" | custom-call | flops 1000 | bytes 1000 | tf_op jit(solution)/shard_map/pallas_call | solution.py:45
  (2 shorter events, 0.0 us)
Async XLA Ops:
  1.0 10.9 %collective-permute-start.1 = (f32[128,384]{1,0:T(8,128)S(1)}, f32[128,384]{1,0:T(8,128)S(1)}, u32[]{:S(2)}, u32[]{:S(2)}) collective-permute-start(f32[128,384]{1,0:T(8,128)S(1)} %get-tuple-element.37.pack.refs_0_), channel_id=1, source_target_pairs={{0,3},{1,2},{2,1},{3,0},{4,7},{5,6},{6,5},{7,4},{8,11},{9,10},{10,... | collective-permute-start | bytes 589832 | tf_op jit(solution)/shard_map/ppermute | solution.py:34
  6.2 9.0 %collective-permute-start = (f32[128,256]{1,0:T(8,128)S(1)}, f32[128,256]{1,0:T(8,128)S(1)}, u32[]{:S(2)}, u32[]{:S(2)}) collective-permute-start(f32[128,256]{1,0:T(8,128)S(1)} %get-tuple-element.38), channel_id=1, source_target_pairs={{0,1},{1,0},{2,3},{3,2},{4,5},{5,4},{6,7},{7,6},{8,9},{9,8},{10,11... | collective-permute-start | bytes 393224 | tf_op jit(solution)/shard_map/ppermute | solution.py:34
  12.0 7.4 %collective-permute-start.2 = (f32[128,256]{1,0:T(8,128)S(1)}, f32[128,256]{1,0:T(8,128)S(1)}, u32[]{:S(2)}, u32[]{:S(2)}) collective-permute-start(f32[128,256]{1,0:T(8,128)S(1)} %get-tuple-element.39), channel_id=1, source_target_pairs={{0,1},{1,0},{2,3},{3,2},{4,5},{5,4},{6,7},{7,6},{8,9},{9,8},{10,11... | collective-permute-start | bytes 393224 | tf_op jit(solution)/shard_map/ppermute | solution.py:34
  15.1 4.3 %collective-permute-start.3 = (f32[128,128]{1,0:T(8,128)S(1)}, f32[128,128]{1,0:T(8,128)S(1)}, u32[]{:S(2)}, u32[]{:S(2)}) collective-permute-start(f32[128,128]{1,0:T(8,128)S(1)} %get-tuple-element.40), channel_id=1, source_target_pairs={{0,1},{1,0},{2,3},{3,2},{4,5},{5,4},{6,7},{7,6},{8,9},{9,8},{10,11... | collective-permute-start | bytes 196616 | tf_op jit(solution)/shard_map/ppermute | solution.py:34
  20.0 1.6 %collective-permute-start.4 = (f32[64,1152]{1,0:T(8,128)S(1)}, f32[64,1152]{1,0:T(8,128)S(1)}, u32[]{:S(2)}, u32[]{:S(2)}) collective-permute-start(f32[64,1152]{1,0:T(8,128)S(1)} %get-tuple-element.43), channel_id=1, source_target_pairs={{0,4},{4,0},{8,12},{12,8},{16,20},{20,16},{24,28},{28,24},{1,5},{5... | collective-permute-start | bytes 884744 | tf_op jit(solution)/shard_map/ppermute | solution.py:34
  20.1 7.1 %collective-permute-start.5 = (f32[32,1024]{1,0:T(8,128)S(1)}, f32[32,1024]{1,0:T(8,128)S(1)}, u32[]{:S(2)}, u32[]{:S(2)}) collective-permute-start(f32[32,1024]{1,0:T(8,128)S(1)} %get-tuple-element.54), channel_id=1, source_target_pairs={{0,8},{4,12},{8,0},{12,4},{16,24},{20,28},{24,16},{28,20},{1,9},{5... | collective-permute-start | bytes 393224 | tf_op jit(solution)/shard_map/ppermute | solution.py:34
  21.6 6.2 %collective-permute-start.6 = (f32[32,1024]{1,0:T(8,128)S(1)}, f32[32,1024]{1,0:T(8,128)S(1)}, u32[]{:S(2)}, u32[]{:S(2)}) collective-permute-start(f32[32,1024]{1,0:T(8,128)S(1)} %shard_map.89), channel_id=1, source_target_pairs={{0,16},{4,28},{8,24},{12,20},{16,0},{20,12},{24,8},{28,4},{1,17},{... | collective-permute-start | bytes 393224 | tf_op jit(solution)/shard_map/ppermute | solution.py:526
  24.2 3.7 %collective-permute-start.7 = (f32[16,128]{1,0:T(8,128)S(1)}, f32[16,128]{1,0:T(8,128)S(1)}, u32[]{:S(2)}, u32[]{:S(2)}) collective-permute-start(f32[16,128]{1,0:T(8,128)S(1)} %get-tuple-element.48.mine.refs_0_), channel_id=1, source_target_pairs={{0,8},{4,12},{8,0},{12,4},{16,24},{20,28},{24,16},{28,20},{1,9},{5... | collective-permute-start | bytes 24584 | tf_op jit(solution)/shard_map/ppermute | solution.py:34
  27.8 1.4 %collective-permute-start.8 = (f32[32,1024]{1,0:T(8,128)S(1)}, f32[32,1024]{1,0:T(8,128)S(1)}, u32[]{:S(2)}, u32[]{:S(2)}) collective-permute-start(f32[32,1024]{1,0:T(8,128)S(1)} %collective-permute-done.5.refs_2_.refs_7_), channel_id=1, source_target_pairs={{0,4},{4,0},{8,12},{12,8},{16,20},{20,16},{24,28},{28,24},{1,5},{5... | collective-permute-start | bytes 393224 | tf_op jit(solution)/shard_map/ppermute | solution.py:34
  28.2 3.7 %collective-permute-start.9 = (f32[32,1024]{1,0:T(8,128)S(1)}, f32[32,1024]{1,0:T(8,128)S(1)}, u32[]{:S(2)}, u32[]{:S(2)}) collective-permute-start(f32[32,1024]{1,0:T(8,128)S(1)} %collective-permute-done.6.refs_9_), channel_id=1, source_target_pairs={{0,4},{4,0},{8,12},{12,8},{16,20},{20,16},{24,28},{28,24},{1,5},{5... | collective-permute-start | bytes 393224 | tf_op jit(solution)/shard_map/ppermute | solution.py:34
  30.2 4.2 %collective-permute-start.10 = (f32[16,128]{1,0:T(8,128)S(1)}, f32[16,128]{1,0:T(8,128)S(1)}, u32[]{:S(2)}, u32[]{:S(2)}) collective-permute-start(f32[16,128]{1,0:T(8,128)S(1)} %shard_map.92.refs_2_), channel_id=1, source_target_pairs={{0,16},{4,20},{8,24},{12,28},{16,0},{20,4},{24,8},{28,12},{1,17},{... | collective-permute-start | bytes 24584 | tf_op jit(solution)/shard_map/ppermute | solution.py:34

commit v8 on v7

--- a/solution.py
+++ b/solution.py
@@ -281,13 +281,17 @@
     return [nt(block, ahead[rhs:]), nt(ahead[:rhs], block)] + result
 
 
-def lead_kernel(plan, level, pattern, *refs):
+def lead_kernel(plan, level, pattern, mine, other, *refs):
     blocks = plan.blocks[level]
     parts = [
         (ref, plan.offset[level] if slot < 2 else 0, slot) for slot, ref in enumerate(refs[:blocks])
     ]
-    whole, cross, start = refs[blocks:]
-    cross[...], start[...] = lead_level(plan, level, pattern, parts, whole)
+    whole, out, far = refs[blocks:]
+    cross, start = lead_level(plan, level, pattern, parts, whole)
+    count, wide = mine.shape
+    far[...] = other[:count, other.shape[1] - wide :]
+    both = jnp.concatenate([undense(mine[...]), undense(far[...])], axis=1)
+    out[...] = dense(start - nt(both, cross))
 
 
 def lower_kernel(plan, pattern, whole, leaf_all, leaf_ahead, near, far, own_part, leaf_part):
@@ -356,18 +360,6 @@
     total = base[:rhs] + nn(undense(far[...]), base[rhs:])
     out[0, 0] = total[:, :rows]
     out[1, 0] = total[:, rows:]
-
-
-def first_update_kernel(plan, start, cross, mine, message, out, other):
-    count, wide = mine.shape
-    other[...] = message[:count, message.shape[1] - wide :]
-    both = jnp.concatenate([undense(mine[...]), undense(other[...])], axis=1)
-    out[...] = dense(start[...] - nt(both, cross[...]))
-
-
-def update_kernel(plan, start, cross, mine, other, out):
-    both = jnp.concatenate([undense(mine[...]), undense(other[...])], axis=1)
-    out[...] = dense(start[...] - nt(both, cross[...]))
 
 
 def partner(block, axis, distance):
@@ -524,18 +516,15 @@
     high_part, _ = lax.optimization_barrier((high_part, u0))
     (far_part,) = kernel(far_kernel, [(2 * high_part.shape[0], wide)], high_part, all_core)
     far = lax.ppermute(far_part, "leaf", [(src, src ^ (6 if src % 2 else 4)) for src in range(plan.groups)])
-    def lead_of(level, *parts):
+    def lead_of(level, mine, other, *parts):
         return kernel(
             lead_kernel,
-            [(full, width), (upd, 2 * upd), (rhs, upd)],
-            ids, *parts,
+            [(full, width)] + [(rhs // 4, 4 * upd)] * 2,
+            ids, mine, other, *parts,
             extra=(level,),
         )
 
-    whole1, cross1, start1 = lead_of(1, all_part, all_core)
-    u1, u0_far = kernel(
-        first_update_kernel, [(rhs // 4, 4 * upd)] * 2, start1, cross1, u0, all_core
-    )
+    whole1, u1, u0_far = lead_of(1, u0, all_core, all_part, all_core)
     u1_far = exchange(u1, "leaf", 2)
 
     whole1, _ = lax.optimization_barrier((whole1, u1))
@@ -556,10 +545,7 @@
     )
     by_x_core = exchange(by_x, "leaf", 1)
     far_core = exchange(far, "leaf", 1)
-    whole2, cross2, start2 = lead_of(2, all_part, all_core, by_x, by_x_core)
-    (u2,) = kernel(
-        update_kernel, [(rhs // 4, 4 * upd)], start2, cross2, u1, u1_far
-    )
+    whole2, u2, u1_far = lead_of(2, u1, u1_far, all_part, all_core, by_x, by_x_core)
     u2_far = exchange(u2, "leaf", 4)
     (base,) = kernel(
         upper_kernel,

time: 35.4 us -> 35.3 us (level)
  Pallas kernels: 8.43 us -> 8.05 us
    pallas_call x13 -> x11, Pallas kernels: 8.43 us -> 8.05 us  [call(): pl.pallas_call(kernel, out_shape=[jax.ShapeDtypeStruct(out, jnp.float32)...]
  transfers between devices with their start and end apart: 11 -> 11, of which waited for: 4 -> 4; matrix products, arithmetic and copies ran while one was open for 0% -> 0% of each run, Pallas kernels for 16% -> 15%
where the time goes in v8:
time: 35.3 us; the launch traced here: 35.1 us
  starting transfers between devices  15.3 us (43%)
  waiting for transfers between devices  11.7 us (33%)
  Pallas kernels  8.05 us (23%)
    ppermute x10, starting transfers between devices, exchange(): lax.ppermute(block, axis, [(src, src ^ mask) for src in range(count)])  13.7 us
    ppermute x10, waiting for transfers between devices, exchange(): lax.ppermute(block, axis, [(src, src ^ mask) for src in range(count)])  11.7 us
    pallas_call x11, Pallas kernels, call(): pl.pallas_call(kernel, out_shape=[jax.ShapeDtypeStruct(out, jnp.float32)...  8.05 us
    ppermute x1, starting transfers between devices, chain(): lax.ppermute(far_part, 'leaf', [(src, src ^ (6 if src % 2 else 4)) for sr...  1.58 us
  transfers between devices with their start and end apart: 11, of which 4 were waited for; matrix products, arithmetic and copies ran while one was open for 0% of the time, Pallas kernels for 15%

profile of v8, /device:TPU:0, one launch (start us, length us, event | category | flops | bytes accessed | tf_op | source)
XLA Modules:
  0.0 35.1 jit_solution(3000461695833989144)
XLA Ops:
  0.0 1.0 %shard_map.82 = (f32[128,384]{1,0:T(8,128)S(1)}, f32[128,256]{1,0:T(8,128)S(1)}, s32[16,32]{1,0:T(8,128)S(1)}) custom-call(s32[2,8,32]{2,1,0:T(8,128)} %pattern.1, f32[1,64,64]{2,1,0:T(8,128)} %lr.1, f32[1,64,64]{2,1,0:T(8,128)} %sr.1, f32[1,64,256]{2,1,0:T(8,128)} %li.1, f32[1,64,256]{2,1,0:T(8,128)} %si.1, f32[1,32,64]{2,1,0:T(8,128)} %lu.1, ...), custom_call_target="tpu_custom_call" | custom-call | flops 1000 | bytes 1000 | tf_op jit(solution)/shard_map/pallas_call | solution.py:45
  1.0 5.1 %collective-permute-start.1 = (f32[128,384]{1,0:T(8,128)S(1)}, f32[128,384]{1,0:T(8,128)S(1)}, u32[]{:S(2)}, u32[]{:S(2)}) collective-permute-start(f32[128,384]{1,0:T(8,128)S(1)} %get-tuple-element.35.pack.refs_0_), channel_id=1, source_target_pairs={{0,3},{1,2},{2,1},{3,0},{4,7},{5,6},{6,5},{7,4},{8,11},{9,10},{10,... | collective-permute-start | bytes 589832 | tf_op jit(solution)/shard_map/ppermute | solution.py:34
  6.2 0.0 collective-permute-start
  6.2 5.8 %collective-permute-done.1.across.refs_3_ = f32[128,384]{1,0:T(8,128)S(1)} collective-permute-done((f32[128,384]{1,0:T(8,128)S(1)}, f32[128,384]{1,0:T(8,128)S(1)}, u32[]{:S(2)}, u32[]{:S(2)}) %collective-permute-start.1) | collective-permute-done | bytes 196640 | tf_op jit(solution)/shard_map/ppermute | solution.py:34
  12.0 3.1 %collective-permute-start.2 = (f32[128,256]{1,0:T(8,128)S(1)}, f32[128,256]{1,0:T(8,128)S(1)}, u32[]{:S(2)}, u32[]{:S(2)}) collective-permute-start(f32[128,256]{1,0:T(8,128)S(1)} %get-tuple-element.37), channel_id=1, source_target_pairs={{0,1},{1,0},{2,3},{3,2},{4,5},{5,4},{6,7},{7,6},{8,9},{9,8},{10,11... | collective-permute-start | bytes 393224 | tf_op jit(solution)/shard_map/ppermute | solution.py:34
  15.1 0.1 collective-permute-start.3
  15.1 0.0 collective-permute-done.refs_1_
  15.2 4.2 %collective-permute-done.3.refs_4_ = f32[128,128]{1,0:T(8,128)S(1)} collective-permute-done((f32[128,128]{1,0:T(8,128)S(1)}, f32[128,128]{1,0:T(8,128)S(1)}, u32[]{:S(2)}, u32[]{:S(2)}) %collective-permute-start.3) | collective-permute-done | bytes 65568 | tf_op jit(solution)/shard_map/ppermute | solution.py:34
  19.3 0.0 collective-permute-done.2.refs_2_
  19.3 0.1 shard_map.84
  19.5 0.5 %shard_map.85 = (f32[256,384]{1,0:T(8,128)S(1)}, f32[96,256]{1,0:T(8,128)S(1)}, f32[16,128]{1,0:T(8,128)S(1)}, f32[64,1152]{1,0:T(8,128)S(1)}) custom-call(f32[128,384]{1,0:T(8,128)S(1)} %get-tuple-element.35.pack.refs_0_, f32[128,256]{1,0:T(8,128)S(1)} %collective-permute-done.refs_1_, f32[128,256]{1,0:T(8,128)S(1)} %collective-permute-done.2.refs_2_, ...), custom_call_target="tpu_custom_call" | custom-call | flops 1000 | bytes 1000 | tf_op jit(solution)/shard_map/pallas_call | solution.py:45
  20.0 0.0 collective-permute-start.4
  20.1 1.6 %collective-permute-start.5 = (f32[32,1024]{1,0:T(8,128)S(1)}, f32[32,1024]{1,0:T(8,128)S(1)}, u32[]{:S(2)}, u32[]{:S(2)}) collective-permute-start(f32[32,1024]{1,0:T(8,128)S(1)} %get-tuple-element.50), channel_id=1, source_target_pairs={{0,8},{4,12},{8,0},{12,4},{16,24},{20,28},{24,16},{28,20},{1,9},{5... | collective-permute-start | bytes 393224 | tf_op jit(solution)/shard_map/ppermute | solution.py:34
  21.6 0.0 collective-permute-done.4.other.refs_1_.all_core.refs_6_
  21.6 1.6 %collective-permute-start.6 = (f32[32,1024]{1,0:T(8,128)S(1)}, f32[32,1024]{1,0:T(8,128)S(1)}, u32[]{:S(2)}, u32[]{:S(2)}) collective-permute-start(f32[32,1024]{1,0:T(8,128)S(1)} %shard_map.88), channel_id=1, source_target_pairs={{0,16},{4,28},{8,24},{12,20},{16,0},{20,12},{24,8},{28,4},{1,17},{... | collective-permute-start | bytes 393224 | tf_op jit(solution)/shard_map/ppermute | solution.py:518
  23.2 0.7 %shard_map.86 = (f32[256,384]{1,0:T(8,128)S(1)}, f32[16,128]{1,0:T(8,128)S(1)}, f32[16,128]{1,0:T(8,128)S(1)}) custom-call(s32[16,32]{1,0:T(8,128)S(1)} %get-tuple-element.34.pattern, f32[16,128]{1,0:T(8,128)S(1)} %get-tuple-element.41.mine.near, f32[64,1152]{1,0:T(8,128)S(1)} %collective-permute-done.4.other.refs_1_.all_core.refs_6_, ...), custom_call_target="tpu_custom_call" | custom-call | flops 1000 | bytes 1000 | tf_op jit(solution)/shard_map/pallas_call | solution.py:45
  24.0 1.5 %collective-permute-start.7 = (f32[16,128]{1,0:T(8,128)S(1)}, f32[16,128]{1,0:T(8,128)S(1)}, u32[]{:S(2)}, u32[]{:S(2)}) collective-permute-start(f32[16,128]{1,0:T(8,128)S(1)} %get-tuple-element.44.mine.refs_0_), channel_id=1, source_target_pairs={{0,8},{4,12},{8,0},{12,4},{16,24},{20,28},{24,16},{28,20},{1,9},{5... | collective-permute-start | bytes 24584 | tf_op jit(solution)/shard_map/ppermute | solution.py:34
  25.5 1.1 %shard_map.87 = (f32[160,64]{1,0:T(8,128)S(1)}, f32[96,64]{1,0:T(8,128)S(1)}) custom-call(s32[16,32]{1,0:T(8,128)S(1)} %get-tuple-element.34.pattern, f32[256,384]{1,0:T(8,128)S(1)} %get-tuple-element.45.whole, f32[256,384]{1,0:T(8,128)S(1)} %get-tuple-element.46.leaf_all, f32[96,256]{1,0:T(8,128)S(1)} %get-tuple-element.47.leaf_ahead, ...), custom_call_target="tpu_custom_call" | custom-call | flops 1000 | bytes 1000 | tf_op jit(solution)/shard_map/pallas_call | solution.py:45
  26.6 0.3 shard_map.89.top_s
  26.9 0.0 collective-permute-done.5.refs_2_.refs_7_
  26.9 0.7 %collective-permute-done.7.other = f32[16,128]{1,0:T(8,128)S(1)} collective-permute-done((f32[16,128]{1,0:T(8,128)S(1)}, f32[16,128]{1,0:T(8,128)S(1)}, u32[]{:S(2)}, u32[]{:S(2)}) %collective-permute-start.7) | collective-permute-done | bytes 8224 | tf_op jit(solution)/shard_map/ppermute | solution.py:34
  27.6 0.0 collective-permute-done.6.refs_9_
  27.6 0.6 %collective-permute-start.8 = (f32[32,1024]{1,0:T(8,128)S(1)}, f32[32,1024]{1,0:T(8,128)S(1)}, u32[]{:S(2)}, u32[]{:S(2)}) collective-permute-start(f32[32,1024]{1,0:T(8,128)S(1)} %collective-permute-done.5.refs_2_.refs_7_), channel_id=1, source_target_pairs={{0,4},{4,0},{8,12},{12,8},{16,20},{20,16},{24,28},{28,24},{1,5},{5... | collective-permute-start | bytes 393224 | tf_op jit(solution)/shard_map/ppermute | solution.py:34
  28.2 0.0 collective-permute-start.9
  28.2 1.0 %collective-permute-done.8.refs_3_.refs_8_ = f32[32,1024]{1,0:T(8,128)S(1)} collective-permute-done((f32[32,1024]{1,0:T(8,128)S(1)}, f32[32,1024]{1,0:T(8,128)S(1)}, u32[]{:S(2)}, u32[]{:S(2)}) %collective-permute-start.8) | collective-permute-done | bytes 131104 | tf_op jit(solution)/shard_map/ppermute | solution.py:34
  29.2 0.7 %shard_map.90 = (f32[256,384]{1,0:T(8,128)S(1)}, f32[16,128]{1,0:T(8,128)S(1)}, f32[16,128]{1,0:T(8,128)S(1)}) custom-call(s32[16,32]{1,0:T(8,128)S(1)} %get-tuple-element.34.pattern, f32[16,128]{1,0:T(8,128)S(1)} %get-tuple-element.44.mine.refs_0_, f32[16,128]{1,0:T(8,128)S(1)} %collective-permute-done.7.other, ...), custom_call_target="tpu_custom_call" | custom-call | flops 1000 | bytes 1000 | tf_op jit(solution)/shard_map/pallas_call | solution.py:45
  30.0 1.7 %collective-permute-start.10 = (f32[16,128]{1,0:T(8,128)S(1)}, f32[16,128]{1,0:T(8,128)S(1)}, u32[]{:S(2)}, u32[]{:S(2)}) collective-permute-start(f32[16,128]{1,0:T(8,128)S(1)} %get-tuple-element.59.refs_2_), channel_id=1, source_target_pairs={{0,16},{4,20},{8,24},{12,28},{16,0},{20,4},{24,8},{28,12},{1,17},{... | collective-permute-start | bytes 24584 | tf_op jit(solution)/shard_map/ppermute | solution.py:34
  31.7 0.0 collective-permute-done.9.refs_10_
  31.7 2.5 %shard_map.91.base = f32[96,128]{1,0:T(8,128)S(1)} custom-call(s32[16,32]{1,0:T(8,128)S(1)} %get-tuple-element.34.pattern, f32[96,64]{1,0:T(8,128)S(1)} %get-tuple-element.49.leaf_part, f32[64,32]{1,0:T(8,128)S(1)} %shard_map.89.top_s, f32[16,128]{1,0:T(8,128)S(1)} %get-tuple-element.44.mine.refs_0_, f32[16,128]{1,0:T(8,128)S(1)} %get-tuple-element.58.refs_1_, ...), custom_call_target="tpu_custom_call" | custom-call | flops 1000 | bytes 1000 | tf_op jit(solution)/shard_map/pallas_call | solution.py:45
  34.2 0.0 collective-permute-done.10.far
  34.2 0.9 %shard_map.92 = f32[2,1,64,64]{3,2,1,0:T(8,128)} custom-call(f32[96,128]{1,0:T(8,128)S(1)} %shard_map.91.base, f32[16,128]{1,0:T(8,128)S(1)} %collective-permute-done.10.far), custom_call_target="tpu_custom_call" | custom-call | flops 1000 | bytes 1000 | tf_op jit(solution)/shard_map/pallas_call | solution.py:45
  (2 shorter events, 0.0 us)
Async XLA Ops:
  1.0 10.9 %collective-permute-start.1 = (f32[128,384]{1,0:T(8,128)S(1)}, f32[128,384]{1,0:T(8,128)S(1)}, u32[]{:S(2)}, u32[]{:S(2)}) collective-permute-start(f32[128,384]{1,0:T(8,128)S(1)} %get-tuple-element.35.pack.refs_0_), channel_id=1, source_target_pairs={{0,3},{1,2},{2,1},{3,0},{4,7},{5,6},{6,5},{7,4},{8,11},{9,10},{10,... | collective-permute-start | bytes 589832 | tf_op jit(solution)/shard_map/ppermute | solution.py:34
  6.2 9.0 %collective-permute-start = (f32[128,256]{1,0:T(8,128)S(1)}, f32[128,256]{1,0:T(8,128)S(1)}, u32[]{:S(2)}, u32[]{:S(2)}) collective-permute-start(f32[128,256]{1,0:T(8,128)S(1)} %get-tuple-element.36), channel_id=1, source_target_pairs={{0,1},{1,0},{2,3},{3,2},{4,5},{5,4},{6,7},{7,6},{8,9},{9,8},{10,11... | collective-permute-start | bytes 393224 | tf_op jit(solution)/shard_map/ppermute | solution.py:34
  12.0 7.4 %collective-permute-start.2 = (f32[128,256]{1,0:T(8,128)S(1)}, f32[128,256]{1,0:T(8,128)S(1)}, u32[]{:S(2)}, u32[]{:S(2)}) collective-permute-start(f32[128,256]{1,0:T(8,128)S(1)} %get-tuple-element.37), channel_id=1, source_target_pairs={{0,1},{1,0},{2,3},{3,2},{4,5},{5,4},{6,7},{7,6},{8,9},{9,8},{10,11... | collective-permute-start | bytes 393224 | tf_op jit(solution)/shard_map/ppermute | solution.py:34
  15.1 4.3 %collective-permute-start.3 = (f32[128,128]{1,0:T(8,128)S(1)}, f32[128,128]{1,0:T(8,128)S(1)}, u32[]{:S(2)}, u32[]{:S(2)}) collective-permute-start(f32[128,128]{1,0:T(8,128)S(1)} %get-tuple-element.38), channel_id=1, source_target_pairs={{0,1},{1,0},{2,3},{3,2},{4,5},{5,4},{6,7},{7,6},{8,9},{9,8},{10,11... | collective-permute-start | bytes 196616 | tf_op jit(solution)/shard_map/ppermute | solution.py:34
  20.0 1.6 %collective-permute-start.4 = (f32[64,1152]{1,0:T(8,128)S(1)}, f32[64,1152]{1,0:T(8,128)S(1)}, u32[]{:S(2)}, u32[]{:S(2)}) collective-permute-start(f32[64,1152]{1,0:T(8,128)S(1)} %get-tuple-element.42), channel_id=1, source_target_pairs={{0,4},{4,0},{8,12},{12,8},{16,20},{20,16},{24,28},{28,24},{1,5},{5... | collective-permute-start | bytes 884744 | tf_op jit(solution)/shard_map/ppermute | solution.py:34
  20.1 6.9 %collective-permute-start.5 = (f32[32,1024]{1,0:T(8,128)S(1)}, f32[32,1024]{1,0:T(8,128)S(1)}, u32[]{:S(2)}, u32[]{:S(2)}) collective-permute-start(f32[32,1024]{1,0:T(8,128)S(1)} %get-tuple-element.50), channel_id=1, source_target_pairs={{0,8},{4,12},{8,0},{12,4},{16,24},{20,28},{24,16},{28,20},{1,9},{5... | collective-permute-start | bytes 393224 | tf_op jit(solution)/shard_map/ppermute | solution.py:34
  21.6 6.0 %collective-permute-start.6 = (f32[32,1024]{1,0:T(8,128)S(1)}, f32[32,1024]{1,0:T(8,128)S(1)}, u32[]{:S(2)}, u32[]{:S(2)}) collective-permute-start(f32[32,1024]{1,0:T(8,128)S(1)} %shard_map.88), channel_id=1, source_target_pairs={{0,16},{4,28},{8,24},{12,20},{16,0},{20,12},{24,8},{28,4},{1,17},{... | collective-permute-start | bytes 393224 | tf_op jit(solution)/shard_map/ppermute | solution.py:518
  24.0 3.7 %collective-permute-start.7 = (f32[16,128]{1,0:T(8,128)S(1)}, f32[16,128]{1,0:T(8,128)S(1)}, u32[]{:S(2)}, u32[]{:S(2)}) collective-permute-start(f32[16,128]{1,0:T(8,128)S(1)} %get-tuple-element.44.mine.refs_0_), channel_id=1, source_target_pairs={{0,8},{4,12},{8,0},{12,4},{16,24},{20,28},{24,16},{28,20},{1,9},{5... | collective-permute-start | bytes 24584 | tf_op jit(solution)/shard_map/ppermute | solution.py:34
  27.6 1.6 %collective-permute-start.8 = (f32[32,1024]{1,0:T(8,128)S(1)}, f32[32,1024]{1,0:T(8,128)S(1)}, u32[]{:S(2)}, u32[]{:S(2)}) collective-permute-start(f32[32,1024]{1,0:T(8,128)S(1)} %collective-permute-done.5.refs_2_.refs_7_), channel_id=1, source_target_pairs={{0,4},{4,0},{8,12},{12,8},{16,20},{20,16},{24,28},{28,24},{1,5},{5... | collective-permute-start | bytes 393224 | tf_op jit(solution)/shard_map/ppermute | solution.py:34
  28.2 3.5 %collective-permute-start.9 = (f32[32,1024]{1,0:T(8,128)S(1)}, f32[32,1024]{1,0:T(8,128)S(1)}, u32[]{:S(2)}, u32[]{:S(2)}) collective-permute-start(f32[32,1024]{1,0:T(8,128)S(1)} %collective-permute-done.6.refs_9_), channel_id=1, source_target_pairs={{0,4},{4,0},{8,12},{12,8},{16,20},{20,16},{24,28},{28,24},{1,5},{5... | collective-permute-start | bytes 393224 | tf_op jit(solution)/shard_map/ppermute | solution.py:34
  30.0 4.2 %collective-permute-start.10 = (f32[16,128]{1,0:T(8,128)S(1)}, f32[16,128]{1,0:T(8,128)S(1)}, u32[]{:S(2)}, u32[]{:S(2)}) collective-permute-start(f32[16,128]{1,0:T(8,128)S(1)} %get-tuple-element.59.refs_2_), channel_id=1, source_target_pairs={{0,16},{4,20},{8,24},{12,28},{16,0},{20,4},{24,8},{28,12},{1,17},{... | collective-permute-start | bytes 24584 | tf_op jit(solution)/shard_map/ppermute | solution.py:34

commit v9 on v7

--- a/solution.py
+++ b/solution.py
@@ -555,8 +555,9 @@
         (by_x, far, u1_far, own_part, top_s)
     )
     by_x_core = exchange(by_x, "leaf", 1)
+    whole2, cross2, start2 = lead_of(2, all_part, all_core, by_x, by_x_core)
+    far, _ = lax.optimization_barrier((far, cross2))
     far_core = exchange(far, "leaf", 1)
-    whole2, cross2, start2 = lead_of(2, all_part, all_core, by_x, by_x_core)
     (u2,) = kernel(
         update_kernel, [(rhs // 4, 4 * upd)], start2, cross2, u1, u1_far
     )

time: 35.4 us -> 35.6 us (level)
  transfers between devices with their start and end apart: 11 -> 11, of which waited for: 4 -> 4; matrix products, arithmetic and copies ran while one was open for 0% -> 0% of each run, Pallas kernels for 16% -> 15%
where the time goes in v9:
time: 35.6 us; the launch traced here: 35.5 us
  starting transfers between devices  15.3 us (43%)
  waiting for transfers between devices  11.7 us (33%)
  Pallas kernels  8.41 us (24%)
    ppermute x10, starting transfers between devices, exchange(): lax.ppermute(block, axis, [(src, src ^ mask) for src in range(count)])  13.8 us
    ppermute x10, waiting for transfers between devices, exchange(): lax.ppermute(block, axis, [(src, src ^ mask) for src in range(count)])  11.7 us
    pallas_call x13, Pallas kernels, call(): pl.pallas_call(kernel, out_shape=[jax.ShapeDtypeStruct(out, jnp.float32)...  8.41 us
    ppermute x1, starting transfers between devices, chain(): lax.ppermute(far_part, 'leaf', [(src, src ^ (6 if src % 2 else 4)) for sr...  1.58 us
  transfers between devices with their start and end apart: 11, of which 4 were waited for; matrix products, arithmetic and copies ran while one was open for 0% of the time, Pallas kernels for 15%

profile of v9, /device:TPU:0, one launch (start us, length us, event | category | flops | bytes accessed | tf_op | source)
XLA Modules:
  0.0 35.5 jit_solution(6200946989962165216)
XLA Ops:
  0.0 1.0 %shard_map.82 = (f32[128,384]{1,0:T(8,128)S(1)}, f32[128,256]{1,0:T(8,128)S(1)}, s32[16,32]{1,0:T(8,128)S(1)}) custom-call(s32[2,8,32]{2,1,0:T(8,128)} %pattern.1, f32[1,64,64]{2,1,0:T(8,128)} %lr.1, f32[1,64,64]{2,1,0:T(8,128)} %sr.1, f32[1,64,256]{2,1,0:T(8,128)} %li.1, f32[1,64,256]{2,1,0:T(8,128)} %si.1, f32[1,32,64]{2,1,0:T(8,128)} %lu.1, ...), custom_call_target="tpu_custom_call" | custom-call | flops 1000 | bytes 1000 | tf_op jit(solution)/shard_map/pallas_call | solution.py:45
  1.0 5.1 %collective-permute-start.1 = (f32[128,384]{1,0:T(8,128)S(1)}, f32[128,384]{1,0:T(8,128)S(1)}, u32[]{:S(2)}, u32[]{:S(2)}) collective-permute-start(f32[128,384]{1,0:T(8,128)S(1)} %get-tuple-element.38.pack.refs_0_), channel_id=1, source_target_pairs={{0,3},{1,2},{2,1},{3,0},{4,7},{5,6},{6,5},{7,4},{8,11},{9,10},{10,... | collective-permute-start | bytes 589832 | tf_op jit(solution)/shard_map/ppermute | solution.py:34
  6.2 0.0 collective-permute-start
  6.2 5.8 %collective-permute-done.1.across.refs_3_ = f32[128,384]{1,0:T(8,128)S(1)} collective-permute-done((f32[128,384]{1,0:T(8,128)S(1)}, f32[128,384]{1,0:T(8,128)S(1)}, u32[]{:S(2)}, u32[]{:S(2)}) %collective-permute-start.1) | collective-permute-done | bytes 196640 | tf_op jit(solution)/shard_map/ppermute | solution.py:34
  12.0 3.1 %collective-permute-start.2 = (f32[128,256]{1,0:T(8,128)S(1)}, f32[128,256]{1,0:T(8,128)S(1)}, u32[]{:S(2)}, u32[]{:S(2)}) collective-permute-start(f32[128,256]{1,0:T(8,128)S(1)} %get-tuple-element.40), channel_id=1, source_target_pairs={{0,1},{1,0},{2,3},{3,2},{4,5},{5,4},{6,7},{7,6},{8,9},{9,8},{10,11... | collective-permute-start | bytes 393224 | tf_op jit(solution)/shard_map/ppermute | solution.py:34
  15.1 0.1 collective-permute-start.3
  15.1 0.0 collective-permute-done.refs_1_
  15.2 4.2 %collective-permute-done.3.refs_4_ = f32[128,128]{1,0:T(8,128)S(1)} collective-permute-done((f32[128,128]{1,0:T(8,128)S(1)}, f32[128,128]{1,0:T(8,128)S(1)}, u32[]{:S(2)}, u32[]{:S(2)}) %collective-permute-start.3) | collective-permute-done | bytes 65568 | tf_op jit(solution)/shard_map/ppermute | solution.py:34
  19.3 0.0 collective-permute-done.2.refs_2_
  19.3 0.1 shard_map.84
  19.5 0.5 %shard_map.85 = (f32[256,384]{1,0:T(8,128)S(1)}, f32[96,256]{1,0:T(8,128)S(1)}, f32[16,128]{1,0:T(8,128)S(1)}, f32[64,1152]{1,0:T(8,128)S(1)}) custom-call(f32[128,384]{1,0:T(8,128)S(1)} %get-tuple-element.38.pack.refs_0_, f32[128,256]{1,0:T(8,128)S(1)} %collective-permute-done.refs_1_, f32[128,256]{1,0:T(8,128)S(1)} %collective-permute-done.2.refs_2_, ...), custom_call_target="tpu_custom_call" | custom-call | flops 1000 | bytes 1000 | tf_op jit(solution)/shard_map/pallas_call | solution.py:45
  20.0 0.0 collective-permute-start.4
  20.1 1.6 %collective-permute-start.5 = (f32[32,1024]{1,0:T(8,128)S(1)}, f32[32,1024]{1,0:T(8,128)S(1)}, u32[]{:S(2)}, u32[]{:S(2)}) collective-permute-start(f32[32,1024]{1,0:T(8,128)S(1)} %get-tuple-element.55), channel_id=1, source_target_pairs={{0,8},{4,12},{8,0},{12,4},{16,24},{20,28},{24,16},{28,20},{1,9},{5... | collective-permute-start | bytes 393224 | tf_op jit(solution)/shard_map/ppermute | solution.py:34
  21.6 0.0 collective-permute-done.4.refs_1_.message.all_core.refs_6_
  21.6 1.6 %collective-permute-start.6 = (f32[32,1024]{1,0:T(8,128)S(1)}, f32[32,1024]{1,0:T(8,128)S(1)}, u32[]{:S(2)}, u32[]{:S(2)}) collective-permute-start(f32[32,1024]{1,0:T(8,128)S(1)} %shard_map.89), channel_id=1, source_target_pairs={{0,16},{4,28},{8,24},{12,20},{16,0},{20,12},{24,8},{28,4},{1,17},{... | collective-permute-start | bytes 393224 | tf_op jit(solution)/shard_map/ppermute | solution.py:526
  23.2 0.6 %shard_map.86 = (f32[256,384]{1,0:T(8,128)S(1)}, f32[32,64]{1,0:T(8,128)S(1)}, f32[64,32]{1,0:T(8,128)S(1)}) custom-call(s32[16,32]{1,0:T(8,128)S(1)} %get-tuple-element.37.pattern, f32[64,1024]{1,0:T(8,128)S(1)} %get-tuple-element.42.refs_5_.refs_0_, f32[64,1152]{1,0:T(8,128)S(1)} %collective-permute-done.4.refs_1_.message.all_core.refs_6_), custom_call_target="tpu_custom_call" | custom-call | flops 1000 | bytes 1000 | tf_op jit(solution)/shard_map/pallas_call | solution.py:45
  23.8 0.4 shard_map.87
  24.2 1.5 %collective-permute-start.7 = (f32[16,128]{1,0:T(8,128)S(1)}, f32[16,128]{1,0:T(8,128)S(1)}, u32[]{:S(2)}, u32[]{:S(2)}) collective-permute-start(f32[16,128]{1,0:T(8,128)S(1)} %get-tuple-element.49.mine.refs_0_), channel_id=1, source_target_pairs={{0,8},{4,12},{8,0},{12,4},{16,24},{20,28},{24,16},{28,20},{1,9},{5... | collective-permute-start | bytes 24584 | tf_op jit(solution)/shard_map/ppermute | solution.py:34
  25.7 1.2 %shard_map.88 = (f32[160,64]{1,0:T(8,128)S(1)}, f32[96,64]{1,0:T(8,128)S(1)}) custom-call(s32[16,32]{1,0:T(8,128)S(1)} %get-tuple-element.37.pattern, f32[256,384]{1,0:T(8,128)S(1)} %get-tuple-element.50.whole, f32[256,384]{1,0:T(8,128)S(1)} %get-tuple-element.51.leaf_all, f32[96,256]{1,0:T(8,128)S(1)} %get-tuple-element.52.leaf_ahead, ...), custom_call_target="tpu_custom_call" | custom-call | flops 1000 | bytes 1000 | tf_op jit(solution)/shard_map/pallas_call | solution.py:45
  26.8 0.3 shard_map.90.top_s
  27.1 0.0 collective-permute-done.5.refs_2_.refs_7_
  27.1 0.7 %collective-permute-done.7.other.refs_1_ = f32[16,128]{1,0:T(8,128)S(1)} collective-permute-done((f32[16,128]{1,0:T(8,128)S(1)}, f32[16,128]{1,0:T(8,128)S(1)}, u32[]{:S(2)}, u32[]{:S(2)}) %collective-permute-start.7) | collective-permute-done | bytes 8224 | tf_op jit(solution)/shard_map/ppermute | solution.py:34
  27.8 0.0 collective-permute-done.6.refs_9_
  27.8 0.4 %collective-permute-start.8 = (f32[32,1024]{1,0:T(8,128)S(1)}, f32[32,1024]{1,0:T(8,128)S(1)}, u32[]{:S(2)}, u32[]{:S(2)}) collective-permute-start(f32[32,1024]{1,0:T(8,128)S(1)} %collective-permute-done.5.refs_2_.refs_7_), channel_id=1, source_target_pairs={{0,4},{4,0},{8,12},{12,8},{16,20},{20,16},{24,28},{28,24},{1,5},{5... | collective-permute-start | bytes 393224 | tf_op jit(solution)/shard_map/ppermute | solution.py:34
  28.2 1.0 %collective-permute-done.8.refs_3_.refs_8_ = f32[32,1024]{1,0:T(8,128)S(1)} collective-permute-done((f32[32,1024]{1,0:T(8,128)S(1)}, f32[32,1024]{1,0:T(8,128)S(1)}, u32[]{:S(2)}, u32[]{:S(2)}) %collective-permute-start.8) | collective-permute-done | bytes 131104 | tf_op jit(solution)/shard_map/ppermute | solution.py:34
  29.2 0.6 %shard_map.91 = (f32[256,384]{1,0:T(8,128)S(1)}, f32[32,64]{1,0:T(8,128)S(1)}, f32[64,32]{1,0:T(8,128)S(1)}) custom-call(s32[16,32]{1,0:T(8,128)S(1)} %get-tuple-element.37.pattern, f32[64,1024]{1,0:T(8,128)S(1)} %get-tuple-element.42.refs_5_.refs_0_, f32[64,1152]{1,0:T(8,128)S(1)} %collective-permute-done.4.refs_1_.message.all_core.refs_6_, ...), custom_call_target="tpu_custom_call" | custom-call | flops 1000 | bytes 1000 | tf_op jit(solution)/shard_map/pallas_call | solution.py:45
  29.8 0.4 %collective-permute-start.9 = (f32[32,1024]{1,0:T(8,128)S(1)}, f32[32,1024]{1,0:T(8,128)S(1)}, u32[]{:S(2)}, u32[]{:S(2)}) collective-permute-start(f32[32,1024]{1,0:T(8,128)S(1)} %collective-permute-done.6.refs_9_), channel_id=1, source_target_pairs={{0,4},{4,0},{8,12},{12,8},{16,20},{20,16},{24,28},{28,24},{1,5},{5... | collective-permute-start | bytes 393224 | tf_op jit(solution)/shard_map/ppermute | solution.py:34
  30.2 0.3 shard_map.92.refs_2_
  30.6 1.5 %collective-permute-start.10 = (f32[16,128]{1,0:T(8,128)S(1)}, f32[16,128]{1,0:T(8,128)S(1)}, u32[]{:S(2)}, u32[]{:S(2)}) collective-permute-start(f32[16,128]{1,0:T(8,128)S(1)} %shard_map.92.refs_2_), channel_id=1, source_target_pairs={{0,16},{4,20},{8,24},{12,28},{16,0},{20,4},{24,8},{28,12},{1,17},{... | collective-permute-start | bytes 24584 | tf_op jit(solution)/shard_map/ppermute | solution.py:34
  32.1 0.0 collective-permute-done.9.refs_10_
  32.1 2.5 %shard_map.93.base = f32[96,128]{1,0:T(8,128)S(1)} custom-call(s32[16,32]{1,0:T(8,128)S(1)} %get-tuple-element.37.pattern, f32[96,64]{1,0:T(8,128)S(1)} %get-tuple-element.54.leaf_part, f32[64,32]{1,0:T(8,128)S(1)} %shard_map.90.top_s, f32[16,128]{1,0:T(8,128)S(1)} %get-tuple-element.49.mine.refs_0_, f32[16,128]{1,0:T(8,128)S(1)} %collective-permute-done.7.other.refs_1_, ...), custom_call_target="tpu_custom_call" | custom-call | flops 1000 | bytes 1000 | tf_op jit(solution)/shard_map/pallas_call | solution.py:45
  34.6 0.0 collective-permute-done.10.far
  34.6 0.9 %shard_map.94 = f32[2,1,64,64]{3,2,1,0:T(8,128)} custom-call(f32[96,128]{1,0:T(8,128)S(1)} %shard_map.93.base, f32[16,128]{1,0:T(8,128)S(1)} %collective-permute-done.10.far), custom_call_target="tpu_custom_call" | custom-call | flops 1000 | bytes 1000 | tf_op jit(solution)/shard_map/pallas_call | solution.py:45
  (2 shorter events, 0.0 us)
Async XLA Ops:
  1.0 10.9 %collective-permute-start.1 = (f32[128,384]{1,0:T(8,128)S(1)}, f32[128,384]{1,0:T(8,128)S(1)}, u32[]{:S(2)}, u32[]{:S(2)}) collective-permute-start(f32[128,384]{1,0:T(8,128)S(1)} %get-tuple-element.38.pack.refs_0_), channel_id=1, source_target_pairs={{0,3},{1,2},{2,1},{3,0},{4,7},{5,6},{6,5},{7,4},{8,11},{9,10},{10,... | collective-permute-start | bytes 589832 | tf_op jit(solution)/shard_map/ppermute | solution.py:34
  6.2 9.0 %collective-permute-start = (f32[128,256]{1,0:T(8,128)S(1)}, f32[128,256]{1,0:T(8,128)S(1)}, u32[]{:S(2)}, u32[]{:S(2)}) collective-permute-start(f32[128,256]{1,0:T(8,128)S(1)} %get-tuple-element.39), channel_id=1, source_target_pairs={{0,1},{1,0},{2,3},{3,2},{4,5},{5,4},{6,7},{7,6},{8,9},{9,8},{10,11... | collective-permute-start | bytes 393224 | tf_op jit(solution)/shard_map/ppermute | solution.py:34
  12.0 7.4 %collective-permute-start.2 = (f32[128,256]{1,0:T(8,128)S(1)}, f32[128,256]{1,0:T(8,128)S(1)}, u32[]{:S(2)}, u32[]{:S(2)}) collective-permute-start(f32[128,256]{1,0:T(8,128)S(1)} %get-tuple-element.40), channel_id=1, source_target_pairs={{0,1},{1,0},{2,3},{3,2},{4,5},{5,4},{6,7},{7,6},{8,9},{9,8},{10,11... | collective-permute-start | bytes 393224 | tf_op jit(solution)/shard_map/ppermute | solution.py:34
  15.1 4.3 %collective-permute-start.3 = (f32[128,128]{1,0:T(8,128)S(1)}, f32[128,128]{1,0:T(8,128)S(1)}, u32[]{:S(2)}, u32[]{:S(2)}) collective-permute-start(f32[128,128]{1,0:T(8,128)S(1)} %get-tuple-element.41), channel_id=1, source_target_pairs={{0,1},{1,0},{2,3},{3,2},{4,5},{5,4},{6,7},{7,6},{8,9},{9,8},{10,11... | collective-permute-start | bytes 196616 | tf_op jit(solution)/shard_map/ppermute | solution.py:34
  20.0 1.6 %collective-permute-start.4 = (f32[64,1152]{1,0:T(8,128)S(1)}, f32[64,1152]{1,0:T(8,128)S(1)}, u32[]{:S(2)}, u32[]{:S(2)}) collective-permute-start(f32[64,1152]{1,0:T(8,128)S(1)} %get-tuple-element.44), channel_id=1, source_target_pairs={{0,4},{4,0},{8,12},{12,8},{16,20},{20,16},{24,28},{28,24},{1,5},{5... | collective-permute-start | bytes 884744 | tf_op jit(solution)/shard_map/ppermute | solution.py:34
  20.1 7.1 %collective-permute-start.5 = (f32[32,1024]{1,0:T(8,128)S(1)}, f32[32,1024]{1,0:T(8,128)S(1)}, u32[]{:S(2)}, u32[]{:S(2)}) collective-permute-start(f32[32,1024]{1,0:T(8,128)S(1)} %get-tuple-element.55), channel_id=1, source_target_pairs={{0,8},{4,12},{8,0},{12,4},{16,24},{20,28},{24,16},{28,20},{1,9},{5... | collective-permute-start | bytes 393224 | tf_op jit(solution)/shard_map/ppermute | solution.py:34
  21.6 6.2 %collective-permute-start.6 = (f32[32,1024]{1,0:T(8,128)S(1)}, f32[32,1024]{1,0:T(8,128)S(1)}, u32[]{:S(2)}, u32[]{:S(2)}) collective-permute-start(f32[32,1024]{1,0:T(8,128)S(1)} %shard_map.89), channel_id=1, source_target_pairs={{0,16},{4,28},{8,24},{12,20},{16,0},{20,12},{24,8},{28,4},{1,17},{... | collective-permute-start | bytes 393224 | tf_op jit(solution)/shard_map/ppermute | solution.py:526
  24.2 3.7 %collective-permute-start.7 = (f32[16,128]{1,0:T(8,128)S(1)}, f32[16,128]{1,0:T(8,128)S(1)}, u32[]{:S(2)}, u32[]{:S(2)}) collective-permute-start(f32[16,128]{1,0:T(8,128)S(1)} %get-tuple-element.49.mine.refs_0_), channel_id=1, source_target_pairs={{0,8},{4,12},{8,0},{12,4},{16,24},{20,28},{24,16},{28,20},{1,9},{5... | collective-permute-start | bytes 24584 | tf_op jit(solution)/shard_map/ppermute | solution.py:34
  27.8 1.4 %collective-permute-start.8 = (f32[32,1024]{1,0:T(8,128)S(1)}, f32[32,1024]{1,0:T(8,128)S(1)}, u32[]{:S(2)}, u32[]{:S(2)}) collective-permute-start(f32[32,1024]{1,0:T(8,128)S(1)} %collective-permute-done.5.refs_2_.refs_7_), channel_id=1, source_target_pairs={{0,4},{4,0},{8,12},{12,8},{16,20},{20,16},{24,28},{28,24},{1,5},{5... | collective-permute-start | bytes 393224 | tf_op jit(solution)/shard_map/ppermute | solution.py:34
  29.8 2.3 %collective-permute-start.9 = (f32[32,1024]{1,0:T(8,128)S(1)}, f32[32,1024]{1,0:T(8,128)S(1)}, u32[]{:S(2)}, u32[]{:S(2)}) collective-permute-start(f32[32,1024]{1,0:T(8,128)S(1)} %collective-permute-done.6.refs_9_), channel_id=1, source_target_pairs={{0,4},{4,0},{8,12},{12,8},{16,20},{20,16},{24,28},{28,24},{1,5},{5... | collective-permute-start | bytes 393224 | tf_op jit(solution)/shard_map/ppermute | solution.py:34
  30.6 4.0 %collective-permute-start.10 = (f32[16,128]{1,0:T(8,128)S(1)}, f32[16,128]{1,0:T(8,128)S(1)}, u32[]{:S(2)}, u32[]{:S(2)}) collective-permute-start(f32[16,128]{1,0:T(8,128)S(1)} %shard_map.92.refs_2_), channel_id=1, source_target_pairs={{0,16},{4,20},{8,24},{12,28},{16,0},{20,4},{24,8},{28,12},{1,17},{... | collective-permute-start | bytes 24584 | tf_op jit(solution)/shard_map/ppermute | solution.py:34
